TPU v7x, 128 devices: a whole 4x4x4 slice. The times are simulated.
128 devices in a mesh: req: 16 (over y, z), seq: 2 (over core), exp: 4 (over x).
Axes of the slice: x: 4, y: 4, z: 4, core: 2. Of those that a mesh axis runs over, the one named last changes fastest.
Arguments:
- residual: bfloat16 [256, 7168], P(('req', 'seq', 'exp')), may hold values from -6 to 6
- queries: bfloat16 [16, 16, 128, 576], P('req', None, 'exp'), may hold values from -60 to 60
- latent_cache: bfloat16 [16, 384, 576], P('req', 'seq'), may hold values from -20 to 20
- blocks: int32 [16, 2, 2], P('req', 'seq'), may hold values from 0 to 2, as said below
- lengths: int32 [16], P('req'), may hold values from 208 to 384, as said below
- value_up: bfloat16 [128, 512, 128], P('exp'), may hold values from -0.25 to 0.25
- out_proj: bfloat16 [16384, 7168], P('exp', ('req', 'seq')), may hold values from -0.046875 to 0.046875
- norm_gain: bfloat16 [7168], replicated, may hold values from 0.099609375 to 1.8984375
- router: bfloat16 [7168, 16], replicated, may hold values from -0.0625 to 0.0625
- expert_ids: int32 [256, 8], P(('req', 'seq', 'exp')), may hold values from 0 to 15, all different within a row; in each aligned block of 2 rows (0 to 1, 2 to 3, ...) at most 2 rows name the same one
- w_gate: bfloat16 [16, 7168, 2048], P('req', None, ('seq', 'exp')), may hold values from -0.0625 to 0.0625
- w_up: bfloat16 [16, 7168, 2048], P('req', None, ('seq', 'exp')), may hold values from -0.0625 to 0.0625
- w_down: bfloat16 [16, 2048, 7168], P('req', ('seq', 'exp')), may hold values from -0.125 to 0.125
Outputs:
- layer_out: bfloat16 [256, 7168], P(('req', 'seq', 'exp'))
Inputs may be any that keep to these rules, and one draw needn't show every extreme that they name: `blocks`: each request and shard lists 2 different block numbers of that shard. `lengths`: some request has exactly 384, some exactly 208. `expert_ids`: each row names 8 different experts; among the rows of one device (aligned blocks of 2 rows) no expert is named more than 2 times, a bound that some block reaches.
All inputs are finite; a program needn't handle non-finite values.
Results may differ from a plain program's by a relative error of at most 0.019.
Values may be sent and summed in bfloat16 or wider, within the bound.
No kernel may reach another device: no remote copies, remote signals or barrier semaphores. Data moves between devices by JAX's collectives and lax.ppermute only.
A program may use at most 128 MiB of HBM per device.

v0:
```python
import jax
import jax.numpy as jnp
from jax import lax
from jax.sharding import PartitionSpec as P

DL = 512
DR = 64
DV = 128
BLOCK = 64


def combined_all(x, axis, join):
    gathered = jax.tree.map(
        lambda a, kind: lax.all_gather(a.astype(kind), axis),
        x,
        (jnp.bfloat16, jnp.bfloat16, jnp.bfloat16),
    )

    def take(source):
        return jax.tree.map(
            lambda a, own: lax.dynamic_index_in_dim(a, source, 0, False).astype(own.dtype),
            gathered,
            x,
        )

    return lax.fori_loop(
        1, lax.axis_size(axis), lambda source, state: join(state, take(source)), take(0)
    )


def merge_parts(former, latter):
    row_max = jnp.maximum(former[0], latter[0])
    left_scale = jnp.exp(former[0] - row_max)
    right_scale = jnp.exp(latter[0] - row_max)
    return (
        row_max,
        left_scale * former[1] + right_scale * latter[1],
        left_scale[..., None] * former[2] + right_scale[..., None] * latter[2],
    )


def pick_rows(block_rows, picks):
    return block_rows[picks]


def shard_softmax(queries, picked, usable):
    scores = jnp.einsum("bqhk,bjk->bqhj", queries, picked, preferred_element_type=jnp.float32) * (
        DV + DR
    ) ** (-0.5)
    row_max = jnp.max(jnp.where(usable, scores, -1e30), axis=-1)
    weights = jnp.where(usable, jnp.exp(scores - row_max[..., None]), 0.0).astype(jnp.bfloat16)
    row_sum = jnp.sum(weights.astype(jnp.float32), -1)
    weighted = jnp.einsum(
        "bqhj,bjd->bqhd", weights, picked[..., :DL], preferred_element_type=jnp.float32
    )
    return (row_max, row_sum, weighted)


def expert_rows(arrived, w_gate, w_up, w_down):
    model_width = w_gate.shape[1]
    flat_rows = arrived.reshape(-1, model_width)
    gate_act = jnp.dot(flat_rows, w_gate[0], preferred_element_type=jnp.float32)
    up_act = jnp.dot(flat_rows, w_up[0], preferred_element_type=jnp.float32)
    activated = (jax.nn.silu(gate_act) * up_act).astype(jnp.bfloat16)
    partial_value = jnp.dot(activated, w_down[0], preferred_element_type=jnp.float32).astype(
        jnp.bfloat16
    )
    return partial_value.reshape(arrived.shape)


def per_device(
    residual,
    queries,
    latent_cache,
    blocks,
    lengths,
    value_up,
    out_proj,
    norm_gain,
    router,
    expert_ids,
    w_gate,
    w_up,
    w_down,
):
    local_reqs, drafts, head_count, qk_width = queries.shape
    shard_len = latent_cache.shape[1]
    picks_count = blocks.shape[2]
    seq_index = lax.axis_index("seq")
    block_view = latent_cache.reshape(local_reqs, shard_len // BLOCK, BLOCK, qk_width)
    picked = jax.vmap(pick_rows)(block_view, blocks[:, 0]).reshape(
        local_reqs, picks_count * BLOCK, qk_width
    )
    positions = (
        seq_index * shard_len + blocks[:, 0, :, None] * BLOCK + jnp.arange(BLOCK, dtype=jnp.int32)
    )
    positions = positions.reshape(local_reqs, picks_count * BLOCK)
    limits = lengths[:, None] - (drafts - 1) + jnp.arange(drafts, dtype=jnp.int32)[None, :]
    usable = positions[:, None, None, :] < limits[:, :, None, None]
    row_max, row_sum, weighted = shard_softmax(queries, picked, usable)
    row_max, row_sum, weighted = combined_all((row_max, row_sum, weighted), "seq", merge_parts)
    latent = (weighted / row_sum[..., None]).astype(jnp.bfloat16)
    head_values = jnp.einsum(
        "bqhd,hdv->bqhv", latent, value_up, preferred_element_type=jnp.float32
    ).astype(jnp.bfloat16)
    flat_values = head_values.reshape(local_reqs * drafts, head_count * DV)
    col_terms = jnp.dot(
        lax.all_gather(flat_values, "req", axis=0, tiled=True),
        out_proj,
        preferred_element_type=jnp.float32,
    )
    token_terms = lax.all_to_all(
        col_terms[None].astype(jnp.bfloat16),
        ("req", "seq", "exp"),
        split_axis=1,
        concat_axis=0,
        tiled=True,
    ).astype(jnp.float32)
    exp_count = lax.axis_size("exp")
    col_blocks = token_terms.shape[0] // exp_count
    rows_here = token_terms.shape[1]
    col_sums = jnp.sum(
        token_terms.reshape(col_blocks, exp_count, rows_here, token_terms.shape[2]), 1
    )
    attended = jnp.transpose(col_sums, (1, 0, 2)).reshape(rows_here, -1).astype(jnp.bfloat16)
    hidden_sum = (residual.astype(jnp.float32) + attended.astype(jnp.float32)).astype(jnp.bfloat16)
    hidden32 = hidden_sum.astype(jnp.float32)
    normed = (
        hidden32
        * lax.rsqrt(jnp.mean(hidden32 * hidden32, -1, keepdims=True) + 1e-06)
        * norm_gain.astype(jnp.float32)
    ).astype(jnp.bfloat16)
    gate_probs = jax.nn.sigmoid(jnp.dot(normed, router, preferred_element_type=jnp.float32))
    expert_count = router.shape[1]
    top_count = expert_ids.shape[1]
    one_hot = (expert_ids[:, :, None] == jnp.arange(expert_count, dtype=jnp.int32)).astype(
        jnp.int32
    )
    pair_hot = one_hot.reshape(rows_here * top_count, expert_count)
    slot_index = jnp.sum((jnp.cumsum(pair_hot, 0) - pair_hot) * pair_hot, -1)
    slot_hot = (slot_index[:, None] == jnp.arange(rows_here, dtype=jnp.int32)).astype(jnp.int32)
    placement = (pair_hot[:, :, None] * slot_hot[:, None, :]).reshape(
        rows_here, top_count, expert_count * rows_here
    )
    chosen = jnp.sum(one_hot.astype(jnp.float32) * gate_probs[:, None, :], -1)
    gate_weights = chosen / jnp.sum(chosen, -1, keepdims=True) * 2.5
    dispatch = jnp.sum(placement, 1).astype(jnp.bfloat16)
    outgoing = jnp.dot(dispatch.T, normed, preferred_element_type=jnp.float32).astype(jnp.bfloat16)
    outgoing = outgoing.reshape(expert_count, rows_here, outgoing.shape[1])
    combine = jnp.sum(gate_weights[:, :, None] * placement.astype(jnp.float32), 1)
    copies = lax.axis_size("seq") * exp_count
    fanned = jnp.broadcast_to(outgoing[:, None], (expert_count, copies) + outgoing.shape[1:])
    fanned = fanned.reshape((expert_count * copies,) + outgoing.shape[1:])
    returned = lax.all_to_all(
        expert_rows(
            lax.all_to_all(fanned, ("req", "seq", "exp"), split_axis=0, concat_axis=0, tiled=True),
            w_gate,
            w_up,
            w_down,
        ),
        ("req", "seq", "exp"),
        split_axis=0,
        concat_axis=0,
        tiled=True,
    )
    returned = returned.reshape((expert_count, copies) + outgoing.shape[1:]).astype(jnp.float32)
    expert_out = jnp.sum(returned, 1).astype(jnp.bfloat16)
    slot_rows = expert_out.reshape(expert_count * rows_here, expert_out.shape[2]).astype(
        jnp.float32
    )
    routed = jnp.dot(combine, slot_rows, precision=lax.Precision.HIGHEST)
    return (hidden32 + routed).astype(jnp.bfloat16)


def solution(mesh):
    in_specs = (
        P(("req", "seq", "exp"), None),
        P("req", None, "exp", None),
        P("req", "seq", None),
        P("req", "seq", None),
        P("req"),
        P("exp", None, None),
        P("exp", ("req", "seq")),
        P(),
        P(),
        P(("req", "seq", "exp"), None),
        P("req", None, ("seq", "exp")),
        P("req", None, ("seq", "exp")),
        P("req", ("seq", "exp"), None),
    )
    out_specs = P(("req", "seq", "exp"), None)
    return jax.shard_map(
        per_device, mesh=mesh, in_specs=in_specs, out_specs=out_specs, check_vma=False
    )
```

profile of v0, /device:TPU:1, one launch (start us, length us, event | category | flops | bytes accessed | tf_op | source)
XLA Modules:
  0.0 256.2 jit_solution(13494878136915248444)
XLA Ops:
  9.3 1.5 gather_fusion
  10.9 1.5 select_reduce_fusion
  12.4 1.2 convolution_convert_fusion.2
  13.9 2.9 %all-gather.2 = bf16[32,32]{1,0:T(8,128)(2,1)S(1)} all-gather(bf16[16,32]{1,0:T(8,128)(2,1)S(1)} %fusion.34), channel_id=4, replica_groups=mesh['req'=16,'seq'=2,'exp'=4] {'seq'}, dimensions={0}, use_global_device_ids=true | all-gather | bytes 3072 | tf_op jit(solution)/shard_map/all_gather | solution.py:14
  16.8 1.8 all-gather
  18.6 10.5 %all-gather.8.cloned.1.call-done = bf16[32,32,512]{2,1,0:T(8,128)(2,1)} async-done(((bf16[16,32,512]{2,1,0:T(8,128)(2,1)}), bf16[32,32,512]{2,1,0:T(8,128)(2,1)}) %all-gather.8.cloned.1.call-update) | async-done | bytes 1048592 | tf_op jit(solution)/shard_map/all_gather | solution.py:14
  29.1 1.5 fusion.22
  30.6 3.1 %fusion.15 = bf16[1,16,32,128]{3,1,2,0:T(8,128)(2,1)S(1)} fusion(bf16[32,512,128]{2,1,0:T(8,128)(2,1)} %param.18, bf16[16,32,512]{2,1,0:T(8,128)(2,1)S(1)} %fusion.22), kind=kOutput, calls=%fused_computation.18 | convolution fusion | flops 67174400 | bytes 4849664 | tf_op jit(solution)/shard_map/bqhd,hdv->bqhv/dot_general | solution.py:103
  35.0 44.1 %all-gather.6.cloned.1.call-done = bf16[256,4096]{1,0:T(8,128)(2,1)} async-done(((bf16[16,4096]{1,0:T(8,128)(2,1)}), bf16[256,4096]{1,0:T(8,128)(2,1)}) %all-gather.6.cloned.1.call-update) | async-done | bytes 2097168 | tf_op jit(solution)/shard_map/all_gather | solution.py:108
  79.1 2.4 fusion.16
  82.2 1.5 reduce.12
  84.3 9.1 %all-to-all-start = ((bf16[128,2,224]{2,1,0:T(2,128)(2,1)}), bf16[128,2,224]{2,1,0:T(2,128)(2,1)S(1)}, u32[]{:S(2)}, u32[]{:S(2)}) async-start(bf16[128,2,224]{2,1,0:T(2,128)(2,1)} %reshape.417), calls=%async_computation | async-start | bytes 262144 | tf_op jit(solution)/shard_map/all_to_all | solution.py:112
  94.2 9.3 %all-to-all-done = bf16[128,2,224]{2,1,0:T(2,128)(2,1)S(1)} async-done(((bf16[128,2,224]{2,1,0:T(2,128)(2,1)}), bf16[128,2,224]{2,1,0:T(2,128)(2,1)S(1)}, u32[]{:S(2)}, u32[]{:S(2)}) %all-to-all-start) | async-done | bytes 114720 | tf_op jit(solution)/shard_map/all_to_all | solution.py:112
  103.6 0.7 bitcast_reduce_fusion.1
  105.5 1.9 broadcast_in_dim.30
  107.4 51.8 %all_to_all.19 = bf16[128,2,7168]{2,1,0:T(2,128)(2,1)} all-to-all(bf16[128,2,7168]{2,1,0:T(2,128)(2,1)S(1)} %bitcast.72), channel_id=1, replica_groups=mesh['req'=16,'seq'=2,'exp'=4] {'req','seq','exp'}, dimensions={0} | all-to-all | bytes 7340032 | tf_op jit(solution)/shard_map/all_to_all | solution.py:156
  159.2 8.4 %reshape.371 = bf16[256,7168]{1,0:T(8,128)(2,1)} reshape(bf16[128,2,7168]{2,1,0:T(2,128)(2,1)} %all_to_all.19) | data formatting | bytes 7340032 | tf_op jit(solution)/shard_map/reshape | solution.py:61
  167.6 4.3 %fusion.4 = f32[256,256]{1,0:T(8,128)S(1)} fusion(bf16[256,7168]{1,0:T(8,128)(2,1)} %reshape.371, bf16[1,7168,256]{2,1,0:T(8,128)(2,1)} %param.23), kind=kOutput, calls=%fused_computation.9 | convolution fusion | flops 939524096 | bytes 7602176 | tf_op jit(solution)/shard_map/dot_general | solution.py:62
  171.9 10.0 %convolution_convert_fusion = bf16[256,7168]{1,0:T(8,128)(2,1)} fusion(bf16[1,256,7168]{2,1,0:T(8,128)(2,1)} %param.25, bf16[256,7168]{1,0:T(8,128)(2,1)} %reshape.371, bf16[1,7168,256]{2,1,0:T(8,128)(2,1)} %param.24, f32[256,256]{1,0:T(8,128)S(1)} %fusion.4), kind=kOutput, calls=%fused_computation.1 | convolution fusion | flops 1881276416 | bytes 14942208 | tf_op jit(solution)/shard_map/dot_general | solution.py:65
  181.9 8.1 %reshape.372 = bf16[128,2,7168]{2,1,0:T(2,128)(2,1)} reshape(bf16[256,7168]{1,0:T(8,128)(2,1)} %convolution_convert_fusion) | data formatting | bytes 7340032 | tf_op jit(solution)/shard_map/reshape | solution.py:68
  190.1 4.8 %all-to-all-start.2 = ((bf16[128,2,7168]{2,1,0:T(2,128)(2,1)}), bf16[128,2,7168]{2,1,0:T(2,128)(2,1)}, u32[]{:S(2)}, u32[]{:S(2)}) async-start(bf16[128,2,7168]{2,1,0:T(2,128)(2,1)} %reshape.372), calls=%async_computation.2 | async-start | bytes 7340032 | tf_op jit(solution)/shard_map/all_to_all | solution.py:154
  195.6 46.9 %all-to-all-done.2 = bf16[128,2,7168]{2,1,0:T(2,128)(2,1)} async-done(((bf16[128,2,7168]{2,1,0:T(2,128)(2,1)}), bf16[128,2,7168]{2,1,0:T(2,128)(2,1)}, u32[]{:S(2)}, u32[]{:S(2)}) %all-to-all-start.2) | async-done | bytes 3670048 | tf_op jit(solution)/shard_map/all_to_all | solution.py:154
  242.5 5.7 %bitcast_reduce_fusion = bf16[16,2,7168]{2,1,0:T(2,128)(2,1)S(1)} fusion(bf16[128,2,7168]{2,1,0:T(2,128)(2,1)} %all-to-all-done.2), kind=kLoop, calls=%fused_computation.5 | loop fusion | flops 1605632 | bytes 4128768 | tf_op jit(solution)/shard_map/reduce_sum | solution.py:167
  248.4 1.0 fusion
  (59 shorter events, 7.8 us)
Async XLA Ops:
  6.5 72.5 %copy-start = (bf16[4096,224]{0,1:T(8,128)(2,1)S(1)}, bf16[4096,224]{0,1:T(8,128)(2,1)}, u32[]{:S(2)}) copy-start(bf16[4096,224]{0,1:T(8,128)(2,1)} %param.19) | copy-start | bytes 5505028
  6.5 22.6 %all-gather.8.cloned.1.call-start = ((), (), s32[]{:S(2)}) async-start(), calls=%async_computation.4 | async-start | bytes 1572864 | tf_op jit(solution)/shard_map/all_gather | solution.py:14
  13.6 65.5 %all-gather.6.cloned.1.call-start = ((), (), s32[]{:S(2)}) async-start(), calls=%async_computation.3 | async-start | bytes 2228224 | tf_op jit(solution)/shard_map/all_gather | solution.py:108
  13.6 20.9 %copy-start.3 = (s32[2,8]{1,0:T(2,128)S(1)}, s32[2,8]{1,0:T(2,128)}, u32[]{:S(2)}) copy-start(s32[2,8]{1,0:T(2,128)} %param.22) | copy-start | bytes 196
  33.7 60.4 %copy-start.2 = (bf16[7168]{0:T(1024)(128)(2,1)S(1)}, bf16[7168]{0:T(1024)(128)(2,1)}, u32[]{:S(2)}) copy-start(bf16[7168]{0:T(1024)(128)(2,1)} %param.20) | copy-start | bytes 43012
  34.5 70.3 %copy-start.1 = (bf16[2,7168]{1,0:T(2,128)(2,1)S(1)}, bf16[2,7168]{1,0:T(2,128)(2,1)}, u32[]{:S(2)}) copy-start(bf16[2,7168]{1,0:T(2,128)(2,1)} %param.13) | copy-start | bytes 86020
  84.3 19.1 %all-to-all-start = ((bf16[128,2,224]{2,1,0:T(2,128)(2,1)}), bf16[128,2,224]{2,1,0:T(2,128)(2,1)S(1)}, u32[]{:S(2)}, u32[]{:S(2)}) async-start(bf16[128,2,224]{2,1,0:T(2,128)(2,1)} %reshape.417), calls=%async_computation | async-start | bytes 262144 | tf_op jit(solution)/shard_map/all_to_all | solution.py:112
  190.1 4.8 %copy-start.4 = (bf16[7168,16]{0,1:T(8,128)(2,1)S(1)}, bf16[7168,16]{0,1:T(8,128)(2,1)}, u32[]{:S(2)}) copy-start(bf16[7168,16]{0,1:T(8,128)(2,1)} %param.21) | copy-start | bytes 688132
  190.1 52.4 %all-to-all-start.2 = ((bf16[128,2,7168]{2,1,0:T(2,128)(2,1)}), bf16[128,2,7168]{2,1,0:T(2,128)(2,1)}, u32[]{:S(2)}, u32[]{:S(2)}) async-start(bf16[128,2,7168]{2,1,0:T(2,128)(2,1)} %reshape.372), calls=%async_computation.2 | async-start | bytes 7340032 | tf_op jit(solution)/shard_map/all_to_all | solution.py:154
Sparse Core Ops, SparseCore 0:
  13.7 15.3 all-gather.7
  34.6 44.4 all-gather.5
where the time goes:
time: 257 us; the launch traced here: 256 us
  waiting for transfers between devices  111 us (43%)
  blocking collectives  56.5 us (22%)
  local copies, waits for them, and re-layouts  24.2 us (9%)
  matrix products  24 us (9%)
  between operations  14.4 us (6%)
  starting transfers between devices  13.9 us (5%)
  other arithmetic  12.3 us (5%)
    all_to_all x1, blocking collectives, per_device(): lax.all_to_all(fanned, ('req', 'seq', 'exp'), split_axis=0, concat_axis=0...  51.8 us
    all_to_all x1, waiting for transfers between devices, per_device(): lax.all_to_all(expert_rows(lax.all_to_all(fanned, ('req', 'seq', 'exp'),...  46.9 us
    all_gather x1, waiting for transfers between devices, per_device(): lax.all_gather(flat_values, 'req', axis=0, tiled=True)  44.1 us
    all_gather x1, waiting for transfers between devices, combined_all(): lax.all_gather(a.astype(kind), axis)  10.5 us
    dot_general x1, matrix products, expert_rows(): jnp.dot(activated, w_down[0], preferred_element_type=jnp.float32)  10 us
    all_to_all x1, waiting for transfers between devices, per_device(): lax.all_to_all(col_terms[None].astype(jnp.bfloat16), ('req', 'seq', 'exp'...  9.29 us
    all_to_all x1, starting transfers between devices, per_device(): lax.all_to_all(col_terms[None].astype(jnp.bfloat16), ('req', 'seq', 'exp'...  9.06 us
    reshape x1, local copies, waits for them, and re-layouts, expert_rows(): flat_rows = arrived.reshape(-1, model_width)  8.4 us
  transfers between devices with their start and end apart: 4, of which 4 were waited for; matrix products, arithmetic and copies ran while one was open for 1% of the time, Pallas kernels for 0%

commit v1 on v0

v1 whole, which is shorter than its diff:
```python
import jax
import jax.numpy as jnp
from jax import lax
from jax.experimental import pallas as pl
from jax.experimental.pallas import tpu as pltpu
from jax.sharding import PartitionSpec as P

DL = 512
DR = 64
DV = 128
BLOCK = 64
F32 = jnp.float32
BF16 = jnp.bfloat16
SWAP = [(0, 1), (1, 0)]


def swap(x):
    return lax.ppermute(x, "seq", SWAP)


def shard_softmax(queries, picked, usable):
    scores = jnp.einsum("qhk,jk->qhj", queries, picked, preferred_element_type=F32) * (
        DV + DR
    ) ** (-0.5)
    row_max = jnp.max(jnp.where(usable, scores, -1e30), axis=-1)
    weights = jnp.where(usable, jnp.exp(scores - row_max[..., None]), 0.0).astype(BF16)
    row_sum = jnp.sum(weights.astype(F32), -1)
    weighted = jnp.einsum("qhj,jd->qhd", weights, picked[:, :DL], preferred_element_type=F32)
    return row_max, row_sum, weighted


def gate_up_kernel(idx, own, other, gain_own, gain_other, w_gate, w_up, router, act, acc_g, acc_u, acc_l, ssq):
    step = pl.program_id(0)
    width = gain_own.shape[-1]

    @pl.when(step == 0)
    def _():
        acc_g[...] = jnp.zeros_like(acc_g)
        acc_u[...] = jnp.zeros_like(acc_u)
        acc_l[...] = jnp.zeros_like(acc_l)
        ssq[...] = jnp.zeros_like(ssq)

    for rows, gain, side in ((own, gain_own, idx[0]), (other, gain_other, 1 - idx[0])):
        start = pl.multiple_of(side * width, 16)
        hidden = rows[0, :, :width].astype(F32)
        ssq[...] += jnp.sum(hidden * hidden, -1, keepdims=True)
        scaled = (hidden * gain[0].astype(F32)).astype(BF16)
        acc_g[...] += jnp.dot(scaled, w_gate[pl.ds(start, width), :], preferred_element_type=F32)
        acc_u[...] += jnp.dot(scaled, w_up[pl.ds(start, width), :], preferred_element_type=F32)
        acc_l[...] += jnp.dot(scaled, router[pl.ds(start, width), :], preferred_element_type=F32)

    @pl.when(step == pl.num_programs(0) - 1)
    def _():
        experts = router.shape[-1]
        columns = 2 * width * pl.num_programs(0)
        scale = lax.rsqrt(ssq[...] / columns + 1e-06)
        named = own[0, :, width : width + experts].astype(F32)
        chosen = named * jax.nn.sigmoid(acc_l[...] * scale)
        mine = lax.broadcasted_iota(jnp.int32, chosen.shape, 1) == idx[1]
        weight = jnp.sum(jnp.where(mine, chosen, 0.0), -1, keepdims=True)
        weight = weight / jnp.sum(chosen, -1, keepdims=True) * 2.5
        act[...] = (jax.nn.silu(acc_g[...] * scale) * (acc_u[...] * scale) * weight).astype(BF16)


def gate_up(idx, own, other, gain_own, gain_other, w_gate, w_up, router):
    steps, tokens, padded = own.shape
    width = gain_own.shape[-1]
    hidden = w_gate.shape[-1]
    experts = router.shape[-1]
    row_spec = pl.BlockSpec((1, tokens, padded), lambda i, idx: (i, 0, 0))
    gain_spec = pl.BlockSpec((1, 1, width), lambda i, idx: (i, 0, 0))
    return pl.pallas_call(
        gate_up_kernel,
        out_shape=jax.ShapeDtypeStruct((tokens, hidden), BF16),
        grid_spec=pltpu.PrefetchScalarGridSpec(
            num_scalar_prefetch=1,
            grid=(steps,),
            in_specs=[
                row_spec,
                row_spec,
                gain_spec,
                gain_spec,
                pl.BlockSpec((2 * width, hidden), lambda i, idx: (i, 0)),
                pl.BlockSpec((2 * width, hidden), lambda i, idx: (i, 0)),
                pl.BlockSpec((2 * width, experts), lambda i, idx: (i, 0)),
            ],
            out_specs=pl.BlockSpec((tokens, hidden), lambda i, idx: (0, 0)),
            scratch_shapes=[
                pltpu.VMEM((tokens, hidden), F32),
                pltpu.VMEM((tokens, hidden), F32),
                pltpu.VMEM((tokens, experts), F32),
                pltpu.VMEM((tokens, 1), F32),
            ],
        ),
        name="gate_up",
    )(idx, own, other, gain_own, gain_other, w_gate, w_up, router)


def down_first_kernel(idx, act, w_down, out):
    out[...] = jnp.dot(act[...], w_down[...], preferred_element_type=F32).astype(BF16)


def down_second_kernel(idx, act, w_down, arrived, out):
    total = jnp.dot(act[...], w_down[...], preferred_element_type=F32) + arrived[...].astype(F32)
    out[...] = total.reshape(out.shape).astype(BF16)


def down(idx, act, w_down, arrived):
    tokens, hidden = act.shape
    half = w_down.shape[1] // 2
    steps = 4
    block = half // steps
    side = (lambda idx: 1 - idx[0]) if arrived is None else (lambda idx: idx[0])
    in_specs = [
        pl.BlockSpec((tokens, hidden), lambda i, idx: (0, 0)),
        pl.BlockSpec((hidden, block), lambda i, idx: (0, side(idx) * steps + i)),
    ]
    operands = [idx, act, w_down]
    if arrived is None:
        kernel = down_first_kernel
        out_shape = jax.ShapeDtypeStruct((tokens, half), BF16)
        out_spec = pl.BlockSpec((tokens, block), lambda i, idx: (0, i))
    else:
        kernel = down_second_kernel
        operands.append(arrived)
        in_specs.append(pl.BlockSpec((tokens, block), lambda i, idx: (0, i)))
        out_shape = jax.ShapeDtypeStruct((tokens // 4, 4, half), BF16)
        out_spec = pl.BlockSpec((tokens // 4, 4, block), lambda i, idx: (0, 0, i))
    return pl.pallas_call(
        kernel,
        out_shape=out_shape,
        grid_spec=pltpu.PrefetchScalarGridSpec(
            num_scalar_prefetch=1, grid=(steps,), in_specs=in_specs, out_specs=out_spec
        ),
        name="down",
    )(*operands)


def per_device(
    residual,
    queries,
    latent_cache,
    blocks,
    lengths,
    value_up,
    out_proj,
    norm_gain,
    router,
    expert_ids,
    w_gate,
    w_up,
    w_down,
):
    drafts, heads, qk_width = queries.shape[1:]
    shard_len = latent_cache.shape[1]
    picks_count = blocks.shape[2]
    n_req, n_exp = lax.axis_size("req"), lax.axis_size("exp")
    s = lax.axis_index("seq")
    x = lax.axis_index("exp")
    r = lax.axis_index("req")
    model_width = residual.shape[1]
    experts = router.shape[1]
    width = out_proj.shape[1]
    padded = -(-width // 128) * 128
    own_rows = residual.shape[0]
    tokens = n_req * drafts

    block_view = latent_cache.reshape(shard_len // BLOCK, BLOCK, qk_width)
    picked = block_view[blocks[0, 0]].reshape(picks_count * BLOCK, qk_width)
    positions = s * shard_len + blocks[0, 0, :, None] * BLOCK + jnp.arange(BLOCK, dtype=jnp.int32)
    positions = positions.reshape(picks_count * BLOCK)
    limits = lengths[0] - (drafts - 1) + jnp.arange(drafts, dtype=jnp.int32)
    usable = positions[None, None, :] < limits[:, None, None]
    row_max, row_sum, weighted = shard_softmax(queries[0], picked, usable)
    half_heads = heads // 2

    def heads_of(a, side):
        a = a.reshape((drafts, 2, half_heads) + a.shape[2:])
        return lax.dynamic_index_in_dim(a, side, 1, False)

    sent = heads_of(weighted, 1 - s).astype(BF16)
    stats = jnp.stack([heads_of(row_max, 1 - s), heads_of(row_sum, 1 - s)])
    other_weighted, other_stats = swap(sent), swap(stats)
    max_own, sum_own, out_own = heads_of(row_max, s), heads_of(row_sum, s), heads_of(weighted, s)
    top = jnp.maximum(max_own, other_stats[0])
    scale_own, scale_other = jnp.exp(max_own - top), jnp.exp(other_stats[0] - top)
    total = scale_own * sum_own + scale_other * other_stats[1]
    latent = scale_own[..., None] * out_own + scale_other[..., None] * other_weighted.astype(F32)
    latent = (latent / total[..., None]).astype(BF16)
    value_half = lax.dynamic_slice_in_dim(value_up, s * half_heads, half_heads, 0)
    head_values = jnp.einsum("qhd,hdv->qhv", latent, value_half, preferred_element_type=F32)
    flat_values = head_values.astype(BF16).reshape(drafts, half_heads * DV)

    named = jnp.sum(
        (expert_ids[:, :, None] == jnp.arange(experts, dtype=jnp.int32)).astype(F32), 1
    ).astype(BF16)
    columns = residual.reshape(own_rows, n_req * 2, width)
    named = jnp.broadcast_to(named[:, None], (own_rows, n_req * 2, experts))
    spare = jnp.zeros((own_rows, n_req * 2, padded - width - experts), BF16)
    side_rows = jnp.concatenate([columns, named, spare], -1)
    side_rows = side_rows.reshape(own_rows, n_req, 2 * padded // 128, 128).transpose(1, 0, 2, 3)
    side_rows = side_rows.reshape(n_req, own_rows * 2 * padded // 128, 128)
    side_rows = jnp.pad(side_rows, ((0, 0), (0, drafts - side_rows.shape[1]), (0, 0)))
    fanned = jnp.concatenate(
        [jnp.broadcast_to(flat_values[None], (n_req,) + flat_values.shape), side_rows], -1
    )
    gathered = lax.all_to_all(fanned, "req", split_axis=0, concat_axis=0, tiled=True)
    gathered_other = swap(gathered)

    def values_of(a):
        return a[:, :, : half_heads * DV].reshape(tokens, half_heads * DV)

    def residual_of(a):
        a = a[:, : own_rows * 2 * padded // 128, half_heads * DV :]
        return a.reshape(n_req, own_rows, 2, padded)

    depth = half_heads * DV
    terms = jnp.dot(
        values_of(gathered),
        lax.dynamic_slice_in_dim(out_proj, s * depth, depth, 0),
        preferred_element_type=F32,
    )
    terms += jnp.dot(
        values_of(gathered_other),
        lax.dynamic_slice_in_dim(out_proj, (1 - s) * depth, depth, 0),
        preferred_element_type=F32,
    )
    terms = jnp.pad(terms.astype(BF16), ((0, 0), (0, padded - width)))
    new = jnp.arange(tokens, dtype=jnp.int32)
    group = 2 * own_rows
    new_exp, new_req = new // (n_req * group), new // group % n_req
    new_seq, new_row = new // own_rows % 2, new % own_rows
    old = ((new_req * 2 + new_seq) * n_exp + new_exp) * own_rows + new_row
    order = (old[:, None] == new[None, :]).astype(BF16)
    terms = jnp.dot(order, terms, preferred_element_type=F32).astype(BF16)
    terms = lax.all_to_all(
        terms.reshape(n_exp, tokens // n_exp, padded), "exp", split_axis=0, concat_axis=0, tiled=True
    )
    attended = jnp.sum(terms.astype(F32), 0).astype(BF16)
    mine, theirs = residual_of(gathered), residual_of(gathered_other)
    both = jnp.where(s == 0, jnp.stack([mine, theirs], 1), jnp.stack([theirs, mine], 1))
    both = lax.dynamic_index_in_dim(both, s, 3, False).reshape(tokens // n_exp, padded)
    hidden_sum = (both.astype(F32) + attended.astype(F32)).astype(BF16)

    fanned = jnp.broadcast_to(hidden_sum[None], (n_req * n_exp,) + hidden_sum.shape)
    own = lax.all_to_all(fanned, ("req", "exp"), split_axis=0, concat_axis=0, tiled=True)
    own = own.reshape(n_req, tokens, padded)
    other = swap(own)
    gains = norm_gain.reshape(n_req, 2, 1, width)
    gain_own = lax.dynamic_index_in_dim(gains, s, 1, False)
    gain_other = lax.dynamic_index_in_dim(gains, 1 - s, 1, False)
    idx = jnp.stack([s, r]).astype(jnp.int32)
    act = gate_up(idx, own, other, gain_own, gain_other, w_gate[0], w_up[0], router)
    arrived = swap(down(idx, act, w_down[0], None))
    pieces = down(idx, act, w_down[0], arrived)
    pieces = lax.all_to_all(pieces, ("exp", "req"), split_axis=0, concat_axis=0, tiled=True)
    routed = jnp.sum(pieces.astype(F32), 0)
    routed = routed.reshape(2, own_rows, model_width // 2)
    routed_mine = lax.dynamic_index_in_dim(routed, s, 0, False)
    routed_theirs = swap(lax.dynamic_index_in_dim(routed, 1 - s, 0, False))
    routed = jnp.where(
        s == 0,
        jnp.concatenate([routed_mine, routed_theirs], -1),
        jnp.concatenate([routed_theirs, routed_mine], -1),
    )
    place = ((x * n_req + r) * 2 + s) * own_rows
    hid_own = lax.dynamic_slice_in_dim(own, place, own_rows, 1)[:, :, :width]
    hid_other = lax.dynamic_slice_in_dim(other, place, own_rows, 1)[:, :, :width]
    hid = jnp.where(s == 0, jnp.stack([hid_own, hid_other], 1), jnp.stack([hid_other, hid_own], 1))
    hid = hid.transpose(2, 0, 1, 3).reshape(own_rows, model_width)
    return (hid.astype(F32) + routed).astype(BF16)


def solution(mesh):
    in_specs = (
        P(("req", "seq", "exp"), None),
        P("req", None, "exp", None),
        P("req", "seq", None),
        P("req", "seq", None),
        P("req"),
        P("exp", None, None),
        P("exp", ("req", "seq")),
        P(),
        P(),
        P(("req", "seq", "exp"), None),
        P("req", None, ("seq", "exp")),
        P("req", None, ("seq", "exp")),
        P("req", ("seq", "exp"), None),
    )
    out_specs = P(("req", "seq", "exp"), None)
    return jax.shard_map(
        per_device, mesh=mesh, in_specs=in_specs, out_specs=out_specs, check_vma=False
    )
```

time: 257 us -> 162 us (0.63)
  waiting for transfers between devices: 111 us -> 35.4 us
  Pallas kernels: 0 us -> 25.9 us
  matrix products: 24 us -> 6.14 us
  local copies, waits for them, and re-layouts: 24.2 us -> 10.4 us
  between operations: 14.4 us -> 1.12 us
  other arithmetic: 12.3 us -> 5.67 us
  starting transfers between devices: 13.9 us -> 19.8 us
    all_gather x2 -> x0, waiting for transfers between devices: 54.6 us -> none  [the longest x1 44.1 us: per_device(): lax.all_gather(flat_values, 'req', axis=0, tiled=True)]
    all_to_all x2, waiting for transfers between devices: 56.2 us -> 28 us  [the longest x1 23.3 us: per_device(): lax.all_to_all(pieces, ('exp', 'req'), split_axis=0, concat_axis=0, tiled...]
    pallas_call x0 -> x3, Pallas kernels: none -> 25.9 us  [the longest x1 15.4 us: gate_up(): pl.pallas_call(gate_up_kernel, out_shape=jax.ShapeDtypeStruct((tokens, hi...]
    dot_general x9 -> x6, matrix products: 24 us -> 6.14 us  [the longest x1 2.42 us: per_device(): jnp.einsum('qhd,hdv->qhv', latent, value_half, preferred_element_type=F32)]
    reshape x3 -> x6, local copies, waits for them, and re-layouts: 16.7 us -> 0.42 us  [the longest x2 0.16 us: heads_of(): a = a.reshape((drafts, 2, half_heads) + a.shape[2:])]
    ppermute x0 -> x6, starting transfers between devices: none -> 10.2 us  [swap(): return lax.ppermute(x, 'seq', SWAP)]
    ppermute x0 -> x6, waiting for transfers between devices: none -> 7.39 us  [swap(): return lax.ppermute(x, 'seq', SWAP)]
    all_to_all x1 -> x2, blocking collectives: 51.8 us -> 56.9 us  [the longest x1 32.1 us: per_device(): lax.all_to_all(fanned, ('req', 'exp'), split_axis=0, concat_axis=0, tiled...]
  transfers between devices with their start and end apart: 4 -> 8, of which waited for: 4 -> 7; matrix products, arithmetic and copies ran while one was open for 1% -> 5% of each run, Pallas kernels for 0% -> 0%
where the time goes in v1:
time: 162 us; the launch traced here: 161 us
  blocking collectives  56.9 us (35%)
  waiting for transfers between devices  35.4 us (22%)
  Pallas kernels  25.9 us (16%)
  starting transfers between devices  19.8 us (12%)
  local copies, waits for them, and re-layouts  10.4 us (6%)
  matrix products  6.14 us (4%)
  other arithmetic  5.67 us (4%)
    all_to_all x1, blocking collectives, per_device(): lax.all_to_all(fanned, ('req', 'exp'), split_axis=0, concat_axis=0, tiled...  32.1 us
    all_to_all x1, blocking collectives, per_device(): lax.all_to_all(fanned, 'req', split_axis=0, concat_axis=0, tiled=True)  24.8 us
    all_to_all x1, waiting for transfers between devices, per_device(): lax.all_to_all(pieces, ('exp', 'req'), split_axis=0, concat_axis=0, tiled...  23.3 us
    pallas_call x1, Pallas kernels, gate_up(): pl.pallas_call(gate_up_kernel, out_shape=jax.ShapeDtypeStruct((tokens, hi...  15.4 us
    pallas_call x2, Pallas kernels, down(): pl.pallas_call(kernel, out_shape=out_shape, grid_spec=pltpu.PrefetchScala...  10.4 us
    ppermute x6, starting transfers between devices, swap(): return lax.ppermute(x, 'seq', SWAP)  10.2 us
    ppermute x6, waiting for transfers between devices, swap(): return lax.ppermute(x, 'seq', SWAP)  7.39 us
    all_to_all x1, starting transfers between devices, per_device(): lax.all_to_all(pieces, ('exp', 'req'), split_axis=0, concat_axis=0, tiled...  5.51 us
  transfers between devices with their start and end apart: 8, of which 7 were waited for; matrix products, arithmetic and copies ran while one was open for 5% of the time, Pallas kernels for 0%

profile of v1, /device:TPU:1, one launch (start us, length us, event | category | flops | bytes accessed | tf_op | source)
XLA Modules:
  0.0 161.2 jit_solution(1840856437805219464)
XLA Ops:
  2.3 1.5 gather_fusion
  3.9 1.5 select_reduce_fusion
  5.9 1.5 collective-permute-start
  9.7 2.4 %fusion.8 = bf16[16,2,8,128]{3,2,1,0:T(8,128)(2,1)S(1)} fusion(bf16[32,512,128]{2,1,0:T(8,128)(2,1)} %param.18, s32[]{:T(128)S(6)} %select_n.126, f32[16,1,16,512]{3,2,1,0:T(8,128)} %constant_dynamic-slice_fusion.2, bf16[16,16,512]{2,0,1:T(8,128)(2,1)} %collective-permute-done.1, f32[16,16]{0,1:T(8,128)S(1)} %copy.102, f32[16,16]{0,1:T(8,128)S(1)} %copy.99, ...), kind=kOutput, calls=%fused_computation.12 | convolution fusion | flops 34373632 | bytes 2952196 | tf_op jit(solution)/shard_map/qhd,hdv->qhv/dot_general | solution.py:191
  12.3 24.8 %all_to_all.20 = bf16[16,16,2176]{2,1,0:T(8,128)(2,1)S(1)} all-to-all(bf16[16,16,2176]{2,1,0:T(8,128)(2,1)S(1)} %fusion.11), channel_id=1, replica_groups=mesh['req'=16,'seq'=2,'exp'=4] {'req'}, dimensions={0} | all-to-all | bytes 2228224 | tf_op jit(solution)/shard_map/all_to_all | solution.py:207
  37.1 1.7 %collective-permute-start.2 = (bf16[16,16,2176]{2,1,0:T(8,128)(2,1)S(1)}, bf16[16,16,2176]{2,1,0:T(8,128)(2,1)}, u32[]{:S(2)}, u32[]{:S(2)}) collective-permute-start(bf16[16,16,2176]{2,1,0:T(8,128)(2,1)S(1)} %all_to_all.20), channel_id=1, source_target_pairs={{0,4},{4,0},{1,5},{5,1},{2,6},{6,2},{3,7},{7,3},{8,12},{12,8},{9,1... | collective-permute-start | bytes 3342344 | tf_op jit(solution)/shard_map/ppermute | solution.py:18
  39.5 1.8 %collective-permute-done.2 = bf16[16,16,2176]{2,1,0:T(8,128)(2,1)} collective-permute-done((bf16[16,16,2176]{2,1,0:T(8,128)(2,1)S(1)}, bf16[16,16,2176]{2,1,0:T(8,128)(2,1)}, u32[]{:S(2)}, u32[]{:S(2)}) %collective-permute-start.2) | collective-permute-done | bytes 1114144 | tf_op jit(solution)/shard_map/ppermute | solution.py:18
  42.1 1.3 slice.45
  43.9 0.9 convolution_convert_fusion
  44.8 4.0 %all-to-all-start.1 = ((bf16[4,64,256]{2,1,0:T(8,128)(2,1)}), bf16[4,64,256]{2,1,0:T(8,128)(2,1)S(1)}, u32[]{:S(2)}, u32[]{:S(2)}) async-start(bf16[4,64,256]{2,1,0:T(8,128)(2,1)} %bitcast.24), calls=%async_computation.1 | async-start | bytes 262144 | tf_op jit(solution)/shard_map/all_to_all | solution.py:236
  48.9 4.7 %all-to-all-done.1 = bf16[4,64,256]{2,1,0:T(8,128)(2,1)S(1)} async-done(((bf16[4,64,256]{2,1,0:T(8,128)(2,1)}), bf16[4,64,256]{2,1,0:T(8,128)(2,1)S(1)}, u32[]{:S(2)}, u32[]{:S(2)}) %all-to-all-start.1) | async-done | bytes 131104 | tf_op jit(solution)/shard_map/all_to_all | solution.py:236
  54.0 32.1 %all_to_all.21 = bf16[64,64,256]{2,1,0:T(8,128)(2,1)} all-to-all(bf16[64,64,256]{2,1,0:T(8,128)(2,1)S(1)} %broadcast_in_dim.58), channel_id=1, replica_groups=mesh['req'=16,'seq'=2,'exp'=4] {'req','exp'}, dimensions={0} | all-to-all | bytes 4194304 | tf_op jit(solution)/shard_map/all_to_all | solution.py:246
  86.0 3.8 %collective-permute-start.3 = (bf16[16,256,256]{2,1,0:T(8,128)(2,1)}, bf16[16,256,256]{2,1,0:T(8,128)(2,1)}, u32[]{:S(2)}, u32[]{:S(2)}) collective-permute-start(bf16[16,256,256]{2,1,0:T(8,128)(2,1)} %bitcast.25.own), channel_id=1, source_target_pairs={{0,4},{4,0},{1,5},{5,1},{2,6},{6,2},{3,7},{7,3},{8,12},{12,8},{9,1... | collective-permute-start | bytes 6291464 | tf_op jit(solution)/shard_map/ppermute | solution.py:18
  89.9 1.6 %copy.114.router = bf16[7168,16]{1,0:T(8,128)(2,1)} copy(bf16[7168,16]{0,1:T(8,128)(2,1)S(1)} %copy-done.1) | data formatting | bytes 458752 | tf_op args[8]
  92.8 1.1 collective-permute-done.3.other
  93.9 15.4 %gate_up.1.act = bf16[256,256]{1,0:T(8,128)(2,1)} custom-call(s32[2]{0:T(128)} %pad_add_fusion.idx, bf16[16,256,256]{2,1,0:T(8,128)(2,1)} %bitcast.25.own, bf16[16,256,256]{2,1,0:T(8,128)(2,1)} %collective-permute-done.3.other, bf16[16,1,224]{2,1,0:T(2,128)(2,1)} %get-tuple-element.11.gain_own, bf16[16,1,224]{2,1,0:T(2,128)(2,1)} %get-tuple-element.10.gain_other, ...), custom_call_target="tpu_custom_call" | custom-call | tf_op jit(solution)/shard_map/gate_up/pallas_call | solution.py:72
  109.3 5.0 %down.2 = bf16[256,3584]{1,0:T(8,128)(2,1)} custom-call(s32[2]{0:T(128)} %pad_add_fusion.idx, bf16[256,256]{1,0:T(8,128)(2,1)} %gate_up.1.act, bf16[256,7168]{1,0:T(8,128)(2,1)} %bitcast.96), custom_call_target="tpu_custom_call" | custom-call | tf_op jit(solution)/shard_map/down/pallas_call | solution.py:129
  114.8 3.8 %collective-permute-done.4.arrived = bf16[256,3584]{1,0:T(8,128)(2,1)} collective-permute-done((bf16[256,3584]{1,0:T(8,128)(2,1)}, bf16[256,3584]{1,0:T(8,128)(2,1)}, u32[]{:S(2)}, u32[]{:S(2)}) %collective-permute-start.4) | collective-permute-done | bytes 1835040 | tf_op jit(solution)/shard_map/ppermute | solution.py:18
  118.6 5.4 %down.3 = bf16[64,4,3584]{2,1,0:T(4,128)(2,1)} custom-call(s32[2]{0:T(128)} %pad_add_fusion.idx, bf16[256,256]{1,0:T(8,128)(2,1)} %gate_up.1.act, bf16[256,7168]{1,0:T(8,128)(2,1)} %bitcast.97, bf16[256,3584]{1,0:T(8,128)(2,1)} %collective-permute-done.4.arrived), custom_call_target="tpu_custom_call" | custom-call | tf_op jit(solution)/shard_map/down/pallas_call | solution.py:129
  124.0 5.5 %all-to-all-start.3 = ((bf16[64,4,3584]{2,1,0:T(4,128)(2,1)}), bf16[64,4,3584]{2,1,0:T(4,128)(2,1)}, u32[]{:S(2)}, u32[]{:S(2)}) async-start(bf16[64,4,3584]{2,1,0:T(4,128)(2,1)} %down.3), calls=%async_computation.3 | async-start | bytes 3670016 | tf_op jit(solution)/shard_map/all_to_all | solution.py:256
  130.4 0.9 dynamic-slice_bitcast_fusion.2
  131.3 23.3 %all-to-all-done.3 = bf16[64,4,3584]{2,1,0:T(4,128)(2,1)} async-done(((bf16[64,4,3584]{2,1,0:T(4,128)(2,1)}), bf16[64,4,3584]{2,1,0:T(4,128)(2,1)}, u32[]{:S(2)}, u32[]{:S(2)}) %all-to-all-start.3) | async-done | bytes 1835040 | tf_op jit(solution)/shard_map/all_to_all | solution.py:256
  154.7 2.3 %convert_reduce_fusion = f32[4,3584]{1,0:T(4,128)S(1)} fusion(bf16[64,4,3584]{2,1,0:T(4,128)(2,1)} %all-to-all-done.3), kind=kLoop, calls=%fused_computation.1 | loop fusion | flops 1820672 | bytes 1892352 | tf_op jit(solution)/shard_map/reduce_sum | solution.py:257
  157.0 2.8 %collective-permute-start.5 = (f32[2,3584]{1,0:T(2,128)S(1)}, f32[2,3584]{1,0:T(2,128)S(1)}, u32[]{:S(2)}, u32[]{:S(2)}) collective-permute-start(f32[2,3584]{1,0:T(2,128)S(1)} %get-tuple-element.9), channel_id=1, source_target_pairs={{0,4},{4,0},{1,5},{5,1},{2,6},{6,2},{3,7},{7,3},{8,12},{12,8},{9,1... | collective-permute-start | bytes 86024 | tf_op jit(solution)/shard_map/ppermute | solution.py:18
  (73 shorter events, 11.1 us)
Async XLA Ops:
  0.0 39.0 %copy-start = (bf16[4096,224]{0,1:T(8,128)(2,1)S(1)}, bf16[4096,224]{0,1:T(8,128)(2,1)}, u32[]{:S(2)}) copy-start(bf16[4096,224]{0,1:T(8,128)(2,1)} %param.19) | copy-start | bytes 5505028
  3.9 4.1 %copy-start.4 = (s32[2,8]{1,0:T(2,128)S(1)}, s32[2,8]{1,0:T(2,128)}, u32[]{:S(2)}) copy-start(s32[2,8]{1,0:T(2,128)} %param.22) | copy-start | bytes 196
  3.9 4.2 %copy-start.2 = (bf16[2,7168]{1,0:T(2,128)(2,1)S(1)}, bf16[2,7168]{1,0:T(2,128)(2,1)}, u32[]{:S(2)}) copy-start(bf16[2,7168]{1,0:T(2,128)(2,1)} %param.13) | copy-start | bytes 86020
  5.9 3.4 %collective-permute-start = (f32[2,16,16]{2,1,0:T(8,128)S(1)}, f32[2,16,16]{2,1,0:T(8,128)S(1)}, u32[]{:S(2)}, u32[]{:S(2)}) collective-permute-start(f32[2,16,16]{2,1,0:T(8,128)S(1)} %pad_maximum_fusion), channel_id=1, source_target_pairs={{0,4},{4,0},{1,5},{5,1},{2,6},{6,2},{3,7},{7,3},{8,12},{12,8},{9,1... | collective-permute-start | bytes 6152 | tf_op jit(solution)/shard_map/ppermute | solution.py:18
  7.9 1.7 %collective-permute-start.1 = (bf16[16,16,512]{2,0,1:T(8,128)(2,1)S(1)}, bf16[16,16,512]{2,0,1:T(8,128)(2,1)}, u32[]{:S(2)}, u32[]{:S(2)}) collective-permute-start(bf16[16,16,512]{2,0,1:T(8,128)(2,1)S(1)} %bitcast.107), channel_id=1, source_target_pairs={{0,4},{4,0},{1,5},{5,1},{2,6},{6,2},{3,7},{7,3},{8,12},{12,8},{9,1... | collective-permute-start | bytes 786440 | tf_op jit(solution)/shard_map/ppermute | solution.py:18
  37.1 4.2 %collective-permute-start.2 = (bf16[16,16,2176]{2,1,0:T(8,128)(2,1)S(1)}, bf16[16,16,2176]{2,1,0:T(8,128)(2,1)}, u32[]{:S(2)}, u32[]{:S(2)}) collective-permute-start(bf16[16,16,2176]{2,1,0:T(8,128)(2,1)S(1)} %all_to_all.20), channel_id=1, source_target_pairs={{0,4},{4,0},{1,5},{5,1},{2,6},{6,2},{3,7},{7,3},{8,12},{12,8},{9,1... | collective-permute-start | bytes 3342344 | tf_op jit(solution)/shard_map/ppermute | solution.py:18
  44.8 8.8 %all-to-all-start.1 = ((bf16[4,64,256]{2,1,0:T(8,128)(2,1)}), bf16[4,64,256]{2,1,0:T(8,128)(2,1)S(1)}, u32[]{:S(2)}, u32[]{:S(2)}) async-start(bf16[4,64,256]{2,1,0:T(8,128)(2,1)} %bitcast.24), calls=%async_computation.1 | async-start | bytes 262144 | tf_op jit(solution)/shard_map/all_to_all | solution.py:236
  53.9 35.9 %copy-start.3 = (bf16[7168]{0:T(1024)(128)(2,1)S(1)}, bf16[7168]{0:T(1024)(128)(2,1)}, u32[]{:S(2)}) copy-start(bf16[7168]{0:T(1024)(128)(2,1)} %param.20) | copy-start | bytes 43012
  53.9 36.0 %copy-start.1 = (bf16[7168,16]{0,1:T(8,128)(2,1)S(1)}, bf16[7168,16]{0,1:T(8,128)(2,1)}, u32[]{:S(2)}) copy-start(bf16[7168,16]{0,1:T(8,128)(2,1)} %param.21) | copy-start | bytes 688132
  86.0 7.9 %collective-permute-start.3 = (bf16[16,256,256]{2,1,0:T(8,128)(2,1)}, bf16[16,256,256]{2,1,0:T(8,128)(2,1)}, u32[]{:S(2)}, u32[]{:S(2)}) collective-permute-start(bf16[16,256,256]{2,1,0:T(8,128)(2,1)} %bitcast.25.own), channel_id=1, source_target_pairs={{0,4},{4,0},{1,5},{5,1},{2,6},{6,2},{3,7},{7,3},{8,12},{12,8},{9,1... | collective-permute-start | bytes 6291464 | tf_op jit(solution)/shard_map/ppermute | solution.py:18
  114.3 4.3 %collective-permute-start.4 = (bf16[256,3584]{1,0:T(8,128)(2,1)}, bf16[256,3584]{1,0:T(8,128)(2,1)}, u32[]{:S(2)}, u32[]{:S(2)}) collective-permute-start(bf16[256,3584]{1,0:T(8,128)(2,1)} %down.2), channel_id=1, source_target_pairs={{0,4},{4,0},{1,5},{5,1},{2,6},{6,2},{3,7},{7,3},{8,12},{12,8},{9,1... | collective-permute-start | bytes 5505032 | tf_op jit(solution)/shard_map/ppermute | solution.py:18
  124.0 30.6 %all-to-all-start.3 = ((bf16[64,4,3584]{2,1,0:T(4,128)(2,1)}), bf16[64,4,3584]{2,1,0:T(4,128)(2,1)}, u32[]{:S(2)}, u32[]{:S(2)}) async-start(bf16[64,4,3584]{2,1,0:T(4,128)(2,1)} %down.3), calls=%async_computation.3 | async-start | bytes 3670016 | tf_op jit(solution)/shard_map/all_to_all | solution.py:256
  157.0 3.6 %collective-permute-start.5 = (f32[2,3584]{1,0:T(2,128)S(1)}, f32[2,3584]{1,0:T(2,128)S(1)}, u32[]{:S(2)}, u32[]{:S(2)}) collective-permute-start(f32[2,3584]{1,0:T(2,128)S(1)} %get-tuple-element.9), channel_id=1, source_target_pairs={{0,4},{4,0},{1,5},{5,1},{2,6},{6,2},{3,7},{7,3},{8,12},{12,8},{9,1... | collective-permute-start | bytes 86024 | tf_op jit(solution)/shard_map/ppermute | solution.py:18

commit v2 on v0

v2 whole, which is shorter than its diff:
```python
import jax
import jax.numpy as jnp
from jax import lax
from jax.experimental import pallas as pl
from jax.experimental.pallas import tpu as pltpu
from jax.sharding import PartitionSpec as P

DL = 512
DR = 64
DV = 128
BLOCK = 64
F32 = jnp.float32
BF16 = jnp.bfloat16
SWAP = [(0, 1), (1, 0)]


def swap(x):
    return lax.ppermute(x, "seq", SWAP)


def vmem():
    return pl.BlockSpec(memory_space=pltpu.VMEM)


def call(kernel, name, out_shape, idx, *operands, scratch=(), limit=24):
    many = isinstance(out_shape, (tuple, list))
    return pl.pallas_call(
        kernel,
        out_shape=out_shape,
        in_specs=[pl.BlockSpec(memory_space=pltpu.SMEM)] + [vmem() for _ in operands],
        out_specs=[vmem() for _ in out_shape] if many else vmem(),
        scratch_shapes=list(scratch),
        compiler_params=pltpu.CompilerParams(vmem_limit_bytes=limit * 2**20),
        name=name,
    )(idx, *operands)


def one_hot(shape, source):
    rows = lax.broadcasted_iota(jnp.int32, shape, 0)
    columns = lax.broadcasted_iota(jnp.int32, shape, 1)
    return jnp.where(source(rows) == columns, 1.0, 0.0).astype(BF16)


def parts_of(a):
    first = a.astype(BF16)
    rest = a - first.astype(F32)
    second = rest.astype(BF16)
    return first, second, (rest - second.astype(F32)).astype(BF16)


def attend_kernel(idx, queries, cache, sent, kept, kept_stats):
    drafts, heads, width = queries.shape
    side, length, first, second = idx[0], idx[2], idx[3], idx[4]
    shard_len = cache.shape[0]
    keys = jnp.concatenate(
        [
            cache[pl.ds(pl.multiple_of(first * BLOCK, BLOCK), BLOCK), :],
            cache[pl.ds(pl.multiple_of(second * BLOCK, BLOCK), BLOCK), :],
        ],
        0,
    )
    rows = queries[...].reshape(drafts * heads, width)
    scores = lax.dot_general(
        rows, keys, (((1,), (1,)), ((), ())), preferred_element_type=F32
    ) * ((DV + DR) ** (-0.5))
    row = lax.broadcasted_iota(jnp.int32, scores.shape, 0)
    col = lax.broadcasted_iota(jnp.int32, scores.shape, 1)
    block = jnp.where(col < BLOCK, first, second - 1)
    usable = side * shard_len + block * BLOCK + col < length - (drafts - 1) + row // heads
    top = jnp.max(jnp.where(usable, scores, -1e30), -1, keepdims=True)
    probs = jnp.where(usable, jnp.exp(scores - top), 0.0).astype(BF16)
    total = jnp.sum(probs.astype(F32), -1, keepdims=True)
    out = jnp.dot(probs, keys[:, :DL], preferred_element_type=F32)
    half = heads // 2

    def split(a):
        a = a.reshape(drafts, 2, half, a.shape[-1])
        low = a[:, 0].reshape(drafts * half, a.shape[-1])
        high = a[:, 1].reshape(drafts * half, a.shape[-1])
        return jnp.where(side == 0, low, high), jnp.where(side == 0, high, low)

    mine, theirs = split(out)
    stats = jnp.concatenate(
        [jnp.broadcast_to(top, (top.shape[0], 128)), jnp.broadcast_to(total, (top.shape[0], 128))],
        -1,
    )
    my_stats, their_stats = split(stats)
    kept[...] = mine
    kept_stats[...] = my_stats
    sent[:, :DL] = theirs.astype(BF16)
    top_parts, sum_parts = parts_of(their_stats[:, :128]), parts_of(their_stats[:, 128:])
    lane = lax.broadcasted_iota(jnp.int32, (drafts * half, 128), 1)
    packed = jnp.zeros((drafts * half, 128), F32)
    for place, part in enumerate(top_parts + sum_parts):
        packed = jnp.where(lane == place, part.astype(F32), packed)
    sent[:, DL:] = packed.astype(BF16)


def values_kernel(idx, kept, kept_stats, arrived, value_up, side_rows, fanned):
    rows = kept.shape[0]
    dests, slabs, drafts, _ = fanned.shape
    half = slabs - 1
    packed = arrived[:, DL:].astype(F32)
    lane = lax.broadcasted_iota(jnp.int32, packed.shape, 1)
    other_top = jnp.sum(jnp.where(lane < 3, packed, 0.0), -1, keepdims=True)
    other_sum = jnp.sum(jnp.where((lane >= 3) & (lane < 6), packed, 0.0), -1, keepdims=True)
    my_top, my_sum = kept_stats[:, 0:1], kept_stats[:, 128:129]
    top = jnp.maximum(my_top, other_top)
    my_scale, other_scale = jnp.exp(my_top - top), jnp.exp(other_top - top)
    total = my_scale * my_sum + other_scale * other_sum
    latent = (my_scale / total) * kept[...] + (other_scale / total) * arrived[:, :DL].astype(F32)
    latent = latent.astype(BF16)
    order = one_hot((rows, rows), lambda i: i % drafts * half + i // drafts)
    latent = jnp.dot(order, latent, preferred_element_type=F32).astype(BF16)
    for head in range(half):
        out = jnp.dot(
            latent[head * drafts : (head + 1) * drafts],
            value_up[idx[0] * half + head],
            preferred_element_type=F32,
        ).astype(BF16)
        for dest in range(dests):
            fanned[dest, head] = out
    for dest in range(dests):
        fanned[dest, half] = side_rows[dest]


def project_terms(gathered, out_proj_t, side):
    reqs, slabs, drafts, lanes = gathered.shape
    half = slabs - 1
    total = None
    for head in range(0, half, 2):
        pair = jnp.concatenate(
            [gathered[:, head].reshape(reqs * drafts, lanes), gathered[:, head + 1].reshape(reqs * drafts, lanes)],
            -1,
        )
        start = pl.multiple_of((side * half + head) * lanes, 256)
        term = lax.dot_general(
            pair,
            out_proj_t[:, pl.ds(start, 2 * lanes)],
            (((1,), (1,)), ((), ())),
            preferred_element_type=F32,
        )
        total = term if total is None else total + term
    return total


def project_own_kernel(idx, gathered, out_proj_t, out):
    out[...] = project_terms(gathered, out_proj_t, idx[0])


def project_both_kernel(idx, started, gathered, gathered_other, out_proj_t, terms, residual):
    reqs, slabs, drafts, lanes = gathered.shape
    exps, _, padded = terms.shape
    width = started.shape[1]
    side = idx[0]
    total = (started[...] + project_terms(gathered_other, out_proj_t, 1 - side)).astype(BF16)
    tokens = reqs * drafts
    own_rows = drafts // (2 * exps)

    def source(i):
        exp, req = i // (tokens // exps), i // (2 * own_rows) % reqs
        seq, row = i // own_rows % 2, i % own_rows
        return ((req * 2 + seq) * exps + exp) * own_rows + row

    total = jnp.dot(one_hot((tokens, tokens), source), total, preferred_element_type=F32)
    total = jnp.concatenate([total, jnp.zeros((tokens, padded - width), F32)], -1)
    terms[...] = total.astype(BF16).reshape(terms.shape)
    tiles = padded // lanes
    for tile in range(tiles):
        picked = jnp.zeros((tokens // exps, lanes), F32)
        for rows, from_side in ((gathered, side), (gathered_other, 1 - side)):

            def residual_source(i):
                req, seq, row = i // (2 * own_rows), i // own_rows % 2, i % own_rows
                place = req * drafts + (row * 2 + side) * tiles + tile
                return jnp.where(seq == from_side, place, -1)

            picked += jnp.dot(
                one_hot((tokens // exps, tokens), residual_source),
                rows[:, slabs - 1].reshape(tokens, lanes),
                preferred_element_type=F32,
            )
        residual[:, tile * lanes : (tile + 1) * lanes] = picked.astype(BF16)


def expert_terms(rows, gains, w_gate, w_up, router_t, side):
    steps, tokens, _ = rows.shape
    width = gains.shape[-1]

    def step(i, state):
        gate, up, logits, squares = state
        start = pl.multiple_of((i * 2 + side) * width, 32)
        hidden = rows[i][:, :width].astype(F32)
        scaled = (hidden * gains[i * 2 + side].astype(F32)).astype(BF16)
        gate += jnp.dot(scaled, w_gate[pl.ds(start, width), :], preferred_element_type=F32)
        up += jnp.dot(scaled, w_up[pl.ds(start, width), :], preferred_element_type=F32)
        logits += lax.dot_general(
            scaled, router_t[i * 2 + side], (((1,), (1,)), ((), ())), preferred_element_type=F32
        )
        return gate, up, logits, squares + hidden * hidden

    state = None
    for i in range(steps):
        if state is None:
            state = (
                jnp.zeros((tokens, w_gate.shape[1]), F32),
                jnp.zeros((tokens, w_up.shape[1]), F32),
                jnp.zeros((tokens, router_t.shape[1]), F32),
                jnp.zeros((tokens, width), F32),
            )
        state = step(i, state)
    gate, up, logits, squares = state
    return gate, up, logits, jnp.sum(squares, -1, keepdims=True)


def gate_up_own_kernel(idx, own, gains, w_gate, w_up, router_t, gate, up, logits, squares):
    a, b, c, d = expert_terms(own, gains, w_gate, w_up, router_t, idx[0])
    gate[...], up[...], logits[...] = a, b, c
    squares[...] = jnp.broadcast_to(d, squares.shape)


def gate_up_both_kernel(idx, gate, up, logits, squares, own, other, gains, w_gate, w_up, router_t, act):
    width = gains.shape[-1]
    experts = logits.shape[1]
    columns = gains.shape[0] * width
    a, b, c, d = expert_terms(other, gains, w_gate, w_up, router_t, 1 - idx[0])
    scale = lax.rsqrt((squares[:, 0:1] + d) / columns + 1e-06)
    named = own[0, :, width : width + experts].astype(F32)
    chosen = named * jax.nn.sigmoid((logits[...] + c) * scale)
    mine = lax.broadcasted_iota(jnp.int32, chosen.shape, 1) == idx[1]
    weight = jnp.sum(jnp.where(mine, chosen, 0.0), -1, keepdims=True)
    weight = weight / jnp.sum(chosen, -1, keepdims=True) * 2.5
    act[...] = (
        jax.nn.silu((gate[...] + a) * scale) * ((up[...] + b) * scale) * weight
    ).astype(BF16)


DOWN_STEPS = 7


def down_first_kernel(idx, act, w_down, out):
    block = out.shape[1] // DOWN_STEPS
    for i in range(DOWN_STEPS):
        start = pl.multiple_of(((1 - idx[0]) * DOWN_STEPS + i) * block, 128)
        out[:, i * block : (i + 1) * block] = jnp.dot(
            act[...], w_down[:, pl.ds(start, block)], preferred_element_type=F32
        ).astype(BF16)


def down_second_kernel(idx, act, w_down, arrived, out):
    block = arrived.shape[1] // DOWN_STEPS
    for i in range(DOWN_STEPS):
        start = pl.multiple_of((idx[0] * DOWN_STEPS + i) * block, 128)
        total = jnp.dot(act[...], w_down[:, pl.ds(start, block)], preferred_element_type=F32)
        total += arrived[:, i * block : (i + 1) * block].astype(F32)
        out[:, :, i * block : (i + 1) * block] = total.reshape(out.shape[:2] + (block,)).astype(BF16)


def per_device(
    residual,
    queries,
    latent_cache,
    blocks,
    lengths,
    value_up,
    out_proj,
    norm_gain,
    router,
    expert_ids,
    w_gate,
    w_up,
    w_down,
):
    drafts, heads, qk_width = queries.shape[1:]
    n_req, n_exp = lax.axis_size("req"), lax.axis_size("exp")
    s = lax.axis_index("seq")
    x = lax.axis_index("exp")
    r = lax.axis_index("req")
    model_width = residual.shape[1]
    experts = router.shape[1]
    width = out_proj.shape[1]
    padded = -(-width // 128) * 128
    own_rows = residual.shape[0]
    tokens = n_req * drafts
    half_heads = heads // 2
    shape = jax.ShapeDtypeStruct

    idx = jnp.concatenate([jnp.stack([s, r]).astype(jnp.int32), lengths, blocks.reshape(-1)])
    half_rows = drafts * half_heads
    sent, kept, kept_stats = call(
        attend_kernel,
        "attend",
        (
            shape((half_rows, DL + 128), BF16),
            shape((half_rows, DL), F32),
            shape((half_rows, 256), F32),
        ),
        idx,
        queries[0],
        latent_cache[0],
    )
    arrived = swap(sent)

    named = jnp.sum(
        (expert_ids[:, :, None] == jnp.arange(experts, dtype=jnp.int32)).astype(F32), 1
    ).astype(BF16)
    columns = residual.reshape(own_rows, n_req * 2, width)
    named = jnp.broadcast_to(named[:, None], (own_rows, n_req * 2, experts))
    spare = jnp.zeros((own_rows, n_req * 2, padded - width - experts), BF16)
    side_rows = jnp.concatenate([columns, named, spare], -1)
    side_rows = side_rows.reshape(own_rows, n_req, 2 * padded // 128, 128).transpose(1, 0, 2, 3)
    side_rows = side_rows.reshape(n_req, own_rows * 2 * padded // 128, 128)
    side_rows = jnp.pad(side_rows, ((0, 0), (0, drafts - side_rows.shape[1]), (0, 0)))
    fanned = call(
        values_kernel,
        "values",
        shape((n_req, half_heads + 1, drafts, DV), BF16),
        idx,
        kept,
        kept_stats,
        arrived,
        value_up,
        side_rows,
    )
    gathered = lax.all_to_all(fanned, "req", split_axis=0, concat_axis=0, tiled=True)
    gathered_other = swap(gathered)
    out_proj_t = out_proj.T
    started = call(
        project_own_kernel, "project_own", shape((tokens, width), F32), idx, gathered, out_proj_t
    )
    terms, resid = call(
        project_both_kernel,
        "project_both",
        (
            shape((n_exp, tokens // n_exp, padded), BF16),
            shape((tokens // n_exp, padded), BF16),
        ),
        idx,
        started,
        gathered,
        gathered_other,
        out_proj_t,
    )
    gains = norm_gain.reshape(n_req * 2, 1, width)
    router_t = router.T.reshape(experts, n_req * 2, width).transpose(1, 0, 2)
    terms, resid, idx, gains, router_t = lax.optimization_barrier(
        (terms, resid, idx, gains, router_t)
    )
    terms = lax.all_to_all(terms, "exp", split_axis=0, concat_axis=0, tiled=True)
    attended = jnp.sum(terms.astype(F32), 0).astype(BF16)
    hidden_sum = (resid.astype(F32) + attended.astype(F32)).astype(BF16)

    fanned = jnp.broadcast_to(hidden_sum[None], (n_req * n_exp,) + hidden_sum.shape)
    own = lax.all_to_all(fanned, ("req", "exp"), split_axis=0, concat_axis=0, tiled=True)
    own = own.reshape(n_req, tokens, padded)
    other = swap(own)
    w_gate, w_up, w_down = w_gate[0], w_up[0], w_down[0]
    hidden_units = w_gate.shape[1]
    started = call(
        gate_up_own_kernel,
        "gate_up_own",
        (
            shape((tokens, hidden_units), F32),
            shape((tokens, hidden_units), F32),
            shape((tokens, experts), F32),
            shape((tokens, 128), F32),
        ),
        idx,
        own,
        gains,
        w_gate,
        w_up,
        router_t,
    )
    act = call(
        gate_up_both_kernel,
        "gate_up_both",
        shape((tokens, hidden_units), BF16),
        idx,
        *started,
        own,
        other,
        gains,
        w_gate,
        w_up,
        router_t,
    )
    half = model_width // 2
    first = call(down_first_kernel, "down_first", shape((tokens, half), BF16), idx, act, w_down)
    pieces = call(
        down_second_kernel,
        "down_second",
        shape((tokens // 4, 4, half), BF16),
        idx,
        act,
        w_down,
        swap(first),
    )
    place = ((x * n_req + r) * 2 + s) * own_rows
    hid_own = lax.dynamic_slice_in_dim(own, place, own_rows, 1)[:, :, :width]
    hid_other = lax.dynamic_slice_in_dim(other, place, own_rows, 1)[:, :, :width]
    hid = jnp.where(s == 0, jnp.stack([hid_own, hid_other], 1), jnp.stack([hid_other, hid_own], 1))
    hid = hid.transpose(2, 0, 1, 3).reshape(own_rows, model_width)
    pieces = lax.all_to_all(pieces, ("exp", "req"), split_axis=0, concat_axis=0, tiled=True)
    routed = jnp.sum(pieces.astype(F32), 0)
    routed = routed.reshape(2, own_rows, half)
    routed_mine = lax.dynamic_index_in_dim(routed, s, 0, False)
    routed_theirs = swap(lax.dynamic_index_in_dim(routed, 1 - s, 0, False))
    routed = jnp.where(
        s == 0,
        jnp.concatenate([routed_mine, routed_theirs], -1),
        jnp.concatenate([routed_theirs, routed_mine], -1),
    )
    return (hid.astype(F32) + routed).astype(BF16)


def solution(mesh):
    in_specs = (
        P(("req", "seq", "exp"), None),
        P("req", None, "exp", None),
        P("req", "seq", None),
        P("req", "seq", None),
        P("req"),
        P("exp", None, None),
        P("exp", ("req", "seq")),
        P(),
        P(),
        P(("req", "seq", "exp"), None),
        P("req", None, ("seq", "exp")),
        P("req", None, ("seq", "exp")),
        P("req", ("seq", "exp"), None),
    )
    out_specs = P(("req", "seq", "exp"), None)
    return jax.shard_map(
        per_device, mesh=mesh, in_specs=in_specs, out_specs=out_specs, check_vma=False
    )
```

time: 257 us -> 141 us (0.55)
  waiting for transfers between devices: 111 us -> 30.1 us
  matrix products: 24 us -> 0 us
  Pallas kernels: 0 us -> 13.7 us
  local copies, waits for them, and re-layouts: 24.2 us -> 10.7 us
  between operations: 14.4 us -> 0.97 us
  blocking collectives: 56.5 us -> 66 us
  other arithmetic: 12.3 us -> 4.57 us
    all_gather x2 -> x0, waiting for transfers between devices: 54.6 us -> none  [the longest x1 44.1 us: per_device(): lax.all_gather(flat_values, 'req', axis=0, tiled=True)]
    all_to_all x2 -> x1, waiting for transfers between devices: 56.2 us -> 24.9 us  [per_device(): lax.all_to_all(pieces, ('exp', 'req'), split_axis=0, concat_axis=0, tiled...]
    dot_general x9 -> x0, matrix products: 24 us -> none  [the longest x1 10 us: expert_rows(): jnp.dot(activated, w_down[0], preferred_element_type=jnp.float32)]
    reshape x3 -> x6, local copies, waits for them, and re-layouts: 16.7 us -> 1.53 us  [the longest x1 0.85 us: per_device(): columns = residual.reshape(own_rows, n_req * 2, width)]
    all_to_all x1 -> x3, blocking collectives: 51.8 us -> 66 us  [the longest x1 32.1 us: per_device(): lax.all_to_all(fanned, ('req', 'exp'), split_axis=0, concat_axis=0, tiled...]
    pallas_call x0 -> x8, Pallas kernels: none -> 13.7 us  [call(): pl.pallas_call(kernel, out_shape=out_shape, in_specs=[pl.BlockSpec(memory...]
    ppermute x0 -> x5, starting transfers between devices: none -> 8.47 us  [swap(): return lax.ppermute(x, 'seq', SWAP)]
    all_to_all x2 -> x1, starting transfers between devices: 13.9 us -> 5.52 us  [per_device(): lax.all_to_all(pieces, ('exp', 'req'), split_axis=0, concat_axis=0, tiled...]
  transfers between devices with their start and end apart: 4 -> 6, of which waited for: 4 -> 4; matrix products, arithmetic and copies ran while one was open for 1% -> 3% of each run, Pallas kernels for 0% -> 2%
where the time goes in v2:
time: 141 us; the launch traced here: 140 us
  blocking collectives  66 us (47%)
  waiting for transfers between devices  30.1 us (21%)
  starting transfers between devices  14 us (10%)
  Pallas kernels  13.7 us (10%)
  local copies, waits for them, and re-layouts  10.7 us (8%)
  other arithmetic  4.57 us (3%)
    all_to_all x1, blocking collectives, per_device(): lax.all_to_all(fanned, ('req', 'exp'), split_axis=0, concat_axis=0, tiled...  32.1 us
    all_to_all x1, blocking collectives, per_device(): lax.all_to_all(fanned, 'req', split_axis=0, concat_axis=0, tiled=True)  25.2 us
    all_to_all x1, waiting for transfers between devices, per_device(): lax.all_to_all(pieces, ('exp', 'req'), split_axis=0, concat_axis=0, tiled...  24.9 us
    pallas_call x8, Pallas kernels, call(): pl.pallas_call(kernel, out_shape=out_shape, in_specs=[pl.BlockSpec(memory...  13.7 us
    all_to_all x1, blocking collectives, per_device(): lax.all_to_all(terms, 'exp', split_axis=0, concat_axis=0, tiled=True)  8.64 us
    ppermute x5, starting transfers between devices, swap(): return lax.ppermute(x, 'seq', SWAP)  8.47 us
    unnamed x22, local copies, waits for them, and re-layouts  7.64 us
    all_to_all x1, starting transfers between devices, per_device(): lax.all_to_all(pieces, ('exp', 'req'), split_axis=0, concat_axis=0, tiled...  5.52 us
  transfers between devices with their start and end apart: 6, of which 4 were waited for; matrix products, arithmetic and copies ran while one was open for 3% of the time, Pallas kernels for 2%

profile of v2, /device:TPU:1, one launch (start us, length us, event | category | flops | bytes accessed | tf_op | source)
XLA Modules:
  0.0 140.0 jit_solution(16699507137738581781)
XLA Ops:
  1.4 1.1 copy-done.7
  2.5 0.9 copy-done.8
  3.4 1.5 %attend.1 = (bf16[256,640]{1,0:T(8,128)(2,1)S(1)}, f32[256,512]{1,0:T(8,128)S(1)}, f32[256,256]{1,0:T(8,128)S(1)}) custom-call(s32[5]{0:T(128)S(1)} %pad_add_fusion.idx, bf16[16,32,576]{2,1,0:T(8,128)(2,1)S(1)} %bitcast.40, bf16[192,576]{1,0:T(8,128)(2,1)S(1)} %bitcast.41), custom_call_target="tpu_custom_call" | custom-call | tf_op jit(solution)/shard_map/attend/pallas_call | solution.py:27
  4.9 1.5 %collective-permute-start = (bf16[256,640]{1,0:T(8,128)(2,1)S(1)}, bf16[256,640]{1,0:T(8,128)(2,1)S(1)}, u32[]{:S(2)}, u32[]{:S(2)}) collective-permute-start(bf16[256,640]{1,0:T(8,128)(2,1)S(1)} %get-tuple-element.21), channel_id=1, source_target_pairs={{0,4},{4,0},{1,5},{5,1},{2,6},{6,2},{3,7},{7,3},{8,12},{12,8},{9,1... | collective-permute-start | bytes 983048 | tf_op jit(solution)/shard_map/ppermute | solution.py:18
  8.2 2.2 %copy-done.5 = bf16[32,512,128]{2,1,0:T(8,128)(2,1)S(1)} copy-done((bf16[32,512,128]{2,1,0:T(8,128)(2,1)S(1)}, bf16[32,512,128]{2,1,0:T(8,128)(2,1)}, u32[]{:S(2)}) %copy-start.5) | copy-done | bytes 4194328
  10.4 1.3 values.1
  11.8 25.2 %all_to_all.20.gathered = bf16[16,17,16,128]{3,2,1,0:T(8,128)(2,1)S(1)} all-to-all(bf16[16,17,16,128]{3,2,1,0:T(8,128)(2,1)S(1)} %values.1), channel_id=1, replica_groups=mesh['req'=16,'seq'=2,'exp'=4] {'req'}, dimensions={0} | all-to-all | bytes 2228224 | tf_op jit(solution)/shard_map/all_to_all | solution.py:325
  37.0 1.4 collective-permute-start.1
  39.0 1.0 project_own.1.started
  40.9 2.1 %project_both.1 = (bf16[4,64,256]{2,1,0:T(8,128)(2,1)S(1)}, bf16[64,256]{1,0:T(8,128)(2,1)S(1)}) custom-call(s32[5]{0:T(128)S(1)} %pad_add_fusion.idx, f32[256,224]{1,0:T(8,128)S(1)} %project_own.1.started, bf16[16,17,16,128]{3,2,1,0:T(8,128)(2,1)S(1)} %all_to_all.20.gathered, bf16[16,17,16,128]{3,2,1,0:T(8,128)(2,1)} %collective-permute-done.1.gathered_other, ...), custom_call_target="tpu_custom_call" | custom-call | tf_op jit(solution)/shard_map/project_both/pallas_call | solution.py:27
  43.0 8.6 %all_to_all.21 = bf16[4,64,256]{2,1,0:T(8,128)(2,1)S(1)} all-to-all(bf16[4,64,256]{2,1,0:T(8,128)(2,1)S(1)} %get-tuple-element.25), channel_id=1, replica_groups=mesh['req'=16,'seq'=2,'exp'=4] {'exp'}, dimensions={0} | all-to-all | bytes 262144 | tf_op jit(solution)/shard_map/all_to_all | solution.py:349
  51.9 32.1 %all_to_all.22 = bf16[64,64,256]{2,1,0:T(8,128)(2,1)S(1)} all-to-all(bf16[64,64,256]{2,1,0:T(8,128)(2,1)S(1)} %broadcast_in_dim.8), channel_id=1, replica_groups=mesh['req'=16,'seq'=2,'exp'=4] {'req','exp'}, dimensions={0} | all-to-all | bytes 4194304 | tf_op jit(solution)/shard_map/all_to_all | solution.py:354
  84.0 3.8 %collective-permute-start.2 = (bf16[16,256,256]{2,1,0:T(8,128)(2,1)S(1)}, bf16[16,256,256]{2,1,0:T(8,128)(2,1)S(1)}, u32[]{:S(2)}, u32[]{:S(2)}) collective-permute-start(bf16[16,256,256]{2,1,0:T(8,128)(2,1)S(1)} %bitcast.26), channel_id=1, source_target_pairs={{0,4},{4,0},{1,5},{5,1},{2,6},{6,2},{3,7},{7,3},{8,12},{12,8},{9,1... | collective-permute-start | bytes 6291464 | tf_op jit(solution)/shard_map/ppermute | solution.py:18
  87.8 2.0 %copy-done.1 = bf16[1,7168,256]{2,1,0:T(8,128)(2,1)S(1)} copy-done((bf16[1,7168,256]{2,1,0:T(8,128)(2,1)S(1)}, bf16[1,7168,256]{2,1,0:T(8,128)(2,1)}, u32[]{:S(2)}) %copy-start.1) | copy-done | bytes 3670040
  89.9 2.3 %gate_up_own.1 = (f32[256,256]{1,0:T(8,128)S(1)}, f32[256,256]{1,0:T(8,128)S(1)}, f32[256,16]{1,0:T(8,128)S(1)}, f32[256,128]{1,0:T(8,128)S(1)}) custom-call(s32[5]{0:T(128)S(1)} %pad_add_fusion.idx, bf16[16,256,256]{2,1,0:T(8,128)(2,1)S(1)} %bitcast.27, bf16[32,1,224]{2,1,0:T(2,128)(2,1)S(1)} %copy.22.gains, bf16[7168,256]{1,0:T(8,128)(2,1)S(1)} %bitcast.30, ...), custom_call_target="tpu_custom_call" | custom-call | tf_op jit(solution)/shard_map/gate_up_own/pallas_call | solution.py:27
  92.2 2.7 %gate_up_both.1.act = bf16[256,256]{1,0:T(8,128)(2,1)S(1)} custom-call(s32[5]{0:T(128)S(1)} %pad_add_fusion.idx, f32[256,256]{1,0:T(8,128)S(1)} %get-tuple-element.29.gate, f32[256,256]{1,0:T(8,128)S(1)} %get-tuple-element.30.up, f32[256,16]{1,0:T(8,128)S(1)} %get-tuple-element.31.logits, f32[256,128]{1,0:T(8,128)S(1)} %get-tuple-element.32.squares, ...), custom_call_target="tpu_custom_call" | custom-call | tf_op jit(solution)/shard_map/gate_up_both/pallas_call | solution.py:27
  95.0 1.2 down_first.1
  96.3 3.8 %collective-permute-done.3.arrived = bf16[256,3584]{1,0:T(8,128)(2,1)S(1)} collective-permute-done((bf16[256,3584]{1,0:T(8,128)(2,1)S(1)}, bf16[256,3584]{1,0:T(8,128)(2,1)S(1)}, u32[]{:S(2)}, u32[]{:S(2)}) %collective-permute-start.3) | collective-permute-done | bytes 1835040 | tf_op jit(solution)/shard_map/ppermute | solution.py:18
  100.1 1.6 %down_second.1 = bf16[64,4,3584]{2,1,0:T(4,128)(2,1)S(1)} custom-call(s32[5]{0:T(128)S(1)} %pad_add_fusion.idx, bf16[256,256]{1,0:T(8,128)(2,1)S(1)} %gate_up_both.1.act, bf16[256,7168]{1,0:T(8,128)(2,1)S(1)} %bitcast.35, bf16[256,3584]{1,0:T(8,128)(2,1)S(1)} %collective-permute-done.3.arrived), custom_call_target="tpu_custom_call" | custom-call | tf_op jit(solution)/shard_map/down_second/pallas_call | solution.py:27
  101.7 1.2 copy-done.4
  103.0 5.5 %all-to-all-start.3 = ((bf16[64,4,3584]{2,1,0:T(4,128)(2,1)}), bf16[64,4,3584]{2,1,0:T(4,128)(2,1)}, u32[]{:S(2)}, u32[]{:S(2)}) async-start(bf16[64,4,3584]{2,1,0:T(4,128)(2,1)} %copy-done.4), calls=%async_computation.3 | async-start | bytes 3670016 | tf_op jit(solution)/shard_map/all_to_all | solution.py:404
  109.4 24.9 %all-to-all-done.3 = bf16[64,4,3584]{2,1,0:T(4,128)(2,1)} async-done(((bf16[64,4,3584]{2,1,0:T(4,128)(2,1)}), bf16[64,4,3584]{2,1,0:T(4,128)(2,1)}, u32[]{:S(2)}, u32[]{:S(2)}) %all-to-all-start.3) | async-done | bytes 1835040 | tf_op jit(solution)/shard_map/all_to_all | solution.py:404
  134.3 2.3 %convert_reduce_fusion = f32[4,3584]{1,0:T(4,128)S(1)} fusion(bf16[64,4,3584]{2,1,0:T(4,128)(2,1)} %all-to-all-done.3), kind=kLoop, calls=%fused_computation | loop fusion | flops 1820672 | bytes 1892352 | tf_op jit(solution)/shard_map/reduce_sum | solution.py:405
  136.6 1.8 %collective-permute-start.4 = (f32[2,3584]{1,0:T(2,128)S(1)}, f32[2,3584]{1,0:T(2,128)S(1)}, u32[]{:S(2)}, u32[]{:S(2)}) collective-permute-start(f32[2,3584]{1,0:T(2,128)S(1)} %get-tuple-element.34), channel_id=1, source_target_pairs={{0,4},{4,0},{1,5},{5,1},{2,6},{6,2},{3,7},{7,3},{8,12},{12,8},{9,1... | collective-permute-start | bytes 86024 | tf_op jit(solution)/shard_map/ppermute | solution.py:18
  (47 shorter events, 7.0 us)
Async XLA Ops:
  1.4 1.1 copy-start.7
  2.5 0.9 copy-start.8
  4.9 3.3 %collective-permute-start = (bf16[256,640]{1,0:T(8,128)(2,1)S(1)}, bf16[256,640]{1,0:T(8,128)(2,1)S(1)}, u32[]{:S(2)}, u32[]{:S(2)}) collective-permute-start(bf16[256,640]{1,0:T(8,128)(2,1)S(1)} %get-tuple-element.21), channel_id=1, source_target_pairs={{0,4},{4,0},{1,5},{5,1},{2,6},{6,2},{3,7},{7,3},{8,12},{12,8},{9,1... | collective-permute-start | bytes 983048 | tf_op jit(solution)/shard_map/ppermute | solution.py:18
  8.2 2.2 %copy-start.5 = (bf16[32,512,128]{2,1,0:T(8,128)(2,1)S(1)}, bf16[32,512,128]{2,1,0:T(8,128)(2,1)}, u32[]{:S(2)}) copy-start(bf16[32,512,128]{2,1,0:T(8,128)(2,1)} %value_up.1) | copy-start | bytes 12582916
  11.7 26.6 %copy-start.10 = (bf16[7168]{0:T(1024)(128)(2,1)S(1)}, bf16[7168]{0:T(1024)(128)(2,1)}, u32[]{:S(2)}) copy-start(bf16[7168]{0:T(1024)(128)(2,1)} %param.20) | copy-start | bytes 43012
  11.8 26.7 %copy-start.9 = (bf16[7168,16]{0,1:T(8,128)(2,1)S(1)}, bf16[7168,16]{0,1:T(8,128)(2,1)}, u32[]{:S(2)}) copy-start(bf16[7168,16]{0,1:T(8,128)(2,1)} %param.21) | copy-start | bytes 688132
  11.8 27.3 %copy-start.3 = (bf16[4096,224]{0,1:T(8,128)(2,1)S(1)}, bf16[4096,224]{0,1:T(8,128)(2,1)}, u32[]{:S(2)}) copy-start(bf16[4096,224]{0,1:T(8,128)(2,1)} %param.19) | copy-start | bytes 5505028
  37.0 3.9 %collective-permute-start.1 = (bf16[16,17,16,128]{3,2,1,0:T(8,128)(2,1)S(1)}, bf16[16,17,16,128]{3,2,1,0:T(8,128)(2,1)}, u32[]{:S(2)}, u32[]{:S(2)}) collective-permute-start(bf16[16,17,16,128]{3,2,1,0:T(8,128)(2,1)S(1)} %all_to_all.20.gathered), channel_id=1, source_target_pairs={{0,4},{4,0},{1,5},{5,1},{2,6},{6,2},{3,7},{7,3},{8,12},{12,8},{9,1... | collective-permute-start | bytes 3342344 | tf_op jit(solution)/shard_map/ppermute | solution.py:18
  51.9 35.9 %copy-start = (bf16[1,7168,256]{2,1,0:T(8,128)(2,1)S(1)}, bf16[1,7168,256]{2,1,0:T(8,128)(2,1)}, u32[]{:S(2)}) copy-start(bf16[1,7168,256]{2,1,0:T(8,128)(2,1)} %param.23) | copy-start | bytes 11010052
  84.0 8.2 %collective-permute-start.2 = (bf16[16,256,256]{2,1,0:T(8,128)(2,1)S(1)}, bf16[16,256,256]{2,1,0:T(8,128)(2,1)S(1)}, u32[]{:S(2)}, u32[]{:S(2)}) collective-permute-start(bf16[16,256,256]{2,1,0:T(8,128)(2,1)S(1)} %bitcast.26), channel_id=1, source_target_pairs={{0,4},{4,0},{1,5},{5,1},{2,6},{6,2},{3,7},{7,3},{8,12},{12,8},{9,1... | collective-permute-start | bytes 6291464 | tf_op jit(solution)/shard_map/ppermute | solution.py:18
  87.8 2.0 %copy-start.1 = (bf16[1,7168,256]{2,1,0:T(8,128)(2,1)S(1)}, bf16[1,7168,256]{2,1,0:T(8,128)(2,1)}, u32[]{:S(2)}) copy-start(bf16[1,7168,256]{2,1,0:T(8,128)(2,1)} %param.24) | copy-start | bytes 11010052
  92.2 2.7 %copy-start.6 = (bf16[16,256,256]{2,1,0:T(8,128)(2,1)}, bf16[16,256,256]{2,1,0:T(8,128)(2,1)S(1)}, u32[]{:S(2)}) copy-start(bf16[16,256,256]{2,1,0:T(8,128)(2,1)S(1)} %collective-permute-done.2.other) | copy-start | bytes 6291460
  92.2 2.8 %copy-start.2 = (bf16[1,256,7168]{2,1,0:T(8,128)(2,1)S(1)}, bf16[1,256,7168]{2,1,0:T(8,128)(2,1)}, u32[]{:S(2)}) copy-start(bf16[1,256,7168]{2,1,0:T(8,128)(2,1)} %param.25) | copy-start | bytes 11010052
  96.2 3.9 %collective-permute-start.3 = (bf16[256,3584]{1,0:T(8,128)(2,1)S(1)}, bf16[256,3584]{1,0:T(8,128)(2,1)S(1)}, u32[]{:S(2)}, u32[]{:S(2)}) collective-permute-start(bf16[256,3584]{1,0:T(8,128)(2,1)S(1)} %down_first.1), channel_id=1, source_target_pairs={{0,4},{4,0},{1,5},{5,1},{2,6},{6,2},{3,7},{7,3},{8,12},{12,8},{9,1... | collective-permute-start | bytes 5505032 | tf_op jit(solution)/shard_map/ppermute | solution.py:18
  101.7 1.3 copy-start.4
  103.0 31.3 %all-to-all-start.3 = ((bf16[64,4,3584]{2,1,0:T(4,128)(2,1)}), bf16[64,4,3584]{2,1,0:T(4,128)(2,1)}, u32[]{:S(2)}, u32[]{:S(2)}) async-start(bf16[64,4,3584]{2,1,0:T(4,128)(2,1)} %copy-done.4), calls=%async_computation.3 | async-start | bytes 3670016 | tf_op jit(solution)/shard_map/all_to_all | solution.py:404
  136.6 2.7 %collective-permute-start.4 = (f32[2,3584]{1,0:T(2,128)S(1)}, f32[2,3584]{1,0:T(2,128)S(1)}, u32[]{:S(2)}, u32[]{:S(2)}) collective-permute-start(f32[2,3584]{1,0:T(2,128)S(1)} %get-tuple-element.34), channel_id=1, source_target_pairs={{0,4},{4,0},{1,5},{5,1},{2,6},{6,2},{3,7},{7,3},{8,12},{12,8},{9,1... | collective-permute-start | bytes 86024 | tf_op jit(solution)/shard_map/ppermute | solution.py:18

commit v3 on v2

--- a/solution.py
+++ b/solution.py
@@ -22,17 +22,19 @@
     return pl.BlockSpec(memory_space=pltpu.VMEM)
 
 
-def call(kernel, name, out_shape, idx, *operands, scratch=(), limit=24):
+def call(kernel, name, out_shape, idx, *operands, outside=(), scratch=(), limit=24):
     many = isinstance(out_shape, (tuple, list))
     return pl.pallas_call(
         kernel,
         out_shape=out_shape,
-        in_specs=[pl.BlockSpec(memory_space=pltpu.SMEM)] + [vmem() for _ in operands],
+        in_specs=[pl.BlockSpec(memory_space=pltpu.SMEM)]
+        + [pl.BlockSpec(memory_space=pltpu.HBM) for _ in outside]
+        + [vmem() for _ in operands],
         out_specs=[vmem() for _ in out_shape] if many else vmem(),
         scratch_shapes=list(scratch),
         compiler_params=pltpu.CompilerParams(vmem_limit_bytes=limit * 2**20),
         name=name,
-    )(idx, *operands)
+    )(idx, *[pltpu.with_memory_space_constraint(a, pltpu.HBM) for a in outside], *operands)
 
 
 def one_hot(shape, source):
@@ -48,18 +50,35 @@
     return first, second, (rest - second.astype(F32)).astype(BF16)
 
 
-def attend_kernel(idx, queries, cache, sent, kept, kept_stats):
+def attend_kernel(
+    idx, queries, cache, value_up, sent, kept, kept_stats, value_half, query_rows, key_rows, sems
+):
     drafts, heads, width = queries.shape
     side, length, first, second = idx[0], idx[2], idx[3], idx[4]
     shard_len = cache.shape[0]
-    keys = jnp.concatenate(
-        [
-            cache[pl.ds(pl.multiple_of(first * BLOCK, BLOCK), BLOCK), :],
-            cache[pl.ds(pl.multiple_of(second * BLOCK, BLOCK), BLOCK), :],
-        ],
-        0,
-    )
-    rows = queries[...].reshape(drafts * heads, width)
+    copies = [
+        pltpu.make_async_copy(
+            cache.at[pl.ds(pl.multiple_of(first * BLOCK, BLOCK), BLOCK), :],
+            key_rows.at[pl.ds(0, BLOCK), :],
+            sems.at[0],
+        ),
+        pltpu.make_async_copy(
+            cache.at[pl.ds(pl.multiple_of(second * BLOCK, BLOCK), BLOCK), :],
+            key_rows.at[pl.ds(BLOCK, BLOCK), :],
+            sems.at[1],
+        ),
+        pltpu.make_async_copy(queries, query_rows, sems.at[2]),
+    ]
+    value_copy = pltpu.make_async_copy(
+        value_up.at[pl.ds(side * (heads // 2), heads // 2)], value_half, sems.at[3]
+    )
+    for copy in copies:
+        copy.start()
+    value_copy.start()
+    for copy in copies:
+        copy.wait()
+    keys = key_rows[...]
+    rows = query_rows[...].reshape(drafts * heads, width)
     scores = lax.dot_general(
         rows, keys, (((1,), (1,)), ((), ())), preferred_element_type=F32
     ) * ((DV + DR) ** (-0.5))
@@ -94,6 +113,7 @@
     for place, part in enumerate(top_parts + sum_parts):
         packed = jnp.where(lane == place, part.astype(F32), packed)
     sent[:, DL:] = packed.astype(BF16)
+    value_copy.wait()
 
 
 def values_kernel(idx, kept, kept_stats, arrived, value_up, side_rows, fanned):
@@ -115,7 +135,7 @@
     for head in range(half):
         out = jnp.dot(
             latent[head * drafts : (head + 1) * drafts],
-            value_up[idx[0] * half + head],
+            value_up[head],
             preferred_element_type=F32,
         ).astype(BF16)
         for dest in range(dests):
@@ -183,7 +203,7 @@
         residual[:, tile * lanes : (tile + 1) * lanes] = picked.astype(BF16)
 
 
-def expert_terms(rows, gains, w_gate, w_up, router_t, side):
+def expert_terms(rows, gains, w_gate, w_up, router_t, side, copies=()):
     steps, tokens, _ = rows.shape
     width = gains.shape[-1]
 
@@ -201,6 +221,8 @@
 
     state = None
     for i in range(steps):
+        if copies and i % (steps // len(copies)) == 0:
+            copies[i * len(copies) // steps].wait()
         if state is None:
             state = (
                 jnp.zeros((tokens, w_gate.shape[1]), F32),
@@ -213,13 +235,35 @@
     return gate, up, logits, jnp.sum(squares, -1, keepdims=True)
 
 
-def gate_up_own_kernel(idx, own, gains, w_gate, w_up, router_t, gate, up, logits, squares):
-    a, b, c, d = expert_terms(own, gains, w_gate, w_up, router_t, idx[0])
+UP_COPIES = 4
+
+
+def gate_up_own_kernel(
+    idx, w_up_there, own, gains, w_gate, router_t, gate, up, logits, squares, w_up, sems
+):
+    rows = w_up.shape[0] // UP_COPIES
+    copies = []
+    for i in range(UP_COPIES):
+        part = pl.ds(i * rows, rows)
+        copies.append(pltpu.make_async_copy(w_up_there.at[part], w_up.at[part], sems.at[i]))
+    for copy in copies:
+        copy.start()
+    a, b, c, d = expert_terms(own, gains, w_gate, w_up, router_t, idx[0], copies)
     gate[...], up[...], logits[...] = a, b, c
     squares[...] = jnp.broadcast_to(d, squares.shape)
 
 
-def gate_up_both_kernel(idx, gate, up, logits, squares, own, other, gains, w_gate, w_up, router_t, act):
+def gate_up_both_kernel(
+    idx, w_down_there, w_down_other_there, gate, up, logits, squares, own, other, gains, w_gate,
+    w_up, router_t, act, w_down, w_down_other, sems,
+):
+    half = pl.ds(pl.multiple_of(idx[0] * w_down.shape[1], 128), w_down.shape[1])
+    copies = [
+        pltpu.make_async_copy(w_down_there.at[:, half], w_down, sems.at[0]),
+        pltpu.make_async_copy(w_down_other_there.at[:, half], w_down_other, sems.at[1]),
+    ]
+    for copy in copies:
+        copy.start()
     width = gains.shape[-1]
     experts = logits.shape[1]
     columns = gains.shape[0] * width
@@ -233,26 +277,19 @@
     act[...] = (
         jax.nn.silu((gate[...] + a) * scale) * ((up[...] + b) * scale) * weight
     ).astype(BF16)
+    for copy in copies:
+        copy.wait()
 
 
 DOWN_STEPS = 7
 
 
-def down_first_kernel(idx, act, w_down, out):
-    block = out.shape[1] // DOWN_STEPS
+def down_kernel(idx, act, act_other, w_down, w_down_other, out):
+    block = out.shape[2] // DOWN_STEPS
     for i in range(DOWN_STEPS):
-        start = pl.multiple_of(((1 - idx[0]) * DOWN_STEPS + i) * block, 128)
-        out[:, i * block : (i + 1) * block] = jnp.dot(
-            act[...], w_down[:, pl.ds(start, block)], preferred_element_type=F32
-        ).astype(BF16)
-
-
-def down_second_kernel(idx, act, w_down, arrived, out):
-    block = arrived.shape[1] // DOWN_STEPS
-    for i in range(DOWN_STEPS):
-        start = pl.multiple_of((idx[0] * DOWN_STEPS + i) * block, 128)
-        total = jnp.dot(act[...], w_down[:, pl.ds(start, block)], preferred_element_type=F32)
-        total += arrived[:, i * block : (i + 1) * block].astype(F32)
+        columns = pl.ds(i * block, block)
+        total = jnp.dot(act[...], w_down[:, columns], preferred_element_type=F32)
+        total += jnp.dot(act_other[...], w_down_other[:, columns], preferred_element_type=F32)
         out[:, :, i * block : (i + 1) * block] = total.reshape(out.shape[:2] + (block,)).astype(BF16)
 
 
@@ -285,21 +322,30 @@
     half_heads = heads // 2
     shape = jax.ShapeDtypeStruct
 
-    idx = jnp.concatenate([jnp.stack([s, r]).astype(jnp.int32), lengths, blocks.reshape(-1)])
+    place = ((x * n_req + r) * 2 + s) * own_rows
+    idx = jnp.concatenate(
+        [jnp.stack([s, r]).astype(jnp.int32), lengths, blocks.reshape(-1), place[None]]
+    )
     half_rows = drafts * half_heads
-    sent, kept, kept_stats = call(
+    sent, kept, kept_stats, value_half = call(
         attend_kernel,
         "attend",
         (
             shape((half_rows, DL + 128), BF16),
             shape((half_rows, DL), F32),
             shape((half_rows, 256), F32),
-        ),
-        idx,
-        queries[0],
-        latent_cache[0],
+            shape((half_heads,) + value_up.shape[1:], BF16),
+        ),
+        idx,
+        outside=(queries[0], latent_cache[0], value_up),
+        scratch=(
+            pltpu.VMEM(queries.shape[1:], BF16),
+            pltpu.VMEM((blocks.shape[2] * BLOCK, qk_width), BF16),
+            pltpu.SemaphoreType.DMA((4,)),
+        ),
     )
     arrived = swap(sent)
+    w_down_other = swap(w_down[0])
 
     named = jnp.sum(
         (expert_ids[:, :, None] == jnp.arange(experts, dtype=jnp.int32)).astype(F32), 1
@@ -319,12 +365,13 @@
         kept,
         kept_stats,
         arrived,
-        value_up,
+        value_half,
         side_rows,
     )
     gathered = lax.all_to_all(fanned, "req", split_axis=0, concat_axis=0, tiled=True)
     gathered_other = swap(gathered)
     out_proj_t = out_proj.T
+    w_gate, w_up, w_down = w_gate[0], w_up[0], w_down[0]
     started = call(
         project_own_kernel, "project_own", shape((tokens, width), F32), idx, gathered, out_proj_t
     )
@@ -343,8 +390,8 @@
     )
     gains = norm_gain.reshape(n_req * 2, 1, width)
     router_t = router.T.reshape(experts, n_req * 2, width).transpose(1, 0, 2)
-    terms, resid, idx, gains, router_t = lax.optimization_barrier(
-        (terms, resid, idx, gains, router_t)
+    terms, resid, idx, gains, router_t, w_down_other = lax.optimization_barrier(
+        (terms, resid, idx, gains, router_t, w_down_other)
     )
     terms = lax.all_to_all(terms, "exp", split_axis=0, concat_axis=0, tiled=True)
     attended = jnp.sum(terms.astype(F32), 0).astype(BF16)
@@ -354,9 +401,8 @@
     own = lax.all_to_all(fanned, ("req", "exp"), split_axis=0, concat_axis=0, tiled=True)
     own = own.reshape(n_req, tokens, padded)
     other = swap(own)
-    w_gate, w_up, w_down = w_gate[0], w_up[0], w_down[0]
     hidden_units = w_gate.shape[1]
-    started = call(
+    *started, w_up = call(
         gate_up_own_kernel,
         "gate_up_own",
         (
@@ -364,18 +410,25 @@
             shape((tokens, hidden_units), F32),
             shape((tokens, experts), F32),
             shape((tokens, 128), F32),
+            shape(w_up.shape, BF16),
         ),
         idx,
         own,
         gains,
         w_gate,
-        w_up,
         router_t,
-    )
-    act = call(
+        outside=(w_up,),
+        scratch=(pltpu.SemaphoreType.DMA((UP_COPIES,)),),
+    )
+    half = model_width // 2
+    act, w_down, w_down_other = call(
         gate_up_both_kernel,
         "gate_up_both",
-        shape((tokens, hidden_units), BF16),
+        (
+            shape((tokens, hidden_units), BF16),
+            shape((hidden_units, half), BF16),
+            shape((hidden_units, half), BF16),
+        ),
         idx,
         *started,
         own,
@@ -384,19 +437,21 @@
         w_gate,
         w_up,
         router_t,
-    )
-    half = model_width // 2
-    first = call(down_first_kernel, "down_first", shape((tokens, half), BF16), idx, act, w_down)
+        outside=(w_down, w_down_other),
+        scratch=(pltpu.SemaphoreType.DMA((2,)),),
+    )
     pieces = call(
-        down_second_kernel,
-        "down_second",
+        down_kernel,
+        "down",
         shape((tokens // 4, 4, half), BF16),
         idx,
         act,
+        swap(act),
         w_down,
-        swap(first),
-    )
-    place = ((x * n_req + r) * 2 + s) * own_rows
+        w_down_other,
+    )
+    pieces, own, other, idx = lax.optimization_barrier((pieces, own, other, idx))
+    s, place = idx[0], idx[-1]
     hid_own = lax.dynamic_slice_in_dim(own, place, own_rows, 1)[:, :, :width]
     hid_other = lax.dynamic_slice_in_dim(other, place, own_rows, 1)[:, :, :width]
     hid = jnp.where(s == 0, jnp.stack([hid_own, hid_other], 1), jnp.stack([hid_other, hid_own], 1))

time: 141 us -> 136 us (0.965)
  waiting for transfers between devices: 30.1 us -> 22.8 us
  local copies, waits for them, and re-layouts: 10.7 us -> 4.95 us
  between operations: 0.97 us -> 6.55 us
  Pallas kernels: 13.7 us -> 18.4 us
  other arithmetic: 4.57 us -> 3.16 us
    unnamed x22 -> x16, local copies, waits for them, and re-layouts: 7.64 us -> 1.28 us
    all_to_all x1, waiting for transfers between devices: 24.9 us -> 18.6 us  [per_device(): lax.all_to_all(pieces, ('exp', 'req'), split_axis=0, concat_axis=0, tiled...]
    pallas_call x8 -> x7, Pallas kernels: 13.7 us -> 18.4 us  [call(): pl.pallas_call(kernel, out_shape=out_shape, in_specs=[pl.BlockSpec(memory...]
    ppermute x5 -> x6, waiting for transfers between devices: 5.19 us -> 4.13 us  [swap(): return lax.ppermute(x, 'seq', SWAP)]
    ppermute x5 -> x6, starting transfers between devices: 8.47 us -> 8.79 us  [swap(): return lax.ppermute(x, 'seq', SWAP)]
  transfers between devices with their start and end apart: 6 -> 7, of which waited for: 4 -> 5; matrix products, arithmetic and copies ran while one was open for 3% -> 3% of each run, Pallas kernels for 2% -> 9%
where the time goes in v3:
time: 136 us
  blocking collectives  65.7 us (48%)
  waiting for transfers between devices  22.8 us (17%)
  Pallas kernels  18.4 us (14%)
  starting transfers between devices  14.3 us (11%)
  between operations  6.55 us (5%)
  local copies, waits for them, and re-layouts  4.95 us (4%)
  other arithmetic  3.16 us (2%)
    all_to_all x1, blocking collectives, per_device(): lax.all_to_all(fanned, ('req', 'exp'), split_axis=0, concat_axis=0, tiled...  32.1 us
    all_to_all x1, blocking collectives, per_device(): lax.all_to_all(fanned, 'req', split_axis=0, concat_axis=0, tiled=True)  24.9 us
    all_to_all x1, waiting for transfers between devices, per_device(): lax.all_to_all(pieces, ('exp', 'req'), split_axis=0, concat_axis=0, tiled...  18.6 us
    pallas_call x7, Pallas kernels, call(): pl.pallas_call(kernel, out_shape=out_shape, in_specs=[pl.BlockSpec(memory...  18.4 us
    ppermute x6, starting transfers between devices, swap(): return lax.ppermute(x, 'seq', SWAP)  8.79 us
    all_to_all x1, blocking collectives, per_device(): lax.all_to_all(terms, 'exp', split_axis=0, concat_axis=0, tiled=True)  8.64 us
    all_to_all x1, starting transfers between devices, per_device(): lax.all_to_all(pieces, ('exp', 'req'), split_axis=0, concat_axis=0, tiled...  5.53 us
    ppermute x6, waiting for transfers between devices, swap(): return lax.ppermute(x, 'seq', SWAP)  4.13 us
  transfers between devices with their start and end apart: 7, of which 5 were waited for; matrix products, arithmetic and copies ran while one was open for 3% of the time, Pallas kernels for 9%

profile of v3, /device:TPU:1, one launch (start us, length us, event | category | flops | bytes accessed | tf_op | source)
XLA Modules:
  0.0 135.8 jit_solution(9438691323714112814)
XLA Ops:
  0.0 1.4 %collective-permute-start.2 = (bf16[256,7168]{1,0:T(8,128)(2,1)}, bf16[256,7168]{1,0:T(8,128)(2,1)}, u32[]{:S(2)}, u32[]{:S(2)}) collective-permute-start(bf16[256,7168]{1,0:T(8,128)(2,1)} %bitcast.40), channel_id=1, source_target_pairs={{0,4},{4,0},{1,5},{5,1},{2,6},{6,2},{3,7},{7,3},{8,12},{12,8},{9,1... | collective-permute-start | bytes 11010056 | tf_op jit(solution)/shard_map/ppermute | solution.py:18
  2.0 0.7 concatenate.12.idx
  2.8 3.4 %attend.1 = (bf16[256,640]{1,0:T(8,128)(2,1)}, f32[256,512]{1,0:T(8,128)S(1)}, f32[256,256]{1,0:T(8,128)S(1)}, bf16[16,512,128]{2,1,0:T(8,128)(2,1)S(1)}) custom-call(s32[6]{0:T(128)S(1)} %concatenate.12.idx, bf16[16,32,576]{2,1,0:T(8,128)(2,1)} %bitcast.42, bf16[192,576]{1,0:T(8,128)(2,1)} %bitcast.43, bf16[32,512,128]{2,1,0:T(8,128)(2,1)} %value_up.1), custom_call_target="tpu_custom_call" | custom-call | tf_op jit(solution)/shard_map/attend/pallas_call | solution.py:27
  6.7 1.4 %collective-permute-done.arrived = bf16[256,640]{1,0:T(8,128)(2,1)S(1)} collective-permute-done((bf16[256,640]{1,0:T(8,128)(2,1)}, bf16[256,640]{1,0:T(8,128)(2,1)S(1)}, u32[]{:S(2)}, u32[]{:S(2)}) %collective-permute-start) | collective-permute-done | bytes 327712 | tf_op jit(solution)/shard_map/ppermute | solution.py:18
  8.1 1.3 values.1
  9.5 24.9 %all_to_all.20.gathered = bf16[16,17,16,128]{3,2,1,0:T(8,128)(2,1)S(1)} all-to-all(bf16[16,17,16,128]{3,2,1,0:T(8,128)(2,1)S(1)} %values.1), channel_id=1, replica_groups=mesh['req'=16,'seq'=2,'exp'=4] {'req'}, dimensions={0} | all-to-all | bytes 2228224 | tf_op jit(solution)/shard_map/all_to_all | solution.py:371
  34.4 1.7 %collective-permute-start.1 = (bf16[16,17,16,128]{3,2,1,0:T(8,128)(2,1)S(1)}, bf16[16,17,16,128]{3,2,1,0:T(8,128)(2,1)}, u32[]{:S(2)}, u32[]{:S(2)}) collective-permute-start(bf16[16,17,16,128]{3,2,1,0:T(8,128)(2,1)S(1)} %all_to_all.20.gathered), channel_id=1, source_target_pairs={{0,4},{4,0},{1,5},{5,1},{2,6},{6,2},{3,7},{7,3},{8,12},{12,8},{9,1... | collective-permute-start | bytes 3342344 | tf_op jit(solution)/shard_map/ppermute | solution.py:18
  36.8 1.0 project_own.1.started
  37.8 0.8 collective-permute-done.1.gathered_other
  38.6 2.1 %project_both.1 = (bf16[4,64,256]{2,1,0:T(8,128)(2,1)S(1)}, bf16[64,256]{1,0:T(8,128)(2,1)S(1)}) custom-call(s32[6]{0:T(128)S(1)} %concatenate.12.idx, f32[256,224]{1,0:T(8,128)S(1)} %project_own.1.started, bf16[16,17,16,128]{3,2,1,0:T(8,128)(2,1)S(1)} %all_to_all.20.gathered, bf16[16,17,16,128]{3,2,1,0:T(8,128)(2,1)} %collective-permute-done.1.gathered_other, ...), custom_call_target="tpu_custom_call" | custom-call | tf_op jit(solution)/shard_map/project_both/pallas_call | solution.py:27
  40.7 8.6 %all_to_all.21 = bf16[4,64,256]{2,1,0:T(8,128)(2,1)S(1)} all-to-all(bf16[4,64,256]{2,1,0:T(8,128)(2,1)S(1)} %get-tuple-element.38), channel_id=1, replica_groups=mesh['req'=16,'seq'=2,'exp'=4] {'exp'}, dimensions={0} | all-to-all | bytes 262144 | tf_op jit(solution)/shard_map/all_to_all | solution.py:396
  49.6 32.1 %all_to_all.22 = bf16[64,64,256]{2,1,0:T(8,128)(2,1)S(1)} all-to-all(bf16[64,64,256]{2,1,0:T(8,128)(2,1)S(1)} %broadcast_in_dim.11), channel_id=1, replica_groups=mesh['req'=16,'seq'=2,'exp'=4] {'req','exp'}, dimensions={0} | all-to-all | bytes 4194304 | tf_op jit(solution)/shard_map/all_to_all | solution.py:401
  81.7 3.8 %collective-permute-start.3 = (bf16[16,256,256]{2,1,0:T(8,128)(2,1)S(1)}, bf16[16,256,256]{2,1,0:T(8,128)(2,1)S(1)}, u32[]{:S(2)}, u32[]{:S(2)}) collective-permute-start(bf16[16,256,256]{2,1,0:T(8,128)(2,1)S(1)} %bitcast.29), channel_id=1, source_target_pairs={{0,4},{4,0},{1,5},{5,1},{2,6},{6,2},{3,7},{7,3},{8,12},{12,8},{9,1... | collective-permute-start | bytes 6291464 | tf_op jit(solution)/shard_map/ppermute | solution.py:18
  85.5 4.4 %gate_up_own.1 = (f32[256,256]{1,0:T(8,128)S(1)}, f32[256,256]{1,0:T(8,128)S(1)}, f32[256,16]{1,0:T(8,128)S(1)}, f32[256,128]{1,0:T(8,128)S(1)}, bf16[7168,256]{1,0:T(8,128)(2,1)S(1)}) custom-call(s32[6]{0:T(128)S(1)} %concatenate.12.idx, bf16[7168,256]{1,0:T(8,128)(2,1)} %bitcast.39, bf16[16,256,256]{2,1,0:T(8,128)(2,1)S(1)} %bitcast.30, ...), custom_call_target="tpu_custom_call" | custom-call | tf_op jit(solution)/shard_map/gate_up_own/pallas_call | solution.py:27
  89.9 4.5 %gate_up_both.1 = (bf16[256,256]{1,0:T(8,128)(2,1)S(1)}, bf16[256,3584]{1,0:T(8,128)(2,1)S(1)}, bf16[256,3584]{1,0:T(8,128)(2,1)S(1)}) custom-call(s32[6]{0:T(128)S(1)} %concatenate.12.idx, bf16[256,7168]{1,0:T(8,128)(2,1)} %bitcast.41, bf16[256,7168]{1,0:T(8,128)(2,1)} %collective-permute-done.2.w_down_other_there, f32[256,256]{1,0:T(8,128)S(1)} %get-tuple-element.41.gate, ...), custom_call_target="tpu_custom_call" | custom-call | tf_op jit(solution)/shard_map/gate_up_both/pallas_call | solution.py:27
  94.6 1.3 collective-permute-done.4.act_other
  95.9 1.7 %down.1 = bf16[64,4,3584]{2,1,0:T(4,128)(2,1)S(1)} custom-call(s32[6]{0:T(128)S(1)} %concatenate.12.idx, bf16[256,256]{1,0:T(8,128)(2,1)S(1)} %get-tuple-element.46.act, bf16[256,256]{1,0:T(8,128)(2,1)S(1)} %collective-permute-done.4.act_other, bf16[256,3584]{1,0:T(8,128)(2,1)S(1)} %get-tuple-element.47.w_down, ...), custom_call_target="tpu_custom_call" | custom-call | tf_op jit(solution)/shard_map/down/pallas_call | solution.py:27
  97.6 1.2 copy-done.2
  98.9 5.5 %all-to-all-start.3 = ((bf16[64,4,3584]{2,1,0:T(4,128)(2,1)}), bf16[64,4,3584]{2,1,0:T(4,128)(2,1)}, u32[]{:S(2)}, u32[]{:S(2)}) async-start(bf16[64,4,3584]{2,1,0:T(4,128)(2,1)} %copy-done.2), calls=%async_computation.3 | async-start | bytes 3670016 | tf_op jit(solution)/shard_map/all_to_all | solution.py:459
  110.6 1.0 dynamic-slice_bitcast_fusion.2
  111.6 18.6 %all-to-all-done.3 = bf16[64,4,3584]{2,1,0:T(4,128)(2,1)} async-done(((bf16[64,4,3584]{2,1,0:T(4,128)(2,1)}), bf16[64,4,3584]{2,1,0:T(4,128)(2,1)}, u32[]{:S(2)}, u32[]{:S(2)}) %all-to-all-start.3) | async-done | bytes 1835040 | tf_op jit(solution)/shard_map/all_to_all | solution.py:459
  130.2 2.3 %convert_reduce_fusion = f32[4,3584]{1,0:T(4,128)S(1)} fusion(bf16[64,4,3584]{2,1,0:T(4,128)(2,1)} %all-to-all-done.3), kind=kLoop, calls=%fused_computation | loop fusion | flops 1820672 | bytes 1892352 | tf_op jit(solution)/shard_map/reduce_sum | solution.py:460
  132.5 1.8 %collective-permute-start.5 = (f32[2,3584]{1,0:T(2,128)S(1)}, f32[2,3584]{1,0:T(2,128)S(1)}, u32[]{:S(2)}, u32[]{:S(2)}) collective-permute-start(f32[2,3584]{1,0:T(2,128)S(1)} %get-tuple-element.54), channel_id=1, source_target_pairs={{0,4},{4,0},{1,5},{5,1},{2,6},{6,2},{3,7},{7,3},{8,12},{12,8},{9,1... | collective-permute-start | bytes 86024 | tf_op jit(solution)/shard_map/ppermute | solution.py:18
  135.2 0.6 fusion.1
  (42 shorter events, 3.0 us)
Async XLA Ops:
  0.0 40.7 %collective-permute-start.2 = (bf16[256,7168]{1,0:T(8,128)(2,1)}, bf16[256,7168]{1,0:T(8,128)(2,1)}, u32[]{:S(2)}, u32[]{:S(2)}) collective-permute-start(bf16[256,7168]{1,0:T(8,128)(2,1)} %bitcast.40), channel_id=1, source_target_pairs={{0,4},{4,0},{1,5},{5,1},{2,6},{6,2},{3,7},{7,3},{8,12},{12,8},{9,1... | collective-permute-start | bytes 11010056 | tf_op jit(solution)/shard_map/ppermute | solution.py:18
  2.8 3.5 %copy-start.5 = (bf16[2,7168]{1,0:T(2,128)(2,1)S(1)}, bf16[2,7168]{1,0:T(2,128)(2,1)}, u32[]{:S(2)}) copy-start(bf16[2,7168]{1,0:T(2,128)(2,1)} %param.13) | copy-start | bytes 86020
  2.8 3.7 %copy-start.7 = (s32[2,8]{1,0:T(2,128)S(1)}, s32[2,8]{1,0:T(2,128)}, u32[]{:S(2)}) copy-start(s32[2,8]{1,0:T(2,128)} %param.22) | copy-start | bytes 196
  6.2 1.9 %collective-permute-start = (bf16[256,640]{1,0:T(8,128)(2,1)}, bf16[256,640]{1,0:T(8,128)(2,1)S(1)}, u32[]{:S(2)}, u32[]{:S(2)}) collective-permute-start(bf16[256,640]{1,0:T(8,128)(2,1)} %get-tuple-element.31), channel_id=1, source_target_pairs={{0,4},{4,0},{1,5},{5,1},{2,6},{6,2},{3,7},{7,3},{8,12},{12,8},{9,1... | collective-permute-start | bytes 983048 | tf_op jit(solution)/shard_map/ppermute | solution.py:18
  9.5 26.6 %copy-start.6 = (bf16[7168]{0:T(1024)(128)(2,1)S(1)}, bf16[7168]{0:T(1024)(128)(2,1)}, u32[]{:S(2)}) copy-start(bf16[7168]{0:T(1024)(128)(2,1)} %param.20) | copy-start | bytes 43012
  9.5 26.7 %copy-start.4 = (bf16[7168,16]{0,1:T(8,128)(2,1)S(1)}, bf16[7168,16]{0,1:T(8,128)(2,1)}, u32[]{:S(2)}) copy-start(bf16[7168,16]{0,1:T(8,128)(2,1)} %param.21) | copy-start | bytes 688132
  9.5 27.3 %copy-start.1 = (bf16[4096,224]{0,1:T(8,128)(2,1)S(1)}, bf16[4096,224]{0,1:T(8,128)(2,1)}, u32[]{:S(2)}) copy-start(bf16[4096,224]{0,1:T(8,128)(2,1)} %param.19) | copy-start | bytes 5505028
  34.4 4.2 %collective-permute-start.1 = (bf16[16,17,16,128]{3,2,1,0:T(8,128)(2,1)S(1)}, bf16[16,17,16,128]{3,2,1,0:T(8,128)(2,1)}, u32[]{:S(2)}, u32[]{:S(2)}) collective-permute-start(bf16[16,17,16,128]{3,2,1,0:T(8,128)(2,1)S(1)} %all_to_all.20.gathered), channel_id=1, source_target_pairs={{0,4},{4,0},{1,5},{5,1},{2,6},{6,2},{3,7},{7,3},{8,12},{12,8},{9,1... | collective-permute-start | bytes 3342344 | tf_op jit(solution)/shard_map/ppermute | solution.py:18
  49.6 35.9 %copy-start = (bf16[1,7168,256]{2,1,0:T(8,128)(2,1)S(1)}, bf16[1,7168,256]{2,1,0:T(8,128)(2,1)}, u32[]{:S(2)}) copy-start(bf16[1,7168,256]{2,1,0:T(8,128)(2,1)} %param.23) | copy-start | bytes 11010052
  81.7 8.2 %collective-permute-start.3 = (bf16[16,256,256]{2,1,0:T(8,128)(2,1)S(1)}, bf16[16,256,256]{2,1,0:T(8,128)(2,1)S(1)}, u32[]{:S(2)}, u32[]{:S(2)}) collective-permute-start(bf16[16,256,256]{2,1,0:T(8,128)(2,1)S(1)} %bitcast.29), channel_id=1, source_target_pairs={{0,4},{4,0},{1,5},{5,1},{2,6},{6,2},{3,7},{7,3},{8,12},{12,8},{9,1... | collective-permute-start | bytes 6291464 | tf_op jit(solution)/shard_map/ppermute | solution.py:18
  89.9 4.6 %copy-start.3 = (bf16[16,256,256]{2,1,0:T(8,128)(2,1)}, bf16[16,256,256]{2,1,0:T(8,128)(2,1)S(1)}, u32[]{:S(2)}) copy-start(bf16[16,256,256]{2,1,0:T(8,128)(2,1)S(1)} %collective-permute-done.3.other) | copy-start | bytes 6291460
  94.5 1.4 %collective-permute-start.4 = (bf16[256,256]{1,0:T(8,128)(2,1)S(1)}, bf16[256,256]{1,0:T(8,128)(2,1)S(1)}, u32[]{:S(2)}, u32[]{:S(2)}) collective-permute-start(bf16[256,256]{1,0:T(8,128)(2,1)S(1)} %get-tuple-element.46.act), channel_id=1, source_target_pairs={{0,4},{4,0},{1,5},{5,1},{2,6},{6,2},{3,7},{7,3},{8,12},{12,8},{9,1... | collective-permute-start | bytes 393224 | tf_op jit(solution)/shard_map/ppermute | solution.py:18
  97.6 1.2 copy-start.2
  98.9 31.3 %all-to-all-start.3 = ((bf16[64,4,3584]{2,1,0:T(4,128)(2,1)}), bf16[64,4,3584]{2,1,0:T(4,128)(2,1)}, u32[]{:S(2)}, u32[]{:S(2)}) async-start(bf16[64,4,3584]{2,1,0:T(4,128)(2,1)} %copy-done.2), calls=%async_computation.3 | async-start | bytes 3670016 | tf_op jit(solution)/shard_map/all_to_all | solution.py:459
  132.5 2.7 %collective-permute-start.5 = (f32[2,3584]{1,0:T(2,128)S(1)}, f32[2,3584]{1,0:T(2,128)S(1)}, u32[]{:S(2)}, u32[]{:S(2)}) collective-permute-start(f32[2,3584]{1,0:T(2,128)S(1)} %get-tuple-element.54), channel_id=1, source_target_pairs={{0,4},{4,0},{1,5},{5,1},{2,6},{6,2},{3,7},{7,3},{8,12},{12,8},{9,1... | collective-permute-start | bytes 86024 | tf_op jit(solution)/shard_map/ppermute | solution.py:18

commit v4 on v3

--- a/solution.py
+++ b/solution.py
@@ -69,12 +69,19 @@
         ),
         pltpu.make_async_copy(queries, query_rows, sems.at[2]),
     ]
-    value_copy = pltpu.make_async_copy(
-        value_up.at[pl.ds(side * (heads // 2), heads // 2)], value_half, sems.at[3]
-    )
-    for copy in copies:
-        copy.start()
-    value_copy.start()
+    quarter = heads // 8
+    value_copies = [
+        pltpu.make_async_copy(
+            value_up.at[pl.ds(side * (heads // 2) + i * quarter, quarter)],
+            value_half.at[pl.ds(i * quarter, quarter)],
+            sems.at[3 + i],
+        )
+        for i in range(4)
+    ]
+    for place, copy in enumerate(copies):
+        copy.start(priority=place // 2)
+    for place, copy in enumerate(value_copies):
+        copy.start(priority=place % 2)
     for copy in copies:
         copy.wait()
     keys = key_rows[...]
@@ -113,10 +120,11 @@
     for place, part in enumerate(top_parts + sum_parts):
         packed = jnp.where(lane == place, part.astype(F32), packed)
     sent[:, DL:] = packed.astype(BF16)
-    value_copy.wait()
-
-
-def values_kernel(idx, kept, kept_stats, arrived, value_up, side_rows, fanned):
+    for copy in value_copies:
+        copy.wait()
+
+
+def values_kernel(idx, kept, kept_stats, arrived, value_up, side_rows, gains, router_t, fanned):
     rows = kept.shape[0]
     dests, slabs, drafts, _ = fanned.shape
     half = slabs - 1
@@ -164,46 +172,60 @@
     return total
 
 
-def project_own_kernel(idx, gathered, out_proj_t, out):
-    out[...] = project_terms(gathered, out_proj_t, idx[0])
-
-
-def project_both_kernel(idx, started, gathered, gathered_other, out_proj_t, terms, residual):
+def project_kernel(idx, other_there, gathered, own_t, out, other_t, sem):
     reqs, slabs, drafts, lanes = gathered.shape
-    exps, _, padded = terms.shape
-    width = started.shape[1]
-    side = idx[0]
-    total = (started[...] + project_terms(gathered_other, out_proj_t, 1 - side)).astype(BF16)
+    _, exps, _, padded = out.shape
+    width = own_t.shape[0]
+    side, exp = idx[0], idx[6]
     tokens = reqs * drafts
     own_rows = drafts // (2 * exps)
 
+    def parts(i):
+        exp, req = i // (tokens // exps), i // (2 * own_rows) % reqs
+        return exp, req, i // own_rows % 2, i % own_rows
+
     def source(i):
-        exp, req = i // (tokens // exps), i // (2 * own_rows) % reqs
-        seq, row = i // own_rows % 2, i % own_rows
+        exp, req, seq, row = parts(i)
         return ((req * 2 + seq) * exps + exp) * own_rows + row
 
-    total = jnp.dot(one_hot((tokens, tokens), source), total, preferred_element_type=F32)
-    total = jnp.concatenate([total, jnp.zeros((tokens, padded - width), F32)], -1)
-    terms[...] = total.astype(BF16).reshape(terms.shape)
+    depth = other_t.shape[1]
+    copy = pltpu.make_async_copy(
+        other_there.at[:, pl.ds(pl.multiple_of(side * depth, depth), depth)], other_t, sem
+    )
+    copy.start()
+    order = one_hot((tokens, tokens), source)
+    beside = gathered[:, slabs - 1].reshape(tokens, lanes)
     tiles = padded // lanes
-    for tile in range(tiles):
-        picked = jnp.zeros((tokens // exps, lanes), F32)
-        for rows, from_side in ((gathered, side), (gathered_other, 1 - side)):
+    for columns_t, column_side in ((own_t, side), (other_t, 1 - side)):
+        if columns_t is other_t:
+            copy.wait()
+        terms = project_terms(gathered, columns_t, side if columns_t is own_t else 0).astype(BF16)
+        terms = jnp.dot(order, terms, preferred_element_type=F32)
+        terms = jnp.concatenate([terms, jnp.zeros((tokens, padded - width), F32)], -1)
+        residual = []
+        for tile in range(tiles):
 
             def residual_source(i):
-                req, seq, row = i // (2 * own_rows), i // own_rows % 2, i % own_rows
-                place = req * drafts + (row * 2 + side) * tiles + tile
-                return jnp.where(seq == from_side, place, -1)
-
-            picked += jnp.dot(
-                one_hot((tokens // exps, tokens), residual_source),
-                rows[:, slabs - 1].reshape(tokens, lanes),
-                preferred_element_type=F32,
+                token_exp, req, seq, row = parts(i)
+                place = req * drafts + (row * 2 + column_side) * tiles + tile
+                return jnp.where((token_exp == exp) & (seq == side), place, -1)
+
+            residual.append(
+                jnp.dot(
+                    one_hot((tokens, tokens), residual_source), beside, preferred_element_type=F32
+                )
             )
-        residual[:, tile * lanes : (tile + 1) * lanes] = picked.astype(BF16)
-
-
-def expert_terms(rows, gains, w_gate, w_up, router_t, side, copies=()):
+        terms = (terms + jnp.concatenate(residual, -1)).astype(BF16)
+        out[column_side] = terms.reshape(out.shape[1:])
+
+
+def hidden_kernel(idx, terms, fanned):
+    hidden = jnp.sum(terms[...].astype(F32), 0).astype(BF16)
+    for dest in range(fanned.shape[0]):
+        fanned[dest] = hidden
+
+
+def expert_terms(rows, gains, w_gate, w_up, router_t, side):
     steps, tokens, _ = rows.shape
     width = gains.shape[-1]
 
@@ -221,8 +243,6 @@
 
     state = None
     for i in range(steps):
-        if copies and i % (steps // len(copies)) == 0:
-            copies[i * len(copies) // steps].wait()
         if state is None:
             state = (
                 jnp.zeros((tokens, w_gate.shape[1]), F32),
@@ -235,35 +255,31 @@
     return gate, up, logits, jnp.sum(squares, -1, keepdims=True)
 
 
-UP_COPIES = 4
-
-
-def gate_up_own_kernel(
-    idx, w_up_there, own, gains, w_gate, router_t, gate, up, logits, squares, w_up, sems
-):
-    rows = w_up.shape[0] // UP_COPIES
-    copies = []
-    for i in range(UP_COPIES):
-        part = pl.ds(i * rows, rows)
-        copies.append(pltpu.make_async_copy(w_up_there.at[part], w_up.at[part], sems.at[i]))
-    for copy in copies:
-        copy.start()
-    a, b, c, d = expert_terms(own, gains, w_gate, w_up, router_t, idx[0], copies)
+def gate_up_own_kernel(idx, own, gains, w_gate, w_up, router_t, gate, up, logits, squares):
+    a, b, c, d = expert_terms(own, gains, w_gate, w_up, router_t, idx[0])
     gate[...], up[...], logits[...] = a, b, c
     squares[...] = jnp.broadcast_to(d, squares.shape)
 
 
 def gate_up_both_kernel(
-    idx, w_down_there, w_down_other_there, gate, up, logits, squares, own, other, gains, w_gate,
-    w_up, router_t, act, w_down, w_down_other, sems,
+    idx, w_down_there, gate, up, logits, squares, own, other, gains, w_gate, w_up, router_t,
+    act, rows_here, w_down_other, sems,
 ):
-    half = pl.ds(pl.multiple_of(idx[0] * w_down.shape[1], 128), w_down.shape[1])
-    copies = [
-        pltpu.make_async_copy(w_down_there.at[:, half], w_down, sems.at[0]),
-        pltpu.make_async_copy(w_down_other_there.at[:, half], w_down_other, sems.at[1]),
-    ]
-    for copy in copies:
-        copy.start()
+    hidden_units, half = w_down_other.shape
+    columns = pl.ds(pl.multiple_of(idx[0] * half, 128), half)
+    copies = []
+    for i in range(2):
+        part = pl.ds(i * (hidden_units // 2), hidden_units // 2)
+        copies.append(
+            pltpu.make_async_copy(
+                w_down_there.at[part, columns], w_down_other.at[part], sems.at[i]
+            )
+        )
+        copies[i].start(priority=i)
+    pick = one_hot((rows_here.shape[1], own.shape[1]), lambda i: jnp.where(i < idx[7], idx[5] + i, -1))
+    for rows, side in ((own, idx[0]), (other, 1 - idx[0])):
+        for i in range(own.shape[0]):
+            rows_here[i * 2 + side] = jnp.dot(pick, rows[i], preferred_element_type=F32)
     width = gains.shape[-1]
     experts = logits.shape[1]
     columns = gains.shape[0] * width
@@ -285,12 +301,37 @@
 
 
 def down_kernel(idx, act, act_other, w_down, w_down_other, out):
-    block = out.shape[2] // DOWN_STEPS
+    half = out.shape[2]
+    block = half // DOWN_STEPS
     for i in range(DOWN_STEPS):
-        columns = pl.ds(i * block, block)
+        columns = pl.ds(pl.multiple_of(idx[0] * half + i * block, 128), block)
         total = jnp.dot(act[...], w_down[:, columns], preferred_element_type=F32)
-        total += jnp.dot(act_other[...], w_down_other[:, columns], preferred_element_type=F32)
+        total += jnp.dot(
+            act_other[...], w_down_other[:, i * block : (i + 1) * block], preferred_element_type=F32
+        )
         out[:, :, i * block : (i + 1) * block] = total.reshape(out.shape[:2] + (block,)).astype(BF16)
+
+
+def routed_kernel(idx, pieces, mine, theirs):
+    rows = mine.shape[0]
+    total = jnp.sum(pieces[...].astype(F32), 0)
+    low, high = total[:rows], total[rows:]
+    mine[...] = jnp.where(idx[0] == 0, low, high)
+    theirs[...] = jnp.where(idx[0] == 0, high, low)
+
+
+def finish_kernel(idx, mine, theirs, rows_here, out):
+    blocks, rows, half = rows_here.shape[0], mine.shape[0], mine.shape[1]
+    width = 2 * half // blocks
+    for side, first, second in ((0, mine, theirs), (1, theirs, mine)):
+
+        @pl.when(idx[0] == side)
+        def _():
+            for block in range(blocks):
+                start = block * width
+                source, offset = (first, start) if start < half else (second, start - half)
+                total = rows_here[block, :rows, :width] + source[:, offset : offset + width]
+                out[:, start : start + width] = total.astype(BF16)
 
 
 def per_device(
@@ -324,7 +365,12 @@
 
     place = ((x * n_req + r) * 2 + s) * own_rows
     idx = jnp.concatenate(
-        [jnp.stack([s, r]).astype(jnp.int32), lengths, blocks.reshape(-1), place[None]]
+        [
+            jnp.stack([s, r]).astype(jnp.int32),
+            lengths,
+            blocks.reshape(-1),
+            jnp.stack([place, x, jnp.int32(own_rows)]).astype(jnp.int32),
+        ]
     )
     half_rows = drafts * half_heads
     sent, kept, kept_stats, value_half = call(
@@ -341,12 +387,17 @@
         scratch=(
             pltpu.VMEM(queries.shape[1:], BF16),
             pltpu.VMEM((blocks.shape[2] * BLOCK, qk_width), BF16),
-            pltpu.SemaphoreType.DMA((4,)),
+            pltpu.SemaphoreType.DMA((7,)),
         ),
     )
     arrived = swap(sent)
-    w_down_other = swap(w_down[0])
-
+    w_gate, w_up, w_down = w_gate[0], w_up[0], w_down[0]
+    out_proj_t = out_proj.T
+    other_t = swap(out_proj_t)
+    w_down_other = swap(w_down)
+
+    gains = norm_gain.reshape(n_req * 2, 1, width)
+    router_t = router.T.reshape(experts, n_req * 2, width).transpose(1, 0, 2)
     named = jnp.sum(
         (expert_ids[:, :, None] == jnp.arange(experts, dtype=jnp.int32)).astype(F32), 1
     ).astype(BF16)
@@ -367,42 +418,40 @@
         arrived,
         value_half,
         side_rows,
+        gains,
+        router_t,
     )
     gathered = lax.all_to_all(fanned, "req", split_axis=0, concat_axis=0, tiled=True)
-    gathered_other = swap(gathered)
-    out_proj_t = out_proj.T
-    w_gate, w_up, w_down = w_gate[0], w_up[0], w_down[0]
-    started = call(
-        project_own_kernel, "project_own", shape((tokens, width), F32), idx, gathered, out_proj_t
-    )
-    terms, resid = call(
-        project_both_kernel,
-        "project_both",
-        (
-            shape((n_exp, tokens // n_exp, padded), BF16),
-            shape((tokens // n_exp, padded), BF16),
-        ),
-        idx,
-        started,
+    terms = call(
+        project_kernel,
+        "project",
+        shape((2, n_exp, tokens // n_exp, padded), BF16),
+        idx,
         gathered,
-        gathered_other,
         out_proj_t,
-    )
-    gains = norm_gain.reshape(n_req * 2, 1, width)
-    router_t = router.T.reshape(experts, n_req * 2, width).transpose(1, 0, 2)
-    terms, resid, idx, gains, router_t, w_down_other = lax.optimization_barrier(
-        (terms, resid, idx, gains, router_t, w_down_other)
-    )
-    terms = lax.all_to_all(terms, "exp", split_axis=0, concat_axis=0, tiled=True)
-    attended = jnp.sum(terms.astype(F32), 0).astype(BF16)
-    hidden_sum = (resid.astype(F32) + attended.astype(F32)).astype(BF16)
-
-    fanned = jnp.broadcast_to(hidden_sum[None], (n_req * n_exp,) + hidden_sum.shape)
+        outside=(other_t,),
+        scratch=(
+            pltpu.VMEM((width, half_heads * DV), BF16),
+            pltpu.SemaphoreType.DMA,
+        ),
+    )
+    terms, idx, gains, router_t, w_down_other = lax.optimization_barrier(
+        (terms, idx, gains, router_t, w_down_other)
+    )
+    terms = terms.reshape(2 * n_exp, tokens // n_exp, padded)
+    terms = lax.all_to_all(terms, ("seq", "exp"), split_axis=0, concat_axis=0, tiled=True)
+    fanned = call(
+        hidden_kernel,
+        "hidden",
+        shape((n_req * n_exp, tokens // n_exp, padded), BF16),
+        idx,
+        terms,
+    )
     own = lax.all_to_all(fanned, ("req", "exp"), split_axis=0, concat_axis=0, tiled=True)
     own = own.reshape(n_req, tokens, padded)
     other = swap(own)
     hidden_units = w_gate.shape[1]
-    *started, w_up = call(
+    started = call(
         gate_up_own_kernel,
         "gate_up_own",
         (
@@ -410,23 +459,21 @@
             shape((tokens, hidden_units), F32),
             shape((tokens, experts), F32),
             shape((tokens, 128), F32),
-            shape(w_up.shape, BF16),
         ),
         idx,
         own,
         gains,
         w_gate,
+        w_up,
         router_t,
-        outside=(w_up,),
-        scratch=(pltpu.SemaphoreType.DMA((UP_COPIES,)),),
     )
     half = model_width // 2
-    act, w_down, w_down_other = call(
+    act, rows_here, w_down_other = call(
         gate_up_both_kernel,
         "gate_up_both",
         (
             shape((tokens, hidden_units), BF16),
-            shape((hidden_units, half), BF16),
+            shape((n_req * 2, 16, padded), F32),
             shape((hidden_units, half), BF16),
         ),
         idx,
@@ -437,7 +484,7 @@
         w_gate,
         w_up,
         router_t,
-        outside=(w_down, w_down_other),
+        outside=(w_down_other,),
         scratch=(pltpu.SemaphoreType.DMA((2,)),),
     )
     pieces = call(
@@ -450,23 +497,23 @@
         w_down,
         w_down_other,
     )
-    pieces, own, other, idx = lax.optimization_barrier((pieces, own, other, idx))
-    s, place = idx[0], idx[-1]
-    hid_own = lax.dynamic_slice_in_dim(own, place, own_rows, 1)[:, :, :width]
-    hid_other = lax.dynamic_slice_in_dim(other, place, own_rows, 1)[:, :, :width]
-    hid = jnp.where(s == 0, jnp.stack([hid_own, hid_other], 1), jnp.stack([hid_other, hid_own], 1))
-    hid = hid.transpose(2, 0, 1, 3).reshape(own_rows, model_width)
     pieces = lax.all_to_all(pieces, ("exp", "req"), split_axis=0, concat_axis=0, tiled=True)
-    routed = jnp.sum(pieces.astype(F32), 0)
-    routed = routed.reshape(2, own_rows, half)
-    routed_mine = lax.dynamic_index_in_dim(routed, s, 0, False)
-    routed_theirs = swap(lax.dynamic_index_in_dim(routed, 1 - s, 0, False))
-    routed = jnp.where(
-        s == 0,
-        jnp.concatenate([routed_mine, routed_theirs], -1),
-        jnp.concatenate([routed_theirs, routed_mine], -1),
-    )
-    return (hid.astype(F32) + routed).astype(BF16)
+    mine, theirs = call(
+        routed_kernel,
+        "routed",
+        (shape((own_rows, half), F32), shape((own_rows, half), F32)),
+        idx,
+        pieces,
+    )
+    return call(
+        finish_kernel,
+        "finish",
+        shape((own_rows, model_width), BF16),
+        idx,
+        mine,
+        swap(theirs),
+        rows_here,
+    )
 
 
 def solution(mesh):

time: 136 us -> 138 us (1.015)
  blocking collectives: 65.7 us -> 99.1 us
  waiting for transfers between devices: 22.8 us -> 3.18 us
  starting transfers between devices: 14.3 us -> 8.56 us
  between operations: 6.55 us -> 0.86 us
  Pallas kernels: 18.4 us -> 20.6 us
  other arithmetic: 3.16 us -> 1.47 us
    all_to_all x1 -> x2, blocking collectives: 8.64 us -> 41.1 us  [the longest x1 29.1 us: per_device(): lax.all_to_all(pieces, ('exp', 'req'), split_axis=0, concat_axis=0, tiled...]
    all_to_all x1 -> x0, waiting for transfers between devices: 18.6 us -> none  [per_device(): lax.all_to_all(pieces, ('exp', 'req'), split_axis=0, concat_axis=0, tiled...]
    all_to_all x1 -> x0, starting transfers between devices: 5.53 us -> none  [per_device(): lax.all_to_all(pieces, ('exp', 'req'), split_axis=0, concat_axis=0, tiled...]
    reduce_sum x2 -> x0, other arithmetic: 2.28 us -> none  [the longest x1 2.26 us: per_device(): routed = jnp.sum(pieces.astype(F32), 0)]
    pallas_call x7 -> x9, Pallas kernels: 18.4 us -> 20.6 us  [call(): pl.pallas_call(kernel, out_shape=out_shape, in_specs=[pl.BlockSpec(memory...]
    reshape x2, local copies, waits for them, and re-layouts: 0.52 us -> 2.19 us  [per_device(): router_t = router.T.reshape(experts, n_req * 2, width).transpose(1, 0, 2)]
  transfers between devices with their start and end apart: 7 -> 6, of which waited for: 5 -> 3; matrix products, arithmetic and copies ran while one was open for 3% -> 4% of each run, Pallas kernels for 9% -> 8%
where the time goes in v4:
time: 138 us
  blocking collectives  99.1 us (72%)
  Pallas kernels  20.6 us (15%)
  starting transfers between devices  8.56 us (6%)
  local copies, waits for them, and re-layouts  4.11 us (3%)
  waiting for transfers between devices  3.18 us (2%)
  other arithmetic  1.47 us (1%)
    all_to_all x1, blocking collectives, per_device(): lax.all_to_all(fanned, ('req', 'exp'), split_axis=0, concat_axis=0, tiled...  32.7 us
    all_to_all x1, blocking collectives, per_device(): lax.all_to_all(pieces, ('exp', 'req'), split_axis=0, concat_axis=0, tiled...  29.1 us
    all_to_all x1, blocking collectives, per_device(): lax.all_to_all(fanned, 'req', split_axis=0, concat_axis=0, tiled=True)  25.2 us
    pallas_call x9, Pallas kernels, call(): pl.pallas_call(kernel, out_shape=out_shape, in_specs=[pl.BlockSpec(memory...  20.6 us
    all_to_all x1, blocking collectives, per_device(): lax.all_to_all(terms, ('seq', 'exp'), split_axis=0, concat_axis=0, tiled=...  12 us
    ppermute x6, starting transfers between devices, swap(): return lax.ppermute(x, 'seq', SWAP)  8.56 us
    ppermute x6, waiting for transfers between devices, swap(): return lax.ppermute(x, 'seq', SWAP)  3.18 us
  transfers between devices with their start and end apart: 6, of which 3 were waited for; matrix products, arithmetic and copies ran while one was open for 4% of the time, Pallas kernels for 8%

profile of v4, /device:TPU:1, one launch (start us, length us, event | category | flops | bytes accessed | tf_op | source)
XLA Modules:
  0.0 137.9 jit_solution(18259535836774021583)
XLA Ops:
  0.0 1.4 %collective-permute-start.2 = (bf16[256,7168]{1,0:T(8,128)(2,1)}, bf16[256,7168]{1,0:T(8,128)(2,1)}, u32[]{:S(2)}, u32[]{:S(2)}) collective-permute-start(bf16[256,7168]{1,0:T(8,128)(2,1)} %bitcast.29), channel_id=1, source_target_pairs={{0,4},{4,0},{1,5},{5,1},{2,6},{6,2},{3,7},{7,3},{8,12},{12,8},{9,1... | collective-permute-start | bytes 11010056 | tf_op jit(solution)/shard_map/ppermute | solution.py:18
  2.0 0.7 concatenate.6.idx
  2.8 3.8 %attend.1 = (bf16[256,640]{1,0:T(8,128)(2,1)}, f32[256,512]{1,0:T(8,128)S(1)}, f32[256,256]{1,0:T(8,128)S(1)}, bf16[16,512,128]{2,1,0:T(8,128)(2,1)S(1)}) custom-call(s32[8]{0:T(128)S(1)} %concatenate.6.idx, bf16[16,32,576]{2,1,0:T(8,128)(2,1)} %bitcast.34, bf16[192,576]{1,0:T(8,128)(2,1)} %bitcast.35, bf16[32,512,128]{2,1,0:T(8,128)(2,1)} %value_up.1), custom_call_target="tpu_custom_call" | custom-call | tf_op jit(solution)/shard_map/attend/pallas_call | solution.py:27
  7.5 0.8 convert_reduce_fusion
  9.0 0.8 reshape.30
  9.8 1.1 reshape.33
  10.9 1.1 copy.25
  12.0 1.3 values.1
  13.4 25.2 %all_to_all.20.gathered = bf16[16,17,16,128]{3,2,1,0:T(8,128)(2,1)S(1)} all-to-all(bf16[16,17,16,128]{3,2,1,0:T(8,128)(2,1)S(1)} %values.1), channel_id=1, replica_groups=mesh['req'=16,'seq'=2,'exp'=4] {'req'}, dimensions={0} | all-to-all | bytes 2228224 | tf_op jit(solution)/shard_map/all_to_all | solution.py:424
  38.6 3.3 %project.1 = bf16[2,4,64,256]{3,2,1,0:T(8,128)(2,1)S(1)} custom-call(s32[8]{0:T(128)S(1)} %concatenate.6.idx, bf16[224,4096]{1,0:T(8,128)(2,1)} %collective-permute-done.other_there, bf16[16,17,16,128]{3,2,1,0:T(8,128)(2,1)S(1)} %all_to_all.20.gathered, bf16[224,4096]{1,0:T(8,128)(2,1)S(1)} %bitcast.32), custom_call_target="tpu_custom_call" | custom-call | tf_op jit(solution)/shard_map/project/pallas_call | solution.py:27
  41.9 12.0 %all_to_all.21.terms = bf16[8,64,256]{2,1,0:T(8,128)(2,1)S(1)} all-to-all(bf16[8,64,256]{2,1,0:T(8,128)(2,1)S(1)} %bitcast.33), channel_id=1, replica_groups=mesh['req'=16,'seq'=2,'exp'=4] {'seq','exp'}, dimensions={0} | all-to-all | bytes 524288 | tf_op jit(solution)/shard_map/all_to_all | solution.py:442
  53.9 0.8 hidden.1
  54.8 32.7 %all_to_all.22 = bf16[64,64,256]{2,1,0:T(8,128)(2,1)S(1)} all-to-all(bf16[64,64,256]{2,1,0:T(8,128)(2,1)S(1)} %hidden.1), channel_id=1, replica_groups=mesh['req'=16,'seq'=2,'exp'=4] {'req','exp'}, dimensions={0} | all-to-all | bytes 4194304 | tf_op jit(solution)/shard_map/all_to_all | solution.py:450
  87.5 3.3 %collective-permute-start.3 = (bf16[16,256,256]{2,1,0:T(8,128)(2,1)S(1)}, bf16[16,256,256]{2,1,0:T(8,128)(2,1)S(1)}, u32[]{:S(2)}, u32[]{:S(2)}) collective-permute-start(bf16[16,256,256]{2,1,0:T(8,128)(2,1)S(1)} %bitcast.19), channel_id=1, source_target_pairs={{0,4},{4,0},{1,5},{5,1},{2,6},{6,2},{3,7},{7,3},{8,12},{12,8},{9,1... | collective-permute-start | bytes 6291464 | tf_op jit(solution)/shard_map/ppermute | solution.py:18
  90.9 2.4 %gate_up_own.1 = (f32[256,256]{1,0:T(8,128)S(1)}, f32[256,256]{1,0:T(8,128)S(1)}, f32[256,16]{1,0:T(8,128)S(1)}, f32[256,128]{1,0:T(8,128)S(1)}) custom-call(s32[8]{0:T(128)S(1)} %concatenate.6.idx, bf16[16,256,256]{2,1,0:T(8,128)(2,1)S(1)} %bitcast.20, bf16[32,1,224]{2,1,0:T(2,128)(2,1)S(1)} %copy.22.gains, bf16[7168,256]{1,0:T(8,128)(2,1)S(1)} %bitcast.22, ...), custom_call_target="tpu_custom_call" | custom-call | tf_op jit(solution)/shard_map/gate_up_own/pallas_call | solution.py:27
  93.3 1.3 collective-permute-done.3.other
  94.6 4.5 %gate_up_both.1 = (bf16[256,256]{1,0:T(8,128)(2,1)S(1)}, f32[32,16,256]{2,1,0:T(8,128)S(1)}, bf16[256,3584]{1,0:T(8,128)(2,1)S(1)}) custom-call(s32[8]{0:T(128)S(1)} %concatenate.6.idx, bf16[256,7168]{1,0:T(8,128)(2,1)} %collective-permute-done.2.w_down_there, f32[256,256]{1,0:T(8,128)S(1)} %get-tuple-element.32.gate, f32[256,256]{1,0:T(8,128)S(1)} %get-tuple-element.33.up, ...), custom_call_target="tpu_custom_call" | custom-call | tf_op jit(solution)/shard_map/gate_up_both/pallas_call | solution.py:27
  99.6 1.0 collective-permute-done.4.act_other
  100.6 1.7 %down.1 = bf16[64,4,3584]{2,1,0:T(4,128)(2,1)S(1)} custom-call(s32[8]{0:T(128)S(1)} %concatenate.6.idx, bf16[256,256]{1,0:T(8,128)(2,1)S(1)} %get-tuple-element.36.act, bf16[256,256]{1,0:T(8,128)(2,1)S(1)} %collective-permute-done.4.act_other, bf16[256,7168]{1,0:T(8,128)(2,1)S(1)} %bitcast.30, bf16[256,3584]{1,0:T(8,128)(2,1)S(1)} %get-tuple-element.37.w_down_other), custom_call_target="tpu_custom_call" | custom-call | tf_op jit(solution)/shard_map/down/pallas_call | solution.py:27
  102.3 29.1 %all_to_all.23.pieces = bf16[64,4,3584]{2,1,0:T(4,128)(2,1)S(1)} all-to-all(bf16[64,4,3584]{2,1,0:T(4,128)(2,1)S(1)} %down.1), channel_id=1, replica_groups=mesh['req'=16,'seq'=2,'exp'=4] {'exp','req'}, dimensions={0} | all-to-all | bytes 3670016 | tf_op jit(solution)/shard_map/all_to_all | solution.py:500
  131.5 1.4 %routed.1 = (f32[2,3584]{1,0:T(2,128)S(1)}, f32[2,3584]{1,0:T(2,128)S(1)}) custom-call(s32[8]{0:T(128)S(1)} %concatenate.6.idx, bf16[64,4,3584]{2,1,0:T(4,128)(2,1)S(1)} %all_to_all.23.pieces), custom_call_target="tpu_custom_call" | custom-call | tf_op jit(solution)/shard_map/routed/pallas_call | solution.py:27
  132.9 2.8 %collective-permute-start.5 = (f32[2,3584]{1,0:T(2,128)S(1)}, f32[2,3584]{1,0:T(2,128)S(1)}, u32[]{:S(2)}, u32[]{:S(2)}) collective-permute-start(f32[2,3584]{1,0:T(2,128)S(1)} %get-tuple-element.39), channel_id=1, source_target_pairs={{0,4},{4,0},{1,5},{5,1},{2,6},{6,2},{3,7},{7,3},{8,12},{12,8},{9,1... | collective-permute-start | bytes 86024 | tf_op jit(solution)/shard_map/ppermute | solution.py:18
  135.7 0.9 collective-permute-done.5.theirs
  136.5 1.4 finish.1
  (34 shorter events, 2.2 us)
Async XLA Ops:
  0.0 41.9 %collective-permute-start.2 = (bf16[256,7168]{1,0:T(8,128)(2,1)}, bf16[256,7168]{1,0:T(8,128)(2,1)}, u32[]{:S(2)}, u32[]{:S(2)}) collective-permute-start(bf16[256,7168]{1,0:T(8,128)(2,1)} %bitcast.29), channel_id=1, source_target_pairs={{0,4},{4,0},{1,5},{5,1},{2,6},{6,2},{3,7},{7,3},{8,12},{12,8},{9,1... | collective-permute-start | bytes 11010056 | tf_op jit(solution)/shard_map/ppermute | solution.py:18
  1.4 37.2 %collective-permute-start = (bf16[224,4096]{1,0:T(8,128)(2,1)}, bf16[224,4096]{1,0:T(8,128)(2,1)}, u32[]{:S(2)}, u32[]{:S(2)}) collective-permute-start(bf16[224,4096]{1,0:T(8,128)(2,1)} %bitcast.31), channel_id=1, source_target_pairs={{0,4},{4,0},{1,5},{5,1},{2,6},{6,2},{3,7},{7,3},{8,12},{12,8},{9,1... | collective-permute-start | bytes 5505032 | tf_op jit(solution)/shard_map/ppermute | solution.py:18
  2.8 4.4 %copy-start.8 = (bf16[7168]{0:T(1024)(128)(2,1)S(1)}, bf16[7168]{0:T(1024)(128)(2,1)}, u32[]{:S(2)}) copy-start(bf16[7168]{0:T(1024)(128)(2,1)} %param.20) | copy-start | bytes 43012
  2.8 4.5 %copy-start.7 = (bf16[2,7168]{1,0:T(2,128)(2,1)S(1)}, bf16[2,7168]{1,0:T(2,128)(2,1)}, u32[]{:S(2)}) copy-start(bf16[2,7168]{1,0:T(2,128)(2,1)} %param.13) | copy-start | bytes 86020
  2.8 7.0 %copy-start.4 = (bf16[7168,16]{0,1:T(8,128)(2,1)S(1)}, bf16[7168,16]{0,1:T(8,128)(2,1)}, u32[]{:S(2)}) copy-start(bf16[7168,16]{0,1:T(8,128)(2,1)} %param.21) | copy-start | bytes 688132
  6.6 5.4 %collective-permute-start.1 = (bf16[256,640]{1,0:T(8,128)(2,1)}, bf16[256,640]{1,0:T(8,128)(2,1)S(1)}, u32[]{:S(2)}, u32[]{:S(2)}) collective-permute-start(bf16[256,640]{1,0:T(8,128)(2,1)} %get-tuple-element.25), channel_id=1, source_target_pairs={{0,4},{4,0},{1,5},{5,1},{2,6},{6,2},{3,7},{7,3},{8,12},{12,8},{9,1... | collective-permute-start | bytes 983048 | tf_op jit(solution)/shard_map/ppermute | solution.py:18
  7.2 2.5 %copy-start.5 = (bf16[32,1,224]{2,0,1:T(8,128)(2,1)}, bf16[32,1,224]{2,0,1:T(8,128)(2,1)S(1)}, u32[]{:S(2)}) copy-start(bf16[32,1,224]{2,0,1:T(8,128)(2,1)S(1)} %reshape.32) | copy-start | bytes 43012
  13.3 25.3 %copy-start.3 = (bf16[4096,224]{0,1:T(8,128)(2,1)S(1)}, bf16[4096,224]{0,1:T(8,128)(2,1)}, u32[]{:S(2)}) copy-start(bf16[4096,224]{0,1:T(8,128)(2,1)} %param.19) | copy-start | bytes 5505028
  38.6 52.3 %copy-start.1 = (bf16[1,7168,256]{2,1,0:T(8,128)(2,1)S(1)}, bf16[1,7168,256]{2,1,0:T(8,128)(2,1)}, u32[]{:S(2)}) copy-start(bf16[1,7168,256]{2,1,0:T(8,128)(2,1)} %param.24) | copy-start | bytes 11010052
  54.7 36.1 %copy-start.6 = (bf16[32,1,224]{2,0,1:T(8,128)(2,1)S(1)}, bf16[32,1,224]{2,0,1:T(8,128)(2,1)}, u32[]{:S(2)}) copy-start(bf16[32,1,224]{2,0,1:T(8,128)(2,1)} %copy-done.5) | copy-start | bytes 43012
  54.7 36.1 %copy-start = (bf16[1,7168,256]{2,1,0:T(8,128)(2,1)S(1)}, bf16[1,7168,256]{2,1,0:T(8,128)(2,1)}, u32[]{:S(2)}) copy-start(bf16[1,7168,256]{2,1,0:T(8,128)(2,1)} %param.23) | copy-start | bytes 11010052
  87.5 7.1 %collective-permute-start.3 = (bf16[16,256,256]{2,1,0:T(8,128)(2,1)S(1)}, bf16[16,256,256]{2,1,0:T(8,128)(2,1)S(1)}, u32[]{:S(2)}, u32[]{:S(2)}) collective-permute-start(bf16[16,256,256]{2,1,0:T(8,128)(2,1)S(1)} %bitcast.19), channel_id=1, source_target_pairs={{0,4},{4,0},{1,5},{5,1},{2,6},{6,2},{3,7},{7,3},{8,12},{12,8},{9,1... | collective-permute-start | bytes 6291464 | tf_op jit(solution)/shard_map/ppermute | solution.py:18
  94.6 6.0 %copy-start.2 = (bf16[1,256,7168]{2,1,0:T(8,128)(2,1)S(1)}, bf16[1,256,7168]{2,1,0:T(8,128)(2,1)}, u32[]{:S(2)}) copy-start(bf16[1,256,7168]{2,1,0:T(8,128)(2,1)} %param.25) | copy-start | bytes 11010052
  99.2 1.4 %collective-permute-start.4 = (bf16[256,256]{1,0:T(8,128)(2,1)S(1)}, bf16[256,256]{1,0:T(8,128)(2,1)S(1)}, u32[]{:S(2)}, u32[]{:S(2)}) collective-permute-start(bf16[256,256]{1,0:T(8,128)(2,1)S(1)} %get-tuple-element.36.act), channel_id=1, source_target_pairs={{0,4},{4,0},{1,5},{5,1},{2,6},{6,2},{3,7},{7,3},{8,12},{12,8},{9,1... | collective-permute-start | bytes 393224 | tf_op jit(solution)/shard_map/ppermute | solution.py:18
  132.9 3.6 %collective-permute-start.5 = (f32[2,3584]{1,0:T(2,128)S(1)}, f32[2,3584]{1,0:T(2,128)S(1)}, u32[]{:S(2)}, u32[]{:S(2)}) collective-permute-start(f32[2,3584]{1,0:T(2,128)S(1)} %get-tuple-element.39), channel_id=1, source_target_pairs={{0,4},{4,0},{1,5},{5,1},{2,6},{6,2},{3,7},{7,3},{8,12},{12,8},{9,1... | collective-permute-start | bytes 86024 | tf_op jit(solution)/shard_map/ppermute | solution.py:18

commit v5 on v4

v5 whole, which is shorter than its diff:
```python
import jax
import jax.numpy as jnp
from jax import lax
from jax.experimental import pallas as pl
from jax.experimental.pallas import tpu as pltpu
from jax.sharding import PartitionSpec as P

DL = 512
DR = 64
DV = 128
BLOCK = 64
F32 = jnp.float32
BF16 = jnp.bfloat16
SWAP = [(0, 1), (1, 0)]


def swap(x):
    return lax.ppermute(x, "seq", SWAP)


def vmem():
    return pl.BlockSpec(memory_space=pltpu.VMEM)


def call(kernel, name, out_shape, *operands, scalars=(), outside=(), scratch=(), limit=24):
    many = isinstance(out_shape, (tuple, list))
    return pl.pallas_call(
        kernel,
        out_shape=out_shape,
        in_specs=[pl.BlockSpec(memory_space=pltpu.SMEM) for _ in scalars]
        + [pl.BlockSpec(memory_space=pltpu.HBM) for _ in outside]
        + [vmem() for _ in operands],
        out_specs=[vmem() for _ in out_shape] if many else vmem(),
        scratch_shapes=list(scratch),
        compiler_params=pltpu.CompilerParams(vmem_limit_bytes=limit * 2**20),
        name=name,
    )(*scalars, *[pltpu.with_memory_space_constraint(a, pltpu.HBM) for a in outside], *operands)


def one_hot(shape, source):
    rows = lax.broadcasted_iota(jnp.int32, shape, 0)
    columns = lax.broadcasted_iota(jnp.int32, shape, 1)
    return jnp.where(source(rows) == columns, 1.0, 0.0).astype(BF16)


def parts_of(a):
    first = a.astype(BF16)
    rest = a - first.astype(F32)
    second = rest.astype(BF16)
    return first, second, (rest - second.astype(F32)).astype(BF16)


def attend_kernel(
    lengths, blocks, queries, cache, value_up, sent, kept, kept_stats, value_half, query_rows, key_rows, sems
):
    drafts, heads, width = queries.shape
    side = lax.axis_index("seq")
    length, first, second = lengths[0], blocks[0], blocks[1]
    shard_len = cache.shape[0]
    copies = [
        pltpu.make_async_copy(
            cache.at[pl.ds(pl.multiple_of(first * BLOCK, BLOCK), BLOCK), :],
            key_rows.at[pl.ds(0, BLOCK), :],
            sems.at[0],
        ),
        pltpu.make_async_copy(
            cache.at[pl.ds(pl.multiple_of(second * BLOCK, BLOCK), BLOCK), :],
            key_rows.at[pl.ds(BLOCK, BLOCK), :],
            sems.at[1],
        ),
        pltpu.make_async_copy(queries, query_rows, sems.at[2]),
    ]
    quarter = heads // 8
    value_copies = [
        pltpu.make_async_copy(
            value_up.at[pl.ds(side * (heads // 2) + i * quarter, quarter)],
            value_half.at[pl.ds(i * quarter, quarter)],
            sems.at[3 + i],
        )
        for i in range(4)
    ]
    for place, copy in enumerate(copies):
        copy.start(priority=place // 2)
    for place, copy in enumerate(value_copies):
        copy.start(priority=place % 2)
    for copy in copies:
        copy.wait()
    keys = key_rows[...]
    rows = query_rows[...].reshape(drafts * heads, width)
    scores = lax.dot_general(
        rows, keys, (((1,), (1,)), ((), ())), preferred_element_type=F32
    ) * ((DV + DR) ** (-0.5))
    row = lax.broadcasted_iota(jnp.int32, scores.shape, 0)
    col = lax.broadcasted_iota(jnp.int32, scores.shape, 1)
    block = jnp.where(col < BLOCK, first, second - 1)
    usable = side * shard_len + block * BLOCK + col < length - (drafts - 1) + row // heads
    top = jnp.max(jnp.where(usable, scores, -1e30), -1, keepdims=True)
    probs = jnp.where(usable, jnp.exp(scores - top), 0.0).astype(BF16)
    total = jnp.sum(probs.astype(F32), -1, keepdims=True)
    out = jnp.dot(probs, keys[:, :DL], preferred_element_type=F32)
    half = heads // 2

    def split(a):
        a = a.reshape(drafts, 2, half, a.shape[-1])
        low = a[:, 0].reshape(drafts * half, a.shape[-1])
        high = a[:, 1].reshape(drafts * half, a.shape[-1])
        return jnp.where(side == 0, low, high), jnp.where(side == 0, high, low)

    mine, theirs = split(out)
    stats = jnp.concatenate(
        [jnp.broadcast_to(top, (top.shape[0], 128)), jnp.broadcast_to(total, (top.shape[0], 128))],
        -1,
    )
    my_stats, their_stats = split(stats)
    kept[...] = mine
    kept_stats[...] = my_stats
    sent[:, :DL] = theirs.astype(BF16)
    top_parts, sum_parts = parts_of(their_stats[:, :128]), parts_of(their_stats[:, 128:])
    lane = lax.broadcasted_iota(jnp.int32, (drafts * half, 128), 1)
    packed = jnp.zeros((drafts * half, 128), F32)
    for place, part in enumerate(top_parts + sum_parts):
        packed = jnp.where(lane == place, part.astype(F32), packed)
    sent[:, DL:] = packed.astype(BF16)
    for copy in value_copies:
        copy.wait()


def values_kernel(kept, kept_stats, arrived, value_up, residual, expert_ids, fanned):
    rows = kept.shape[0]
    dests, slabs, drafts, _ = fanned.shape
    half = slabs - 1
    packed = arrived[:, DL:].astype(F32)
    lane = lax.broadcasted_iota(jnp.int32, packed.shape, 1)
    other_top = jnp.sum(jnp.where(lane < 3, packed, 0.0), -1, keepdims=True)
    other_sum = jnp.sum(jnp.where((lane >= 3) & (lane < 6), packed, 0.0), -1, keepdims=True)
    my_top, my_sum = kept_stats[:, 0:1], kept_stats[:, 128:129]
    top = jnp.maximum(my_top, other_top)
    my_scale, other_scale = jnp.exp(my_top - top), jnp.exp(other_top - top)
    total = my_scale * my_sum + other_scale * other_sum
    latent = (my_scale / total) * kept[...] + (other_scale / total) * arrived[:, :DL].astype(F32)
    latent = latent.astype(BF16)
    order = one_hot((rows, rows), lambda i: i % drafts * half + i // drafts)
    latent = jnp.dot(order, latent, preferred_element_type=F32).astype(BF16)
    for head in range(half):
        out = jnp.dot(
            latent[head * drafts : (head + 1) * drafts],
            value_up[head],
            preferred_element_type=F32,
        ).astype(BF16)
        for dest in range(dests):
            fanned[dest, head] = out
    own_rows, model_width = residual.shape
    width = model_width // (2 * dests)
    lane = lax.broadcasted_iota(jnp.int32, (own_rows, 128), 1)
    named = jnp.zeros((own_rows, 128), F32)
    for k in range(expert_ids.shape[1]):
        named += jnp.where(expert_ids[:, k : k + 1] + (width - 128) == lane, 1.0, 0.0)
    values = residual[...].astype(F32)
    values = jnp.concatenate([values, jnp.zeros((own_rows, 128), F32)], -1)
    for dest in range(dests):
        pieces = []
        for row in range(own_rows):
            for core in range(2):
                start = (dest * 2 + core) * width
                pieces.append(values[row : row + 1, start : start + 128])
                tail = values[row : row + 1, start + 128 : start + 256]
                pieces.append(jnp.where(lane[:1] < width - 128, tail, named[row : row + 1]))
        pieces.append(jnp.zeros((drafts - len(pieces), 128), F32))
        fanned[dest, half] = jnp.concatenate(pieces, 0).astype(BF16)


def project_terms(gathered, out_proj_t, side):
    reqs, slabs, drafts, lanes = gathered.shape
    half = slabs - 1
    total = None
    for head in range(0, half, 2):
        pair = jnp.concatenate(
            [gathered[:, head].reshape(reqs * drafts, lanes), gathered[:, head + 1].reshape(reqs * drafts, lanes)],
            -1,
        )
        start = pl.multiple_of((side * half + head) * lanes, 256)
        term = lax.dot_general(
            pair,
            out_proj_t[:, pl.ds(start, 2 * lanes)],
            (((1,), (1,)), ((), ())),
            preferred_element_type=F32,
        )
        total = term if total is None else total + term
    return total


def project_own_kernel(gathered, out_proj_t, swapped, out):
    out[...] = project_terms(gathered, out_proj_t, lax.axis_index("seq"))


def project_both_kernel(started, gathered, gathered_other, out_proj_t, terms, residual):
    reqs, slabs, drafts, lanes = gathered.shape
    exps, _, padded = terms.shape
    width = started.shape[1]
    side = lax.axis_index("seq")
    total = (started[...] + project_terms(gathered_other, out_proj_t, 1 - side)).astype(BF16)
    tokens = reqs * drafts
    own_rows = drafts // (2 * exps)

    def source(i):
        exp, req = i // (tokens // exps), i // (2 * own_rows) % reqs
        seq, row = i // own_rows % 2, i % own_rows
        return ((req * 2 + seq) * exps + exp) * own_rows + row

    total = jnp.dot(one_hot((tokens, tokens), source), total, preferred_element_type=F32)
    total = jnp.concatenate([total, jnp.zeros((tokens, padded - width), F32)], -1)
    terms[...] = total.astype(BF16).reshape(terms.shape)
    tiles = padded // lanes
    for tile in range(tiles):
        picked = jnp.zeros((tokens // exps, lanes), F32)
        for rows, from_side in ((gathered, side), (gathered_other, 1 - side)):

            def residual_source(i):
                req, seq, row = i // (2 * own_rows), i // own_rows % 2, i % own_rows
                place = req * drafts + (row * 2 + side) * tiles + tile
                return jnp.where(seq == from_side, place, -1)

            picked += jnp.dot(
                one_hot((tokens // exps, tokens), residual_source),
                rows[:, slabs - 1].reshape(tokens, lanes),
                preferred_element_type=F32,
            )
        residual[:, tile * lanes : (tile + 1) * lanes] = picked.astype(BF16)


def hidden_kernel(terms, residual, fanned):
    attended = jnp.sum(terms[...].astype(F32), 0).astype(BF16)
    hidden = (residual[...].astype(F32) + attended.astype(F32)).astype(BF16)
    for dest in range(fanned.shape[0]):
        fanned[dest] = hidden


def expert_terms(rows, gains, w_gate, w_up, router_t, side):
    steps, tokens, _ = rows.shape
    width = gains.shape[1] // (2 * steps)
    gate = jnp.zeros((tokens, w_gate.shape[1]), F32)
    up = jnp.zeros((tokens, w_up.shape[1]), F32)
    logits = jnp.zeros((tokens, router_t.shape[0]), F32)
    squares = jnp.zeros((tokens, width), F32)

    def columns_of(a, i):
        low = a[:, i * 2 * width : (i * 2 + 1) * width].astype(F32)
        high = a[:, (i * 2 + 1) * width : (i * 2 + 2) * width].astype(F32)
        return jnp.where(side == 0, low, high)

    for i in range(steps):
        start = pl.multiple_of((i * 2 + side) * width, 32)
        hidden = rows[i][:, :width].astype(F32)
        scaled = (hidden * columns_of(gains, i)).astype(BF16)
        gate += jnp.dot(scaled, w_gate[pl.ds(start, width), :], preferred_element_type=F32)
        up += jnp.dot(scaled, w_up[pl.ds(start, width), :], preferred_element_type=F32)
        logits += lax.dot_general(
            scaled,
            columns_of(router_t, i).astype(BF16),
            (((1,), (1,)), ((), ())),
            preferred_element_type=F32,
        )
        squares += hidden * hidden
    return gate, up, logits, jnp.sum(squares, -1, keepdims=True)


def gate_up_own_kernel(own, gains, w_gate, w_up, router_t, gate, up, logits, squares):
    a, b, c, d = expert_terms(own, gains, w_gate, w_up, router_t, lax.axis_index("seq"))
    gate[...], up[...], logits[...] = a, b, c
    squares[...] = jnp.broadcast_to(d, squares.shape)


def gate_up_both_kernel(
    gate, up, logits, squares, own, other, gains, w_gate, w_up, router_t, act, rows_here
):
    side = lax.axis_index("seq")
    own_rows = rows_here.shape[1]
    place = (lax.axis_index("exp") * own.shape[0] + lax.axis_index("req")) * 2 + side
    place = place * own_rows
    around = pl.ds(pl.multiple_of(place // 16 * 16, 16), 16)
    near = lax.broadcasted_iota(jnp.int32, (16, own.shape[2]), 0)
    for rows, from_side in ((own, side), (other, 1 - side)):
        for i in range(own.shape[0]):
            tile = rows[i, around, :].astype(F32)
            picked = [
                jnp.sum(jnp.where(near == place % 16 + row, tile, 0.0), 0, keepdims=True)
                for row in range(own_rows)
            ]
            rows_here[i * 2 + from_side] = jnp.concatenate(picked, 0)
    width = gains.shape[1] // (2 * own.shape[0])
    experts = logits.shape[1]
    columns = gains.shape[1]
    a, b, c, d = expert_terms(other, gains, w_gate, w_up, router_t, 1 - side)
    scale = lax.rsqrt((squares[:, 0:1] + d) / columns + 1e-06)
    named = own[0, :, width : width + experts].astype(F32)
    chosen = named * jax.nn.sigmoid((logits[...] + c) * scale)
    mine = lax.broadcasted_iota(jnp.int32, chosen.shape, 1) == lax.axis_index("req")
    weight = jnp.sum(jnp.where(mine, chosen, 0.0), -1, keepdims=True)
    weight = weight / jnp.sum(chosen, -1, keepdims=True) * 2.5
    act[...] = (
        jax.nn.silu((gate[...] + a) * scale) * ((up[...] + b) * scale) * weight
    ).astype(BF16)


DOWN_STEPS = 7


def down_kernel(act, act_other, w_down, w_down_other, out):
    half = out.shape[2]
    block = half // DOWN_STEPS
    for i in range(DOWN_STEPS):
        columns = pl.ds(pl.multiple_of(lax.axis_index("seq") * half + i * block, 128), block)
        total = jnp.dot(act[...], w_down[:, columns], preferred_element_type=F32)
        total += jnp.dot(act_other[...], w_down_other[:, columns], preferred_element_type=F32)
        out[:, :, i * block : (i + 1) * block] = total.reshape(out.shape[:2] + (block,)).astype(BF16)


def routed_kernel(pieces, mine, theirs):
    rows = mine.shape[0]
    total = jnp.sum(pieces[...].astype(F32), 0)
    side = lax.axis_index("seq")
    low, high = total[:rows], total[rows:]
    mine[...] = jnp.where(side == 0, low, high)
    theirs[...] = jnp.where(side == 0, high, low)


def finish_kernel(mine, theirs, rows_here, out):
    blocks, rows, half = rows_here.shape[0], mine.shape[0], mine.shape[1]
    width = 2 * half // blocks
    for side, first, second in ((0, mine, theirs), (1, theirs, mine)):

        @pl.when(lax.axis_index("seq") == side)
        def _():
            for block in range(blocks):
                start = block * width
                source, offset = (first, start) if start < half else (second, start - half)
                total = rows_here[block, :rows, :width] + source[:, offset : offset + width]
                out[:, start : start + width] = total.astype(BF16)


def per_device(
    residual,
    queries,
    latent_cache,
    blocks,
    lengths,
    value_up,
    out_proj,
    norm_gain,
    router,
    expert_ids,
    w_gate,
    w_up,
    w_down,
):
    drafts, heads, qk_width = queries.shape[1:]
    n_req, n_exp = lax.axis_size("req"), lax.axis_size("exp")
    model_width = residual.shape[1]
    experts = router.shape[1]
    width = out_proj.shape[1]
    padded = -(-width // 128) * 128
    own_rows = residual.shape[0]
    tokens = n_req * drafts
    half_heads = heads // 2
    half_rows = drafts * half_heads
    half = model_width // 2
    shape = jax.ShapeDtypeStruct
    w_gate, w_up, w_down = w_gate[0], w_up[0], w_down[0]
    hidden_units = w_gate.shape[1]
    gains, router_t, out_proj_t = norm_gain.reshape(1, model_width), router.T, out_proj.T

    sent, kept, kept_stats, value_half = call(
        attend_kernel,
        "attend",
        (
            shape((half_rows, DL + 128), BF16),
            shape((half_rows, DL), F32),
            shape((half_rows, 256), F32),
            shape((half_heads,) + value_up.shape[1:], BF16),
        ),
        scalars=(lengths, blocks.reshape(-1)),
        outside=(queries[0], latent_cache[0], value_up),
        scratch=(
            pltpu.VMEM(queries.shape[1:], BF16),
            pltpu.VMEM((blocks.shape[2] * BLOCK, qk_width), BF16),
            pltpu.SemaphoreType.DMA((7,)),
        ),
    )
    arrived = swap(sent)
    w_down_other = swap(w_down)
    fanned = call(
        values_kernel,
        "values",
        shape((n_req, half_heads + 1, drafts, DV), BF16),
        kept,
        kept_stats,
        arrived,
        value_half,
        residual,
        expert_ids,
    )
    gathered = lax.all_to_all(fanned, "req", split_axis=0, concat_axis=0, tiled=True)
    gathered_other = swap(gathered)
    started = call(
        project_own_kernel,
        "project_own",
        shape((tokens, width), F32),
        gathered,
        out_proj_t,
        w_down_other,
    )
    terms, resid = call(
        project_both_kernel,
        "project_both",
        (
            shape((n_exp, tokens // n_exp, padded), BF16),
            shape((tokens // n_exp, padded), BF16),
        ),
        started,
        gathered,
        gathered_other,
        out_proj_t,
    )
    terms = lax.all_to_all(terms, "exp", split_axis=0, concat_axis=0, tiled=True)
    fanned = call(
        hidden_kernel,
        "hidden",
        shape((n_req * n_exp, tokens // n_exp, padded), BF16),
        terms,
        resid,
    )
    own = lax.all_to_all(fanned, ("req", "exp"), split_axis=0, concat_axis=0, tiled=True)
    own = own.reshape(n_req, tokens, padded)
    other = swap(own)
    started = call(
        gate_up_own_kernel,
        "gate_up_own",
        (
            shape((tokens, hidden_units), F32),
            shape((tokens, hidden_units), F32),
            shape((tokens, experts), F32),
            shape((tokens, 128), F32),
        ),
        own,
        gains,
        w_gate,
        w_up,
        router_t,
    )
    act, rows_here = call(
        gate_up_both_kernel,
        "gate_up_both",
        (
            shape((tokens, hidden_units), BF16),
            shape((n_req * 2, own_rows, padded), F32),
        ),
        *started,
        own,
        other,
        gains,
        w_gate,
        w_up,
        router_t,
    )
    pieces = call(
        down_kernel,
        "down",
        shape((tokens // 4, 4, half), BF16),
        act,
        swap(act),
        w_down,
        w_down_other,
    )
    pieces = lax.all_to_all(pieces, ("exp", "req"), split_axis=0, concat_axis=0, tiled=True)
    mine, theirs = call(
        routed_kernel,
        "routed",
        (shape((own_rows, half), F32), shape((own_rows, half), F32)),
        pieces,
    )
    return call(
        finish_kernel,
        "finish",
        shape((own_rows, model_width), BF16),
        mine,
        swap(theirs),
        rows_here,
    )


def solution(mesh):
    in_specs = (
        P(("req", "seq", "exp"), None),
        P("req", None, "exp", None),
        P("req", "seq", None),
        P("req", "seq", None),
        P("req"),
        P("exp", None, None),
        P("exp", ("req", "seq")),
        P(),
        P(),
        P(("req", "seq", "exp"), None),
        P("req", None, ("seq", "exp")),
        P("req", None, ("seq", "exp")),
        P("req", ("seq", "exp"), None),
    )
    out_specs = P(("req", "seq", "exp"), None)
    return jax.shard_map(
        per_device, mesh=mesh, in_specs=in_specs, out_specs=out_specs, check_vma=False
    )
```

time: 138 us -> 128 us (0.928)
  Pallas kernels: 20.6 us -> 13 us
  waiting for transfers between devices: 3.18 us -> 7.71 us
  blocking collectives: 99.1 us -> 95.2 us
  local copies, waits for them, and re-layouts: 4.11 us -> 0.7 us
  starting transfers between devices: 8.56 us -> 10.2 us
  other arithmetic: 1.47 us -> 0 us
    pallas_call x9 -> x10, Pallas kernels: 20.6 us -> 13 us  [call(): pl.pallas_call(kernel, out_shape=out_shape, in_specs=[pl.BlockSpec(memory...]
    ppermute x6, waiting for transfers between devices: 3.18 us -> 7.71 us  [swap(): return lax.ppermute(x, 'seq', SWAP)]
    all_to_all x1, blocking collectives: 12 us -> 8.78 us  [per_device(): lax.all_to_all(terms, 'exp', split_axis=0, concat_axis=0, tiled=True)]
    reshape x6 -> x1, local copies, waits for them, and re-layouts: 3.19 us -> 0.02 us  [per_device(): norm_gain.reshape(1, model_width)]
    ppermute x6, starting transfers between devices: 8.56 us -> 10.2 us  [swap(): return lax.ppermute(x, 'seq', SWAP)]
  transfers between devices with their start and end apart: 6 -> 6, of which waited for: 3 -> 5; matrix products, arithmetic and copies ran while one was open for 4% -> 0% of each run, Pallas kernels for 8% -> 5%
where the time goes in v5:
time: 128 us
  blocking collectives  95.2 us (74%)
  Pallas kernels  13 us (10%)
  starting transfers between devices  10.2 us (8%)
  waiting for transfers between devices  7.71 us (6%)
    all_to_all x1, blocking collectives, per_device(): lax.all_to_all(fanned, ('req', 'exp'), split_axis=0, concat_axis=0, tiled...  32.1 us
    all_to_all x1, blocking collectives, per_device(): lax.all_to_all(pieces, ('exp', 'req'), split_axis=0, concat_axis=0, tiled...  29.4 us
    all_to_all x1, blocking collectives, per_device(): lax.all_to_all(fanned, 'req', split_axis=0, concat_axis=0, tiled=True)  24.9 us
    pallas_call x10, Pallas kernels, call(): pl.pallas_call(kernel, out_shape=out_shape, in_specs=[pl.BlockSpec(memory...  13 us
    ppermute x6, starting transfers between devices, swap(): return lax.ppermute(x, 'seq', SWAP)  10.2 us
    all_to_all x1, blocking collectives, per_device(): lax.all_to_all(terms, 'exp', split_axis=0, concat_axis=0, tiled=True)  8.78 us
    ppermute x6, waiting for transfers between devices, swap(): return lax.ppermute(x, 'seq', SWAP)  7.71 us
  transfers between devices with their start and end apart: 6, of which 5 were waited for; matrix products, arithmetic and copies ran while one was open for 0% of the time, Pallas kernels for 5%

profile of v5, /device:TPU:1, one launch (start us, length us, event | category | flops | bytes accessed | tf_op | source)
XLA Modules:
  0.0 127.5 jit_solution(9475231728500054169)
XLA Ops:
  0.0 1.4 %collective-permute-start.1 = (bf16[256,7168]{1,0:T(8,128)(2,1)}, bf16[256,7168]{1,0:T(8,128)(2,1)S(1)}, u32[]{:S(2)}, u32[]{:S(2)}) collective-permute-start(bf16[256,7168]{1,0:T(8,128)(2,1)} %bitcast.18), channel_id=1, source_target_pairs={{0,4},{4,0},{1,5},{5,1},{2,6},{6,2},{3,7},{7,3},{8,12},{12,8},{9,1... | collective-permute-start | bytes 11010056 | tf_op jit(solution)/shard_map/ppermute | solution.py:18
  2.0 0.6 copy-done.7
  2.7 3.0 %attend.1 = (bf16[256,640]{1,0:T(8,128)(2,1)S(1)}, f32[256,512]{1,0:T(8,128)S(1)}, f32[256,256]{1,0:T(8,128)S(1)}, bf16[16,512,128]{2,1,0:T(8,128)(2,1)S(1)}) custom-call(s32[1]{0:T(128)S(6)} %copy.14.lengths, s32[2]{0:T(128)S(1)} %bitcast.22, bf16[16,32,576]{2,1,0:T(8,128)(2,1)} %bitcast.23, bf16[192,576]{1,0:T(8,128)(2,1)} %bitcast.24, ...), custom_call_target="tpu_custom_call" | custom-call | tf_op jit(solution)/shard_map/attend/pallas_call | solution.py:27
  5.8 2.3 %collective-permute-done.arrived = bf16[256,640]{1,0:T(8,128)(2,1)S(1)} collective-permute-done((bf16[256,640]{1,0:T(8,128)(2,1)S(1)}, bf16[256,640]{1,0:T(8,128)(2,1)S(1)}, u32[]{:S(2)}, u32[]{:S(2)}) %collective-permute-start) | collective-permute-done | bytes 327712 | tf_op jit(solution)/shard_map/ppermute | solution.py:18
  8.1 1.1 values.1
  9.2 24.9 %all_to_all.20.gathered = bf16[16,17,16,128]{3,2,1,0:T(8,128)(2,1)S(1)} all-to-all(bf16[16,17,16,128]{3,2,1,0:T(8,128)(2,1)S(1)} %values.1), channel_id=1, replica_groups=mesh['req'=16,'seq'=2,'exp'=4] {'req'}, dimensions={0} | all-to-all | bytes 2228224 | tf_op jit(solution)/shard_map/all_to_all | solution.py:402
  34.1 1.7 %collective-permute-start.2 = (bf16[16,17,16,128]{3,2,1,0:T(8,128)(2,1)S(1)}, bf16[16,17,16,128]{3,2,1,0:T(8,128)(2,1)S(1)}, u32[]{:S(2)}, u32[]{:S(2)}) collective-permute-start(bf16[16,17,16,128]{3,2,1,0:T(8,128)(2,1)S(1)} %all_to_all.20.gathered), channel_id=1, source_target_pairs={{0,4},{4,0},{1,5},{5,1},{2,6},{6,2},{3,7},{7,3},{8,12},{12,8},{9,1... | collective-permute-start | bytes 3342344 | tf_op jit(solution)/shard_map/ppermute | solution.py:18
  35.8 0.5 project_own.1.started
  36.3 1.9 %collective-permute-done.2.gathered_other = bf16[16,17,16,128]{3,2,1,0:T(8,128)(2,1)S(1)} collective-permute-done((bf16[16,17,16,128]{3,2,1,0:T(8,128)(2,1)S(1)}, bf16[16,17,16,128]{3,2,1,0:T(8,128)(2,1)S(1)}, u32[]{:S(2)}, u32[]{:S(2)}) %collective-permute-start.2) | collective-permute-done | bytes 1114144 | tf_op jit(solution)/shard_map/ppermute | solution.py:18
  38.2 0.8 project_both.1
  39.0 8.8 %all_to_all.21.terms = bf16[4,64,256]{2,1,0:T(8,128)(2,1)S(1)} all-to-all(bf16[4,64,256]{2,1,0:T(8,128)(2,1)S(1)} %get-tuple-element.23), channel_id=1, replica_groups=mesh['req'=16,'seq'=2,'exp'=4] {'exp'}, dimensions={0} | all-to-all | bytes 262144 | tf_op jit(solution)/shard_map/all_to_all | solution.py:424
  48.0 32.1 %all_to_all.22 = bf16[64,64,256]{2,1,0:T(8,128)(2,1)S(1)} all-to-all(bf16[64,64,256]{2,1,0:T(8,128)(2,1)S(1)} %hidden.1), channel_id=1, replica_groups=mesh['req'=16,'seq'=2,'exp'=4] {'req','exp'}, dimensions={0} | all-to-all | bytes 4194304 | tf_op jit(solution)/shard_map/all_to_all | solution.py:432
  80.1 3.8 %collective-permute-start.3 = (bf16[16,256,256]{2,1,0:T(8,128)(2,1)S(1)}, bf16[16,256,256]{2,1,0:T(8,128)(2,1)S(1)}, u32[]{:S(2)}, u32[]{:S(2)}) collective-permute-start(bf16[16,256,256]{2,1,0:T(8,128)(2,1)S(1)} %bitcast.9), channel_id=1, source_target_pairs={{0,4},{4,0},{1,5},{5,1},{2,6},{6,2},{3,7},{7,3},{8,12},{12,8},{9,1... | collective-permute-start | bytes 6291464 | tf_op jit(solution)/shard_map/ppermute | solution.py:18
  84.0 2.0 %gate_up_own.1 = (f32[256,256]{1,0:T(8,128)S(1)}, f32[256,256]{1,0:T(8,128)S(1)}, f32[256,16]{1,0:T(8,128)S(1)}, f32[256,128]{1,0:T(8,128)S(1)}) custom-call(bf16[16,256,256]{2,1,0:T(8,128)(2,1)S(1)} %bitcast.10, bf16[1,7168]{1,0:T(2,128)(2,1)S(1)} %reshape.11.gains, bf16[7168,256]{1,0:T(8,128)(2,1)S(1)} %bitcast.12, bf16[7168,256]{1,0:T(8,128)(2,1)S(1)} %bitcast.14, ...), custom_call_target="tpu_custom_call" | custom-call | tf_op jit(solution)/shard_map/gate_up_own/pallas_call | solution.py:27
  86.0 1.7 %collective-permute-done.3.other = bf16[16,256,256]{2,1,0:T(8,128)(2,1)S(1)} collective-permute-done((bf16[16,256,256]{2,1,0:T(8,128)(2,1)S(1)}, bf16[16,256,256]{2,1,0:T(8,128)(2,1)S(1)}, u32[]{:S(2)}, u32[]{:S(2)}) %collective-permute-start.3) | collective-permute-done | bytes 2097184 | tf_op jit(solution)/shard_map/ppermute | solution.py:18
  87.7 2.5 %gate_up_both.1 = (bf16[256,256]{1,0:T(8,128)(2,1)S(1)}, f32[32,2,256]{2,1,0:T(2,128)S(1)}) custom-call(f32[256,256]{1,0:T(8,128)S(1)} %get-tuple-element.25.gate, f32[256,256]{1,0:T(8,128)S(1)} %get-tuple-element.26.up, f32[256,16]{1,0:T(8,128)S(1)} %get-tuple-element.27.logits, f32[256,128]{1,0:T(8,128)S(1)} %get-tuple-element.28.squares, ...), custom_call_target="tpu_custom_call" | custom-call | tf_op jit(solution)/shard_map/gate_up_both/pallas_call | solution.py:27
  90.2 0.5 collective-permute-start.4
  90.6 1.0 collective-permute-done.4.act_other
  91.6 1.2 down.1
  92.8 29.4 %all_to_all.23.pieces = bf16[64,4,3584]{2,1,0:T(4,128)(2,1)S(1)} all-to-all(bf16[64,4,3584]{2,1,0:T(4,128)(2,1)S(1)} %down.1), channel_id=1, replica_groups=mesh['req'=16,'seq'=2,'exp'=4] {'exp','req'}, dimensions={0} | all-to-all | bytes 3670016 | tf_op jit(solution)/shard_map/all_to_all | solution.py:474
  122.2 0.9 routed.1
  123.1 2.8 %collective-permute-start.5 = (f32[2,3584]{1,0:T(2,128)S(1)}, f32[2,3584]{1,0:T(2,128)S(1)}, u32[]{:S(2)}, u32[]{:S(2)}) collective-permute-start(f32[2,3584]{1,0:T(2,128)S(1)} %get-tuple-element.31), channel_id=1, source_target_pairs={{0,4},{4,0},{1,5},{5,1},{2,6},{6,2},{3,7},{7,3},{8,12},{12,8},{9,1... | collective-permute-start | bytes 86024 | tf_op jit(solution)/shard_map/ppermute | solution.py:18
  125.9 0.9 collective-permute-done.5.theirs
  126.8 0.8 finish.1
  (21 shorter events, 0.4 us)
Async XLA Ops:
  0.0 35.8 %collective-permute-start.1 = (bf16[256,7168]{1,0:T(8,128)(2,1)}, bf16[256,7168]{1,0:T(8,128)(2,1)S(1)}, u32[]{:S(2)}, u32[]{:S(2)}) collective-permute-start(bf16[256,7168]{1,0:T(8,128)(2,1)} %bitcast.18), channel_id=1, source_target_pairs={{0,4},{4,0},{1,5},{5,1},{2,6},{6,2},{3,7},{7,3},{8,12},{12,8},{9,1... | collective-permute-start | bytes 11010056 | tf_op jit(solution)/shard_map/ppermute | solution.py:18
  2.0 0.7 copy-start.7
  2.7 5.4 %copy-start.5 = (bf16[2,7168]{1,0:T(2,128)(2,1)S(1)}, bf16[2,7168]{1,0:T(2,128)(2,1)}, u32[]{:S(2)}) copy-start(bf16[2,7168]{1,0:T(2,128)(2,1)} %residual.1) | copy-start | bytes 86020
  2.7 5.4 %copy-start.6 = (s32[2,8]{1,0:T(2,128)S(1)}, s32[2,8]{1,0:T(2,128)}, u32[]{:S(2)}) copy-start(s32[2,8]{1,0:T(2,128)} %expert_ids.1) | copy-start | bytes 196
  5.7 2.4 %collective-permute-start = (bf16[256,640]{1,0:T(8,128)(2,1)S(1)}, bf16[256,640]{1,0:T(8,128)(2,1)S(1)}, u32[]{:S(2)}, u32[]{:S(2)}) collective-permute-start(bf16[256,640]{1,0:T(8,128)(2,1)S(1)} %get-tuple-element.21), channel_id=1, source_target_pairs={{0,4},{4,0},{1,5},{5,1},{2,6},{6,2},{3,7},{7,3},{8,12},{12,8},{9,1... | collective-permute-start | bytes 983048 | tf_op jit(solution)/shard_map/ppermute | solution.py:18
  9.2 26.6 %copy-start.2 = (bf16[4096,224]{0,1:T(8,128)(2,1)S(1)}, bf16[4096,224]{0,1:T(8,128)(2,1)}, u32[]{:S(2)}) copy-start(bf16[4096,224]{0,1:T(8,128)(2,1)} %param.19) | copy-start | bytes 5505028
  34.1 4.0 %collective-permute-start.2 = (bf16[16,17,16,128]{3,2,1,0:T(8,128)(2,1)S(1)}, bf16[16,17,16,128]{3,2,1,0:T(8,128)(2,1)S(1)}, u32[]{:S(2)}, u32[]{:S(2)}) collective-permute-start(bf16[16,17,16,128]{3,2,1,0:T(8,128)(2,1)S(1)} %all_to_all.20.gathered), channel_id=1, source_target_pairs={{0,4},{4,0},{1,5},{5,1},{2,6},{6,2},{3,7},{7,3},{8,12},{12,8},{9,1... | collective-permute-start | bytes 3342344 | tf_op jit(solution)/shard_map/ppermute | solution.py:18
  38.2 45.8 %copy-start.1 = (bf16[1,7168,256]{2,1,0:T(8,128)(2,1)S(1)}, bf16[1,7168,256]{2,1,0:T(8,128)(2,1)}, u32[]{:S(2)}) copy-start(bf16[1,7168,256]{2,1,0:T(8,128)(2,1)} %param.24) | copy-start | bytes 11010052
  48.0 35.9 %copy-start.8 = (bf16[7168]{0:T(1024)(128)(2,1)S(1)}, bf16[7168]{0:T(1024)(128)(2,1)}, u32[]{:S(2)}) copy-start(bf16[7168]{0:T(1024)(128)(2,1)} %param.20) | copy-start | bytes 43012
  48.0 35.9 %copy-start = (bf16[1,7168,256]{2,1,0:T(8,128)(2,1)S(1)}, bf16[1,7168,256]{2,1,0:T(8,128)(2,1)}, u32[]{:S(2)}) copy-start(bf16[1,7168,256]{2,1,0:T(8,128)(2,1)} %param.23) | copy-start | bytes 11010052
  48.0 35.9 %copy-start.4 = (bf16[7168,16]{0,1:T(8,128)(2,1)S(1)}, bf16[7168,16]{0,1:T(8,128)(2,1)}, u32[]{:S(2)}) copy-start(bf16[7168,16]{0,1:T(8,128)(2,1)} %param.21) | copy-start | bytes 688132
  80.1 7.6 %collective-permute-start.3 = (bf16[16,256,256]{2,1,0:T(8,128)(2,1)S(1)}, bf16[16,256,256]{2,1,0:T(8,128)(2,1)S(1)}, u32[]{:S(2)}, u32[]{:S(2)}) collective-permute-start(bf16[16,256,256]{2,1,0:T(8,128)(2,1)S(1)} %bitcast.9), channel_id=1, source_target_pairs={{0,4},{4,0},{1,5},{5,1},{2,6},{6,2},{3,7},{7,3},{8,12},{12,8},{9,1... | collective-permute-start | bytes 6291464 | tf_op jit(solution)/shard_map/ppermute | solution.py:18
  87.7 3.9 %copy-start.3 = (bf16[1,256,7168]{2,1,0:T(8,128)(2,1)S(1)}, bf16[1,256,7168]{2,1,0:T(8,128)(2,1)}, u32[]{:S(2)}) copy-start(bf16[1,256,7168]{2,1,0:T(8,128)(2,1)} %param.25) | copy-start | bytes 11010052
  90.2 1.5 %collective-permute-start.4 = (bf16[256,256]{1,0:T(8,128)(2,1)S(1)}, bf16[256,256]{1,0:T(8,128)(2,1)S(1)}, u32[]{:S(2)}, u32[]{:S(2)}) collective-permute-start(bf16[256,256]{1,0:T(8,128)(2,1)S(1)} %get-tuple-element.29.act), channel_id=1, source_target_pairs={{0,4},{4,0},{1,5},{5,1},{2,6},{6,2},{3,7},{7,3},{8,12},{12,8},{9,1... | collective-permute-start | bytes 393224 | tf_op jit(solution)/shard_map/ppermute | solution.py:18
  123.1 3.6 %collective-permute-start.5 = (f32[2,3584]{1,0:T(2,128)S(1)}, f32[2,3584]{1,0:T(2,128)S(1)}, u32[]{:S(2)}, u32[]{:S(2)}) collective-permute-start(f32[2,3584]{1,0:T(2,128)S(1)} %get-tuple-element.31), channel_id=1, source_target_pairs={{0,4},{4,0},{1,5},{5,1},{2,6},{6,2},{3,7},{7,3},{8,12},{12,8},{9,1... | collective-permute-start | bytes 86024 | tf_op jit(solution)/shard_map/ppermute | solution.py:18

commit v6 on v5

--- a/solution.py
+++ b/solution.py
@@ -4,6 +4,7 @@
 from jax.experimental import pallas as pl
 from jax.experimental.pallas import tpu as pltpu
 from jax.sharding import PartitionSpec as P
+
 
 DL = 512
 DR = 64
@@ -22,7 +23,7 @@
     return pl.BlockSpec(memory_space=pltpu.VMEM)
 
 
-def call(kernel, name, out_shape, *operands, scalars=(), outside=(), scratch=(), limit=24):
+def call(kernel, out_shape, *operands, scalars=(), outside=(), scratch=(), limit=24):
     many = isinstance(out_shape, (tuple, list))
     return pl.pallas_call(
         kernel,
@@ -33,7 +34,6 @@
         out_specs=[vmem() for _ in out_shape] if many else vmem(),
         scratch_shapes=list(scratch),
         compiler_params=pltpu.CompilerParams(vmem_limit_bytes=limit * 2**20),
-        name=name,
     )(*scalars, *[pltpu.with_memory_space_constraint(a, pltpu.HBM) for a in outside], *operands)
 
 
@@ -189,18 +189,42 @@
     return total
 
 
-def project_own_kernel(gathered, out_proj_t, swapped, out):
+def residual_rows(gathered, column_side, tiles):
+    reqs, slabs, drafts, lanes = gathered.shape
+    beside = gathered[:, slabs - 1].reshape(reqs * drafts, lanes)
+    picked = []
+    for tile in range(tiles):
+
+        def source(i):
+            return i // 2 * drafts + (i % 2 * 2 + column_side) * tiles + tile
+
+        order = one_hot((reqs * 2, reqs * drafts), source)
+        picked.append(jnp.dot(order, beside, preferred_element_type=F32))
+    return jnp.concatenate(picked, -1).astype(BF16)
+
+
+def project_other_kernel(gathered, other_t, swapped, out):
+    tokens = gathered.shape[0] * gathered.shape[2]
+    side = lax.axis_index("seq")
+    width, padded = other_t.shape[0], out.shape[1]
+    total = project_terms(gathered, other_t, side)
+    total = jnp.concatenate([total, jnp.zeros((tokens, padded - width), F32)], -1)
+    out[:tokens] = total.astype(BF16)
+    out[tokens:] = residual_rows(gathered, 1 - side, padded // gathered.shape[3])
+
+
+def project_own_kernel(gathered, out_proj_t, out):
     out[...] = project_terms(gathered, out_proj_t, lax.axis_index("seq"))
 
 
-def project_both_kernel(started, gathered, gathered_other, out_proj_t, terms, residual):
-    reqs, slabs, drafts, lanes = gathered.shape
+def project_sum_kernel(started, arrived, gathered, terms, residual):
+    reqs, _, drafts, lanes = gathered.shape
     exps, _, padded = terms.shape
     width = started.shape[1]
     side = lax.axis_index("seq")
-    total = (started[...] + project_terms(gathered_other, out_proj_t, 1 - side)).astype(BF16)
     tokens = reqs * drafts
     own_rows = drafts // (2 * exps)
+    total = (started[...] + arrived[:tokens, :width].astype(F32)).astype(BF16)
 
     def source(i):
         exp, req = i // (tokens // exps), i // (2 * own_rows) % reqs
@@ -210,22 +234,19 @@
     total = jnp.dot(one_hot((tokens, tokens), source), total, preferred_element_type=F32)
     total = jnp.concatenate([total, jnp.zeros((tokens, padded - width), F32)], -1)
     terms[...] = total.astype(BF16).reshape(terms.shape)
-    tiles = padded // lanes
-    for tile in range(tiles):
-        picked = jnp.zeros((tokens // exps, lanes), F32)
-        for rows, from_side in ((gathered, side), (gathered_other, 1 - side)):
-
-            def residual_source(i):
-                req, seq, row = i // (2 * own_rows), i // own_rows % 2, i % own_rows
-                place = req * drafts + (row * 2 + side) * tiles + tile
-                return jnp.where(seq == from_side, place, -1)
-
-            picked += jnp.dot(
-                one_hot((tokens // exps, tokens), residual_source),
-                rows[:, slabs - 1].reshape(tokens, lanes),
-                preferred_element_type=F32,
-            )
-        residual[:, tile * lanes : (tile + 1) * lanes] = picked.astype(BF16)
+    picked = jnp.zeros(residual.shape, F32)
+    for rows, from_side in (
+        (residual_rows(gathered, side, padded // lanes), side),
+        (arrived[tokens:], 1 - side),
+    ):
+
+        def residual_source(i):
+            req, seq, row = i // (2 * own_rows), i // own_rows % 2, i % own_rows
+            return jnp.where(seq == from_side, req * own_rows + row, -1)
+
+        order = one_hot((residual.shape[0], rows.shape[0]), residual_source)
+        picked += jnp.dot(order, rows, preferred_element_type=F32)
+    residual[...] = picked.astype(BF16)
 
 
 def hidden_kernel(terms, residual, fanned):
@@ -271,7 +292,8 @@
 
 
 def gate_up_both_kernel(
-    gate, up, logits, squares, own, other, gains, w_gate, w_up, router_t, act, rows_here
+    gate, up, logits, squares, own, other, gains, w_gate, w_up, router_t,
+    act_mine, act_theirs, rows_here,
 ):
     side = lax.axis_index("seq")
     own_rows = rows_here.shape[1]
@@ -297,45 +319,37 @@
     mine = lax.broadcasted_iota(jnp.int32, chosen.shape, 1) == lax.axis_index("req")
     weight = jnp.sum(jnp.where(mine, chosen, 0.0), -1, keepdims=True)
     weight = weight / jnp.sum(chosen, -1, keepdims=True) * 2.5
-    act[...] = (
-        jax.nn.silu((gate[...] + a) * scale) * ((up[...] + b) * scale) * weight
-    ).astype(BF16)
-
-
-DOWN_STEPS = 7
+    act = (jax.nn.silu((gate[...] + a) * scale) * ((up[...] + b) * scale) * weight).astype(BF16)
+    tokens = act.shape[0]
+    reqs = own.shape[0]
+    for out, seq in ((act_mine, side), (act_theirs, 1 - side)):
+
+        def source(i):
+            exp, req, row = i // (reqs * own_rows), i // own_rows % reqs, i % own_rows
+            return ((exp * reqs + req) * 2 + seq) * own_rows + row
+
+        order = one_hot((tokens // 2, tokens), source)
+        out[...] = jnp.dot(order, act, preferred_element_type=F32).astype(BF16)
+
+
+DOWN_STEPS = 14
 
 
 def down_kernel(act, act_other, w_down, w_down_other, out):
-    half = out.shape[2]
-    block = half // DOWN_STEPS
+    block = out.shape[2] // DOWN_STEPS
     for i in range(DOWN_STEPS):
-        columns = pl.ds(pl.multiple_of(lax.axis_index("seq") * half + i * block, 128), block)
+        columns = slice(i * block, (i + 1) * block)
         total = jnp.dot(act[...], w_down[:, columns], preferred_element_type=F32)
         total += jnp.dot(act_other[...], w_down_other[:, columns], preferred_element_type=F32)
-        out[:, :, i * block : (i + 1) * block] = total.reshape(out.shape[:2] + (block,)).astype(BF16)
-
-
-def routed_kernel(pieces, mine, theirs):
-    rows = mine.shape[0]
+        out[:, :, columns] = total.reshape(out.shape[:2] + (block,)).astype(BF16)
+
+
+def finish_kernel(pieces, rows_here, out):
+    blocks, rows = rows_here.shape[0], out.shape[0]
+    width = out.shape[1] // blocks
     total = jnp.sum(pieces[...].astype(F32), 0)
-    side = lax.axis_index("seq")
-    low, high = total[:rows], total[rows:]
-    mine[...] = jnp.where(side == 0, low, high)
-    theirs[...] = jnp.where(side == 0, high, low)
-
-
-def finish_kernel(mine, theirs, rows_here, out):
-    blocks, rows, half = rows_here.shape[0], mine.shape[0], mine.shape[1]
-    width = 2 * half // blocks
-    for side, first, second in ((0, mine, theirs), (1, theirs, mine)):
-
-        @pl.when(lax.axis_index("seq") == side)
-        def _():
-            for block in range(blocks):
-                start = block * width
-                source, offset = (first, start) if start < half else (second, start - half)
-                total = rows_here[block, :rows, :width] + source[:, offset : offset + width]
-                out[:, start : start + width] = total.astype(BF16)
+    hidden = jnp.concatenate([rows_here[block, :rows, :width] for block in range(blocks)], -1)
+    out[...] = (hidden + total).astype(BF16)
 
 
 def per_device(
@@ -363,7 +377,6 @@
     tokens = n_req * drafts
     half_heads = heads // 2
     half_rows = drafts * half_heads
-    half = model_width // 2
     shape = jax.ShapeDtypeStruct
     w_gate, w_up, w_down = w_gate[0], w_up[0], w_down[0]
     hidden_units = w_gate.shape[1]
@@ -371,7 +384,6 @@
 
     sent, kept, kept_stats, value_half = call(
         attend_kernel,
-        "attend",
         (
             shape((half_rows, DL + 128), BF16),
             shape((half_rows, DL), F32),
@@ -387,10 +399,10 @@
         ),
     )
     arrived = swap(sent)
+    other_t = swap(out_proj_t)
     w_down_other = swap(w_down)
     fanned = call(
         values_kernel,
-        "values",
         shape((n_req, half_heads + 1, drafts, DV), BF16),
         kept,
         kept_stats,
@@ -400,41 +412,35 @@
         expert_ids,
     )
     gathered = lax.all_to_all(fanned, "req", split_axis=0, concat_axis=0, tiled=True)
-    gathered_other = swap(gathered)
-    started = call(
-        project_own_kernel,
-        "project_own",
-        shape((tokens, width), F32),
-        gathered,
-        out_proj_t,
-        w_down_other,
-    )
+    arrived = swap(
+        call(
+            project_other_kernel,
+            shape((tokens + n_req * own_rows, padded), BF16),
+            gathered,
+            other_t,
+            w_down_other,
+        )
+    )
+    started = call(project_own_kernel, shape((tokens, width), F32), gathered, out_proj_t)
     terms, resid = call(
-        project_both_kernel,
-        "project_both",
+        project_sum_kernel,
         (
             shape((n_exp, tokens // n_exp, padded), BF16),
             shape((tokens // n_exp, padded), BF16),
         ),
         started,
+        arrived,
         gathered,
-        gathered_other,
-        out_proj_t,
     )
     terms = lax.all_to_all(terms, "exp", split_axis=0, concat_axis=0, tiled=True)
     fanned = call(
-        hidden_kernel,
-        "hidden",
-        shape((n_req * n_exp, tokens // n_exp, padded), BF16),
-        terms,
-        resid,
+        hidden_kernel, shape((n_req * n_exp, tokens // n_exp, padded), BF16), terms, resid
     )
     own = lax.all_to_all(fanned, ("req", "exp"), split_axis=0, concat_axis=0, tiled=True)
     own = own.reshape(n_req, tokens, padded)
     other = swap(own)
     started = call(
         gate_up_own_kernel,
-        "gate_up_own",
         (
             shape((tokens, hidden_units), F32),
             shape((tokens, hidden_units), F32),
@@ -447,11 +453,11 @@
         w_up,
         router_t,
     )
-    act, rows_here = call(
+    act_mine, act_theirs, rows_here = call(
         gate_up_both_kernel,
-        "gate_up_both",
         (
-            shape((tokens, hidden_units), BF16),
+            shape((tokens // 2, hidden_units), BF16),
+            shape((tokens // 2, hidden_units), BF16),
             shape((n_req * 2, own_rows, padded), F32),
         ),
         *started,
@@ -464,28 +470,14 @@
     )
     pieces = call(
         down_kernel,
-        "down",
-        shape((tokens // 4, 4, half), BF16),
-        act,
-        swap(act),
+        shape((n_req * n_exp, own_rows, model_width), BF16),
+        act_mine,
+        swap(act_theirs),
         w_down,
         w_down_other,
     )
     pieces = lax.all_to_all(pieces, ("exp", "req"), split_axis=0, concat_axis=0, tiled=True)
-    mine, theirs = call(
-        routed_kernel,
-        "routed",
-        (shape((own_rows, half), F32), shape((own_rows, half), F32)),
-        pieces,
-    )
-    return call(
-        finish_kernel,
-        "finish",
-        shape((own_rows, model_width), BF16),
-        mine,
-        swap(theirs),
-        rows_here,
-    )
+    return call(finish_kernel, shape((own_rows, model_width), BF16), pieces, rows_here)
 
 
 def solution(mesh):
@@ -505,6 +497,5 @@
         P("req", ("seq", "exp"), None),
     )
     out_specs = P(("req", "seq", "exp"), None)
-    return jax.shard_map(
-        per_device, mesh=mesh, in_specs=in_specs, out_specs=out_specs, check_vma=False
-    )
+
+    return jax.shard_map(per_device, mesh=mesh, in_specs=in_specs, out_specs=out_specs, check_vma=False)

time: 128 us -> 129 us (level)
  Pallas kernels: 13 us -> 15.3 us
  starting transfers between devices: 10.2 us -> 7.94 us
    pallas_call x10, Pallas kernels: 13 us -> 15.3 us  [call(): pl.pallas_call(kernel, out_shape=out_shape, in_specs=[pl.BlockSpec(memory...]
    ppermute x6, starting transfers between devices: 10.2 us -> 7.94 us  [swap(): return lax.ppermute(x, 'seq', SWAP)]
  transfers between devices with their start and end apart: 6 -> 6, of which waited for: 5 -> 4; matrix products, arithmetic and copies ran while one was open for 0% -> 0% of each run, Pallas kernels for 5% -> 5%
where the time goes in v6:
time: 129 us; the launch traced here: 128 us
  blocking collectives  95.4 us (74%)
  Pallas kernels  15.3 us (12%)
  starting transfers between devices  7.94 us (6%)
  waiting for transfers between devices  7.53 us (6%)
    all_to_all x1, blocking collectives, per_device(): lax.all_to_all(fanned, ('req', 'exp'), split_axis=0, concat_axis=0, tiled...  32.1 us
    all_to_all x1, blocking collectives, per_device(): lax.all_to_all(pieces, ('exp', 'req'), split_axis=0, concat_axis=0, tiled...  29.6 us
    all_to_all x1, blocking collectives, per_device(): lax.all_to_all(fanned, 'req', split_axis=0, concat_axis=0, tiled=True)  24.8 us
    pallas_call x10, Pallas kernels, call(): pl.pallas_call(kernel, out_shape=out_shape, in_specs=[pl.BlockSpec(memory...  15.3 us
    all_to_all x1, blocking collectives, per_device(): lax.all_to_all(terms, 'exp', split_axis=0, concat_axis=0, tiled=True)  8.91 us
    ppermute x6, starting transfers between devices, swap(): return lax.ppermute(x, 'seq', SWAP)  7.94 us
    ppermute x6, waiting for transfers between devices, swap(): return lax.ppermute(x, 'seq', SWAP)  7.53 us
  transfers between devices with their start and end apart: 6, of which 4 were waited for; matrix products, arithmetic and copies ran while one was open for 0% of the time, Pallas kernels for 5%

profile of v6, /device:TPU:1, one launch (start us, length us, event | category | flops | bytes accessed | tf_op | source)
XLA Modules:
  0.0 127.7 jit_solution(3711561278401465714)
XLA Ops:
  0.0 1.4 %collective-permute-start.2 = (bf16[256,7168]{1,0:T(8,128)(2,1)}, bf16[256,7168]{1,0:T(8,128)(2,1)S(1)}, u32[]{:S(2)}, u32[]{:S(2)}) collective-permute-start(bf16[256,7168]{1,0:T(8,128)(2,1)} %bitcast.16), channel_id=1, source_target_pairs={{0,4},{4,0},{1,5},{5,1},{2,6},{6,2},{3,7},{7,3},{8,12},{12,8},{9,1... | collective-permute-start | bytes 11010056 | tf_op jit(solution)/shard_map/ppermute | solution.py:19
  2.0 0.6 copy-done.7
  2.7 3.0 %shard_map.127 = (bf16[256,640]{1,0:T(8,128)(2,1)S(1)}, f32[256,512]{1,0:T(8,128)S(1)}, f32[256,256]{1,0:T(8,128)S(1)}, bf16[16,512,128]{2,1,0:T(8,128)(2,1)S(1)}) custom-call(s32[1]{0:T(128)S(6)} %copy.14.lengths, s32[2]{0:T(128)S(1)} %bitcast.22, bf16[16,32,576]{2,1,0:T(8,128)(2,1)} %bitcast.23, bf16[192,576]{1,0:T(8,128)(2,1)} %bitcast.24, ...), custom_call_target="tpu_custom_call" | custom-call | tf_op jit(solution)/shard_map/pallas_call | solution.py:28
  5.7 0.6 collective-permute-start
  6.3 4.4 %collective-permute-done.arrived = bf16[256,640]{1,0:T(8,128)(2,1)S(1)} collective-permute-done((bf16[256,640]{1,0:T(8,128)(2,1)S(1)}, bf16[256,640]{1,0:T(8,128)(2,1)S(1)}, u32[]{:S(2)}, u32[]{:S(2)}) %collective-permute-start) | collective-permute-done | bytes 327712 | tf_op jit(solution)/shard_map/ppermute | solution.py:19
  10.7 1.1 shard_map.128
  11.8 24.8 %all_to_all.20.gathered = bf16[16,17,16,128]{3,2,1,0:T(8,128)(2,1)S(1)} all-to-all(bf16[16,17,16,128]{3,2,1,0:T(8,128)(2,1)S(1)} %shard_map.128), channel_id=1, replica_groups=mesh['req'=16,'seq'=2,'exp'=4] {'req'}, dimensions={0} | all-to-all | bytes 2228224 | tf_op jit(solution)/shard_map/all_to_all | solution.py:414
  36.6 0.5 shard_map.130
  37.1 1.7 %collective-permute-start.3 = (bf16[288,256]{1,0:T(8,128)(2,1)S(1)}, bf16[288,256]{1,0:T(8,128)(2,1)S(1)}, u32[]{:S(2)}, u32[]{:S(2)}) collective-permute-start(bf16[288,256]{1,0:T(8,128)(2,1)S(1)} %shard_map.130), channel_id=1, source_target_pairs={{0,4},{4,0},{1,5},{5,1},{2,6},{6,2},{3,7},{7,3},{8,12},{12,8},{9,1... | collective-permute-start | bytes 442376 | tf_op jit(solution)/shard_map/ppermute | solution.py:19
  38.8 0.5 shard_map.129.started
  39.3 0.5 collective-permute-done.3.arrived
  39.9 0.3 shard_map.131
  40.1 8.9 %all_to_all.21.terms = bf16[4,64,256]{2,1,0:T(8,128)(2,1)S(1)} all-to-all(bf16[4,64,256]{2,1,0:T(8,128)(2,1)S(1)} %get-tuple-element.22), channel_id=1, replica_groups=mesh['req'=16,'seq'=2,'exp'=4] {'exp'}, dimensions={0} | all-to-all | bytes 262144 | tf_op jit(solution)/shard_map/all_to_all | solution.py:435
  49.0 0.3 shard_map.132
  49.3 32.1 %all_to_all.22 = bf16[64,64,256]{2,1,0:T(8,128)(2,1)S(1)} all-to-all(bf16[64,64,256]{2,1,0:T(8,128)(2,1)S(1)} %shard_map.132), channel_id=1, replica_groups=mesh['req'=16,'seq'=2,'exp'=4] {'req','exp'}, dimensions={0} | all-to-all | bytes 4194304 | tf_op jit(solution)/shard_map/all_to_all | solution.py:439
  81.5 3.8 %collective-permute-start.4 = (bf16[16,256,256]{2,1,0:T(8,128)(2,1)S(1)}, bf16[16,256,256]{2,1,0:T(8,128)(2,1)S(1)}, u32[]{:S(2)}, u32[]{:S(2)}) collective-permute-start(bf16[16,256,256]{2,1,0:T(8,128)(2,1)S(1)} %bitcast.9), channel_id=1, source_target_pairs={{0,4},{4,0},{1,5},{5,1},{2,6},{6,2},{3,7},{7,3},{8,12},{12,8},{9,1... | collective-permute-start | bytes 6291464 | tf_op jit(solution)/shard_map/ppermute | solution.py:19
  85.3 2.0 %shard_map.133 = (f32[256,256]{1,0:T(8,128)S(1)}, f32[256,256]{1,0:T(8,128)S(1)}, f32[256,16]{1,0:T(8,128)S(1)}, f32[256,128]{1,0:T(8,128)S(1)}) custom-call(bf16[16,256,256]{2,1,0:T(8,128)(2,1)S(1)} %bitcast.10, bf16[1,7168]{1,0:T(2,128)(2,1)S(1)} %reshape.11.gains, bf16[7168,256]{1,0:T(8,128)(2,1)S(1)} %bitcast.12, bf16[7168,256]{1,0:T(8,128)(2,1)S(1)} %bitcast.14, ...), custom_call_target="tpu_custom_call" | custom-call | tf_op jit(solution)/shard_map/pallas_call | solution.py:28
  87.3 1.7 %collective-permute-done.4.other = bf16[16,256,256]{2,1,0:T(8,128)(2,1)S(1)} collective-permute-done((bf16[16,256,256]{2,1,0:T(8,128)(2,1)S(1)}, bf16[16,256,256]{2,1,0:T(8,128)(2,1)S(1)}, u32[]{:S(2)}, u32[]{:S(2)}) %collective-permute-start.4) | collective-permute-done | bytes 2097184 | tf_op jit(solution)/shard_map/ppermute | solution.py:19
  89.0 2.6 %shard_map.134 = (bf16[128,256]{1,0:T(8,128)(2,1)S(1)}, bf16[128,256]{1,0:T(8,128)(2,1)S(1)}, f32[32,2,256]{2,1,0:T(2,128)S(1)}) custom-call(f32[256,256]{1,0:T(8,128)S(1)} %get-tuple-element.24.gate, f32[256,256]{1,0:T(8,128)S(1)} %get-tuple-element.25.up, f32[256,16]{1,0:T(8,128)S(1)} %get-tuple-element.26.logits, ...), custom_call_target="tpu_custom_call" | custom-call | tf_op jit(solution)/shard_map/pallas_call | solution.py:28
  91.6 0.5 collective-permute-start.5
  92.1 0.9 collective-permute-done.5.act_other
  93.0 2.6 %shard_map.135 = bf16[64,2,7168]{2,1,0:T(2,128)(2,1)S(1)} custom-call(bf16[128,256]{1,0:T(8,128)(2,1)S(1)} %get-tuple-element.28.act, bf16[128,256]{1,0:T(8,128)(2,1)S(1)} %collective-permute-done.5.act_other, bf16[256,7168]{1,0:T(8,128)(2,1)S(1)} %bitcast.17, bf16[256,7168]{1,0:T(8,128)(2,1)S(1)} %collective-permute-done.2.swapped.w_down_other), custom_call_target="tpu_custom_call" | custom-call | tf_op jit(solution)/shard_map/pallas_call | solution.py:28
  95.6 29.6 %all_to_all.23.pieces = bf16[64,2,7168]{2,1,0:T(2,128)(2,1)S(1)} all-to-all(bf16[64,2,7168]{2,1,0:T(2,128)(2,1)S(1)} %shard_map.135), channel_id=1, replica_groups=mesh['req'=16,'seq'=2,'exp'=4] {'exp','req'}, dimensions={0} | all-to-all | bytes 3670016 | tf_op jit(solution)/shard_map/all_to_all | solution.py:479
  125.2 2.5 %shard_map.136 = bf16[2,7168]{1,0:T(2,128)(2,1)} custom-call(bf16[64,2,7168]{2,1,0:T(2,128)(2,1)S(1)} %all_to_all.23.pieces, f32[32,2,256]{2,1,0:T(2,128)S(1)} %get-tuple-element.30.rows_here), custom_call_target="tpu_custom_call" | custom-call | tf_op jit(solution)/shard_map/pallas_call | solution.py:28
  (21 shorter events, 0.1 us)
Async XLA Ops:
  0.0 36.6 %collective-permute-start.2 = (bf16[256,7168]{1,0:T(8,128)(2,1)}, bf16[256,7168]{1,0:T(8,128)(2,1)S(1)}, u32[]{:S(2)}, u32[]{:S(2)}) collective-permute-start(bf16[256,7168]{1,0:T(8,128)(2,1)} %bitcast.16), channel_id=1, source_target_pairs={{0,4},{4,0},{1,5},{5,1},{2,6},{6,2},{3,7},{7,3},{8,12},{12,8},{9,1... | collective-permute-start | bytes 11010056 | tf_op jit(solution)/shard_map/ppermute | solution.py:19
  1.4 35.2 %collective-permute-start.1 = (bf16[224,4096]{1,0:T(8,128)(2,1)}, bf16[224,4096]{1,0:T(8,128)(2,1)S(1)}, u32[]{:S(2)}, u32[]{:S(2)}) collective-permute-start(bf16[224,4096]{1,0:T(8,128)(2,1)} %bitcast.18), channel_id=1, source_target_pairs={{0,4},{4,0},{1,5},{5,1},{2,6},{6,2},{3,7},{7,3},{8,12},{12,8},{9,1... | collective-permute-start | bytes 5505032 | tf_op jit(solution)/shard_map/ppermute | solution.py:19
  2.0 0.7 copy-start.7
  2.7 8.0 %copy-start.5 = (bf16[2,7168]{1,0:T(2,128)(2,1)S(1)}, bf16[2,7168]{1,0:T(2,128)(2,1)}, u32[]{:S(2)}) copy-start(bf16[2,7168]{1,0:T(2,128)(2,1)} %residual.1) | copy-start | bytes 86020
  2.7 8.0 %copy-start.6 = (s32[2,8]{1,0:T(2,128)S(1)}, s32[2,8]{1,0:T(2,128)}, u32[]{:S(2)}) copy-start(s32[2,8]{1,0:T(2,128)} %expert_ids.1) | copy-start | bytes 196
  5.7 5.0 %collective-permute-start = (bf16[256,640]{1,0:T(8,128)(2,1)S(1)}, bf16[256,640]{1,0:T(8,128)(2,1)S(1)}, u32[]{:S(2)}, u32[]{:S(2)}) collective-permute-start(bf16[256,640]{1,0:T(8,128)(2,1)S(1)} %get-tuple-element.20), channel_id=1, source_target_pairs={{0,4},{4,0},{1,5},{5,1},{2,6},{6,2},{3,7},{7,3},{8,12},{12,8},{9,1... | collective-permute-start | bytes 983048 | tf_op jit(solution)/shard_map/ppermute | solution.py:19
  36.6 2.3 %copy-start.3 = (bf16[4096,224]{0,1:T(8,128)(2,1)S(1)}, bf16[4096,224]{0,1:T(8,128)(2,1)}, u32[]{:S(2)}) copy-start(bf16[4096,224]{0,1:T(8,128)(2,1)} %param.19) | copy-start | bytes 5505028
  37.1 2.8 %collective-permute-start.3 = (bf16[288,256]{1,0:T(8,128)(2,1)S(1)}, bf16[288,256]{1,0:T(8,128)(2,1)S(1)}, u32[]{:S(2)}, u32[]{:S(2)}) collective-permute-start(bf16[288,256]{1,0:T(8,128)(2,1)S(1)} %shard_map.130), channel_id=1, source_target_pairs={{0,4},{4,0},{1,5},{5,1},{2,6},{6,2},{3,7},{7,3},{8,12},{12,8},{9,1... | collective-permute-start | bytes 442376 | tf_op jit(solution)/shard_map/ppermute | solution.py:19
  39.9 45.4 %copy-start.1 = (bf16[1,7168,256]{2,1,0:T(8,128)(2,1)S(1)}, bf16[1,7168,256]{2,1,0:T(8,128)(2,1)}, u32[]{:S(2)}) copy-start(bf16[1,7168,256]{2,1,0:T(8,128)(2,1)} %param.24) | copy-start | bytes 11010052
  49.3 35.9 %copy-start.8 = (bf16[7168]{0:T(1024)(128)(2,1)S(1)}, bf16[7168]{0:T(1024)(128)(2,1)}, u32[]{:S(2)}) copy-start(bf16[7168]{0:T(1024)(128)(2,1)} %param.20) | copy-start | bytes 43012
  49.3 35.9 %copy-start = (bf16[1,7168,256]{2,1,0:T(8,128)(2,1)S(1)}, bf16[1,7168,256]{2,1,0:T(8,128)(2,1)}, u32[]{:S(2)}) copy-start(bf16[1,7168,256]{2,1,0:T(8,128)(2,1)} %param.23) | copy-start | bytes 11010052
  49.3 35.9 %copy-start.4 = (bf16[7168,16]{0,1:T(8,128)(2,1)S(1)}, bf16[7168,16]{0,1:T(8,128)(2,1)}, u32[]{:S(2)}) copy-start(bf16[7168,16]{0,1:T(8,128)(2,1)} %param.21) | copy-start | bytes 688132
  81.5 7.5 %collective-permute-start.4 = (bf16[16,256,256]{2,1,0:T(8,128)(2,1)S(1)}, bf16[16,256,256]{2,1,0:T(8,128)(2,1)S(1)}, u32[]{:S(2)}, u32[]{:S(2)}) collective-permute-start(bf16[16,256,256]{2,1,0:T(8,128)(2,1)S(1)} %bitcast.9), channel_id=1, source_target_pairs={{0,4},{4,0},{1,5},{5,1},{2,6},{6,2},{3,7},{7,3},{8,12},{12,8},{9,1... | collective-permute-start | bytes 6291464 | tf_op jit(solution)/shard_map/ppermute | solution.py:19
  89.0 4.0 %copy-start.2 = (bf16[1,256,7168]{2,1,0:T(8,128)(2,1)S(1)}, bf16[1,256,7168]{2,1,0:T(8,128)(2,1)}, u32[]{:S(2)}) copy-start(bf16[1,256,7168]{2,1,0:T(8,128)(2,1)} %param.25) | copy-start | bytes 11010052
  91.6 1.4 %collective-permute-start.5 = (bf16[128,256]{1,0:T(8,128)(2,1)S(1)}, bf16[128,256]{1,0:T(8,128)(2,1)S(1)}, u32[]{:S(2)}, u32[]{:S(2)}) collective-permute-start(bf16[128,256]{1,0:T(8,128)(2,1)S(1)} %get-tuple-element.29), channel_id=1, source_target_pairs={{0,4},{4,0},{1,5},{5,1},{2,6},{6,2},{3,7},{7,3},{8,12},{12,8},{9,1... | collective-permute-start | bytes 196616 | tf_op jit(solution)/shard_map/ppermute | solution.py:19

commit v7 on v6

--- a/solution.py
+++ b/solution.py
@@ -321,34 +321,43 @@
     weight = weight / jnp.sum(chosen, -1, keepdims=True) * 2.5
     act = (jax.nn.silu((gate[...] + a) * scale) * ((up[...] + b) * scale) * weight).astype(BF16)
     tokens = act.shape[0]
-    reqs = own.shape[0]
     for out, seq in ((act_mine, side), (act_theirs, 1 - side)):
 
         def source(i):
-            exp, req, row = i // (reqs * own_rows), i // own_rows % reqs, i % own_rows
-            return ((exp * reqs + req) * 2 + seq) * own_rows + row
+            row, group = i // (tokens // (2 * own_rows)), i % (tokens // (2 * own_rows))
+            return (group * 2 + seq) * own_rows + row
 
         order = one_hot((tokens // 2, tokens), source)
         out[...] = jnp.dot(order, act, preferred_element_type=F32).astype(BF16)
 
 
-DOWN_STEPS = 14
-
-
-def down_kernel(act, act_other, w_down, w_down_other, out):
-    block = out.shape[2] // DOWN_STEPS
-    for i in range(DOWN_STEPS):
-        columns = slice(i * block, (i + 1) * block)
+CHUNKS = 8
+
+
+def down_kernel(act, act_other, w_down, w_down_other, out, rows_here):
+    groups, rows, block = out.shape
+    own_rows = rows // CHUNKS
+    for chunk in range(CHUNKS):
+        columns = slice(chunk * block, (chunk + 1) * block)
         total = jnp.dot(act[...], w_down[:, columns], preferred_element_type=F32)
         total += jnp.dot(act_other[...], w_down_other[:, columns], preferred_element_type=F32)
-        out[:, :, columns] = total.reshape(out.shape[:2] + (block,)).astype(BF16)
-
-
-def finish_kernel(pieces, rows_here, out):
-    blocks, rows = rows_here.shape[0], out.shape[0]
+        for row in range(own_rows):
+            for tile in range(block // 128):
+                rows_here[tile, pl.ds(chunk * own_rows + row, groups, stride=rows), :] = total[
+                    row * groups : (row + 1) * groups, tile * 128 : (tile + 1) * 128
+                ]
+    for tile in range(block // 128):
+        out[:, :, tile * 128 : (tile + 1) * 128] = (
+            rows_here[tile].reshape(groups, rows, 128).astype(BF16)
+        )
+
+
+def finish_kernel(pieces, hidden_rows, out):
+    blocks, rows = hidden_rows.shape[0], out.shape[0]
     width = out.shape[1] // blocks
     total = jnp.sum(pieces[...].astype(F32), 0)
-    hidden = jnp.concatenate([rows_here[block, :rows, :width] for block in range(blocks)], -1)
+    total = jnp.concatenate([total[i * rows : (i + 1) * rows] for i in range(CHUNKS)], -1)
+    hidden = jnp.concatenate([hidden_rows[block, :rows, :width] for block in range(blocks)], -1)
     out[...] = (hidden + total).astype(BF16)
 
 
@@ -470,11 +479,12 @@
     )
     pieces = call(
         down_kernel,
-        shape((n_req * n_exp, own_rows, model_width), BF16),
+        shape((n_req * n_exp, own_rows * CHUNKS, model_width // CHUNKS), BF16),
         act_mine,
         swap(act_theirs),
         w_down,
         w_down_other,
+        scratch=(pltpu.VMEM((model_width // CHUNKS // 128, n_req * n_exp * own_rows * CHUNKS, 128), F32),),
     )
     pieces = lax.all_to_all(pieces, ("exp", "req"), split_axis=0, concat_axis=0, tiled=True)
     return call(finish_kernel, shape((own_rows, model_width), BF16), pieces, rows_here)

time: 129 us -> 128 us (level)
  no operation moved by 1% of the time
where the time goes in v7:
time: 128 us; the launch traced here: 126 us
  blocking collectives  95.2 us (74%)
  Pallas kernels  14.2 us (11%)
  starting transfers between devices  7.93 us (6%)
  waiting for transfers between devices  7.51 us (6%)
    all_to_all x1, blocking collectives, per_device(): lax.all_to_all(fanned, ('req', 'exp'), split_axis=0, concat_axis=0, tiled...  32.1 us
    all_to_all x1, blocking collectives, per_device(): lax.all_to_all(pieces, ('exp', 'req'), split_axis=0, concat_axis=0, tiled...  29.4 us
    all_to_all x1, blocking collectives, per_device(): lax.all_to_all(fanned, 'req', split_axis=0, concat_axis=0, tiled=True)  24.8 us
    pallas_call x10, Pallas kernels, call(): pl.pallas_call(kernel, out_shape=out_shape, in_specs=[pl.BlockSpec(memory...  14.2 us
    all_to_all x1, blocking collectives, per_device(): lax.all_to_all(terms, 'exp', split_axis=0, concat_axis=0, tiled=True)  8.9 us
    ppermute x6, starting transfers between devices, swap(): return lax.ppermute(x, 'seq', SWAP)  7.93 us
    ppermute x6, waiting for transfers between devices, swap(): return lax.ppermute(x, 'seq', SWAP)  7.51 us
  transfers between devices with their start and end apart: 6, of which 4 were waited for; matrix products, arithmetic and copies ran while one was open for 0% of the time, Pallas kernels for 5%

profile of v7, /device:TPU:1, one launch (start us, length us, event | category | flops | bytes accessed | tf_op | source)
XLA Modules:
  0.0 126.4 jit_solution(17877488313453985739)
XLA Ops:
  0.0 1.4 %collective-permute-start.2 = (bf16[256,7168]{1,0:T(8,128)(2,1)}, bf16[256,7168]{1,0:T(8,128)(2,1)S(1)}, u32[]{:S(2)}, u32[]{:S(2)}) collective-permute-start(bf16[256,7168]{1,0:T(8,128)(2,1)} %bitcast.16), channel_id=1, source_target_pairs={{0,4},{4,0},{1,5},{5,1},{2,6},{6,2},{3,7},{7,3},{8,12},{12,8},{9,1... | collective-permute-start | bytes 11010056 | tf_op jit(solution)/shard_map/ppermute | solution.py:19
  2.0 0.6 copy-done.7
  2.7 3.0 %shard_map.127 = (bf16[256,640]{1,0:T(8,128)(2,1)S(1)}, f32[256,512]{1,0:T(8,128)S(1)}, f32[256,256]{1,0:T(8,128)S(1)}, bf16[16,512,128]{2,1,0:T(8,128)(2,1)S(1)}) custom-call(s32[1]{0:T(128)S(6)} %copy.14.lengths, s32[2]{0:T(128)S(1)} %bitcast.22, bf16[16,32,576]{2,1,0:T(8,128)(2,1)} %bitcast.23, bf16[192,576]{1,0:T(8,128)(2,1)} %bitcast.24, ...), custom_call_target="tpu_custom_call" | custom-call | tf_op jit(solution)/shard_map/pallas_call | solution.py:28
  5.7 0.6 collective-permute-start
  6.3 4.4 %collective-permute-done.arrived = bf16[256,640]{1,0:T(8,128)(2,1)S(1)} collective-permute-done((bf16[256,640]{1,0:T(8,128)(2,1)S(1)}, bf16[256,640]{1,0:T(8,128)(2,1)S(1)}, u32[]{:S(2)}, u32[]{:S(2)}) %collective-permute-start) | collective-permute-done | bytes 327712 | tf_op jit(solution)/shard_map/ppermute | solution.py:19
  10.7 1.1 shard_map.128
  11.8 24.8 %all_to_all.20.gathered = bf16[16,17,16,128]{3,2,1,0:T(8,128)(2,1)S(1)} all-to-all(bf16[16,17,16,128]{3,2,1,0:T(8,128)(2,1)S(1)} %shard_map.128), channel_id=1, replica_groups=mesh['req'=16,'seq'=2,'exp'=4] {'req'}, dimensions={0} | all-to-all | bytes 2228224 | tf_op jit(solution)/shard_map/all_to_all | solution.py:423
  36.6 0.5 shard_map.130
  37.1 1.7 %collective-permute-start.3 = (bf16[288,256]{1,0:T(8,128)(2,1)S(1)}, bf16[288,256]{1,0:T(8,128)(2,1)S(1)}, u32[]{:S(2)}, u32[]{:S(2)}) collective-permute-start(bf16[288,256]{1,0:T(8,128)(2,1)S(1)} %shard_map.130), channel_id=1, source_target_pairs={{0,4},{4,0},{1,5},{5,1},{2,6},{6,2},{3,7},{7,3},{8,12},{12,8},{9,1... | collective-permute-start | bytes 442376 | tf_op jit(solution)/shard_map/ppermute | solution.py:19
  38.8 0.5 shard_map.129.started
  39.3 0.5 collective-permute-done.3.arrived
  39.9 0.3 shard_map.131
  40.1 8.9 %all_to_all.21.terms = bf16[4,64,256]{2,1,0:T(8,128)(2,1)S(1)} all-to-all(bf16[4,64,256]{2,1,0:T(8,128)(2,1)S(1)} %get-tuple-element.22), channel_id=1, replica_groups=mesh['req'=16,'seq'=2,'exp'=4] {'exp'}, dimensions={0} | all-to-all | bytes 262144 | tf_op jit(solution)/shard_map/all_to_all | solution.py:444
  49.0 0.3 shard_map.132
  49.3 32.1 %all_to_all.22 = bf16[64,64,256]{2,1,0:T(8,128)(2,1)S(1)} all-to-all(bf16[64,64,256]{2,1,0:T(8,128)(2,1)S(1)} %shard_map.132), channel_id=1, replica_groups=mesh['req'=16,'seq'=2,'exp'=4] {'req','exp'}, dimensions={0} | all-to-all | bytes 4194304 | tf_op jit(solution)/shard_map/all_to_all | solution.py:448
  81.4 3.8 %collective-permute-start.4 = (bf16[16,256,256]{2,1,0:T(8,128)(2,1)S(1)}, bf16[16,256,256]{2,1,0:T(8,128)(2,1)S(1)}, u32[]{:S(2)}, u32[]{:S(2)}) collective-permute-start(bf16[16,256,256]{2,1,0:T(8,128)(2,1)S(1)} %bitcast.9), channel_id=1, source_target_pairs={{0,4},{4,0},{1,5},{5,1},{2,6},{6,2},{3,7},{7,3},{8,12},{12,8},{9,1... | collective-permute-start | bytes 6291464 | tf_op jit(solution)/shard_map/ppermute | solution.py:19
  85.3 2.1 %shard_map.133 = (f32[256,256]{1,0:T(8,128)S(1)}, f32[256,256]{1,0:T(8,128)S(1)}, f32[256,16]{1,0:T(8,128)S(1)}, f32[256,128]{1,0:T(8,128)S(1)}) custom-call(bf16[16,256,256]{2,1,0:T(8,128)(2,1)S(1)} %bitcast.10, bf16[1,7168]{1,0:T(2,128)(2,1)S(1)} %reshape.11.gains, bf16[7168,256]{1,0:T(8,128)(2,1)S(1)} %bitcast.12, bf16[7168,256]{1,0:T(8,128)(2,1)S(1)} %bitcast.14, ...), custom_call_target="tpu_custom_call" | custom-call | tf_op jit(solution)/shard_map/pallas_call | solution.py:28
  87.3 1.7 %collective-permute-done.4.other = bf16[16,256,256]{2,1,0:T(8,128)(2,1)S(1)} collective-permute-done((bf16[16,256,256]{2,1,0:T(8,128)(2,1)S(1)}, bf16[16,256,256]{2,1,0:T(8,128)(2,1)S(1)}, u32[]{:S(2)}, u32[]{:S(2)}) %collective-permute-start.4) | collective-permute-done | bytes 2097184 | tf_op jit(solution)/shard_map/ppermute | solution.py:19
  89.0 2.6 %shard_map.134 = (bf16[128,256]{1,0:T(8,128)(2,1)S(1)}, bf16[128,256]{1,0:T(8,128)(2,1)S(1)}, f32[32,2,256]{2,1,0:T(2,128)S(1)}) custom-call(f32[256,256]{1,0:T(8,128)S(1)} %get-tuple-element.24.gate, f32[256,256]{1,0:T(8,128)S(1)} %get-tuple-element.25.up, f32[256,16]{1,0:T(8,128)S(1)} %get-tuple-element.26.logits, ...), custom_call_target="tpu_custom_call" | custom-call | tf_op jit(solution)/shard_map/pallas_call | solution.py:28
  91.6 0.4 collective-permute-start.5
  92.1 0.9 collective-permute-done.5.act_other
  93.0 3.0 %shard_map.135 = bf16[64,16,896]{2,1,0:T(8,128)(2,1)S(1)} custom-call(bf16[128,256]{1,0:T(8,128)(2,1)S(1)} %get-tuple-element.28.act, bf16[128,256]{1,0:T(8,128)(2,1)S(1)} %collective-permute-done.5.act_other, bf16[256,7168]{1,0:T(8,128)(2,1)S(1)} %bitcast.17, bf16[256,7168]{1,0:T(8,128)(2,1)S(1)} %collective-permute-done.2.swapped.w_down_other), custom_call_target="tpu_custom_call" | custom-call | tf_op jit(solution)/shard_map/pallas_call | solution.py:28
  96.0 29.4 %all_to_all.23.pieces = bf16[64,16,896]{2,1,0:T(8,128)(2,1)S(1)} all-to-all(bf16[64,16,896]{2,1,0:T(8,128)(2,1)S(1)} %shard_map.135), channel_id=1, replica_groups=mesh['req'=16,'seq'=2,'exp'=4] {'exp','req'}, dimensions={0} | all-to-all | bytes 3670016 | tf_op jit(solution)/shard_map/all_to_all | solution.py:489
  125.4 1.0 shard_map.136
  (21 shorter events, 0.1 us)
Async XLA Ops:
  0.0 36.6 %collective-permute-start.2 = (bf16[256,7168]{1,0:T(8,128)(2,1)}, bf16[256,7168]{1,0:T(8,128)(2,1)S(1)}, u32[]{:S(2)}, u32[]{:S(2)}) collective-permute-start(bf16[256,7168]{1,0:T(8,128)(2,1)} %bitcast.16), channel_id=1, source_target_pairs={{0,4},{4,0},{1,5},{5,1},{2,6},{6,2},{3,7},{7,3},{8,12},{12,8},{9,1... | collective-permute-start | bytes 11010056 | tf_op jit(solution)/shard_map/ppermute | solution.py:19
  1.4 35.2 %collective-permute-start.1 = (bf16[224,4096]{1,0:T(8,128)(2,1)}, bf16[224,4096]{1,0:T(8,128)(2,1)S(1)}, u32[]{:S(2)}, u32[]{:S(2)}) collective-permute-start(bf16[224,4096]{1,0:T(8,128)(2,1)} %bitcast.18), channel_id=1, source_target_pairs={{0,4},{4,0},{1,5},{5,1},{2,6},{6,2},{3,7},{7,3},{8,12},{12,8},{9,1... | collective-permute-start | bytes 5505032 | tf_op jit(solution)/shard_map/ppermute | solution.py:19
  2.0 0.7 copy-start.7
  2.7 8.0 %copy-start.5 = (bf16[2,7168]{1,0:T(2,128)(2,1)S(1)}, bf16[2,7168]{1,0:T(2,128)(2,1)}, u32[]{:S(2)}) copy-start(bf16[2,7168]{1,0:T(2,128)(2,1)} %residual.1) | copy-start | bytes 86020
  2.7 8.0 %copy-start.6 = (s32[2,8]{1,0:T(2,128)S(1)}, s32[2,8]{1,0:T(2,128)}, u32[]{:S(2)}) copy-start(s32[2,8]{1,0:T(2,128)} %expert_ids.1) | copy-start | bytes 196
  5.7 5.0 %collective-permute-start = (bf16[256,640]{1,0:T(8,128)(2,1)S(1)}, bf16[256,640]{1,0:T(8,128)(2,1)S(1)}, u32[]{:S(2)}, u32[]{:S(2)}) collective-permute-start(bf16[256,640]{1,0:T(8,128)(2,1)S(1)} %get-tuple-element.20), channel_id=1, source_target_pairs={{0,4},{4,0},{1,5},{5,1},{2,6},{6,2},{3,7},{7,3},{8,12},{12,8},{9,1... | collective-permute-start | bytes 983048 | tf_op jit(solution)/shard_map/ppermute | solution.py:19
  36.6 2.3 %copy-start.3 = (bf16[4096,224]{0,1:T(8,128)(2,1)S(1)}, bf16[4096,224]{0,1:T(8,128)(2,1)}, u32[]{:S(2)}) copy-start(bf16[4096,224]{0,1:T(8,128)(2,1)} %param.19) | copy-start | bytes 5505028
  37.1 2.8 %collective-permute-start.3 = (bf16[288,256]{1,0:T(8,128)(2,1)S(1)}, bf16[288,256]{1,0:T(8,128)(2,1)S(1)}, u32[]{:S(2)}, u32[]{:S(2)}) collective-permute-start(bf16[288,256]{1,0:T(8,128)(2,1)S(1)} %shard_map.130), channel_id=1, source_target_pairs={{0,4},{4,0},{1,5},{5,1},{2,6},{6,2},{3,7},{7,3},{8,12},{12,8},{9,1... | collective-permute-start | bytes 442376 | tf_op jit(solution)/shard_map/ppermute | solution.py:19
  39.9 45.4 %copy-start.1 = (bf16[1,7168,256]{2,1,0:T(8,128)(2,1)S(1)}, bf16[1,7168,256]{2,1,0:T(8,128)(2,1)}, u32[]{:S(2)}) copy-start(bf16[1,7168,256]{2,1,0:T(8,128)(2,1)} %param.24) | copy-start | bytes 11010052
  49.3 35.9 %copy-start.8 = (bf16[7168]{0:T(1024)(128)(2,1)S(1)}, bf16[7168]{0:T(1024)(128)(2,1)}, u32[]{:S(2)}) copy-start(bf16[7168]{0:T(1024)(128)(2,1)} %param.20) | copy-start | bytes 43012
  49.3 35.9 %copy-start = (bf16[1,7168,256]{2,1,0:T(8,128)(2,1)S(1)}, bf16[1,7168,256]{2,1,0:T(8,128)(2,1)}, u32[]{:S(2)}) copy-start(bf16[1,7168,256]{2,1,0:T(8,128)(2,1)} %param.23) | copy-start | bytes 11010052
  49.3 35.9 %copy-start.4 = (bf16[7168,16]{0,1:T(8,128)(2,1)S(1)}, bf16[7168,16]{0,1:T(8,128)(2,1)}, u32[]{:S(2)}) copy-start(bf16[7168,16]{0,1:T(8,128)(2,1)} %param.21) | copy-start | bytes 688132
  81.4 7.5 %collective-permute-start.4 = (bf16[16,256,256]{2,1,0:T(8,128)(2,1)S(1)}, bf16[16,256,256]{2,1,0:T(8,128)(2,1)S(1)}, u32[]{:S(2)}, u32[]{:S(2)}) collective-permute-start(bf16[16,256,256]{2,1,0:T(8,128)(2,1)S(1)} %bitcast.9), channel_id=1, source_target_pairs={{0,4},{4,0},{1,5},{5,1},{2,6},{6,2},{3,7},{7,3},{8,12},{12,8},{9,1... | collective-permute-start | bytes 6291464 | tf_op jit(solution)/shard_map/ppermute | solution.py:19
  89.0 4.0 %copy-start.2 = (bf16[1,256,7168]{2,1,0:T(8,128)(2,1)S(1)}, bf16[1,256,7168]{2,1,0:T(8,128)(2,1)}, u32[]{:S(2)}) copy-start(bf16[1,256,7168]{2,1,0:T(8,128)(2,1)} %param.25) | copy-start | bytes 11010052
  91.6 1.4 %collective-permute-start.5 = (bf16[128,256]{1,0:T(8,128)(2,1)S(1)}, bf16[128,256]{1,0:T(8,128)(2,1)S(1)}, u32[]{:S(2)}, u32[]{:S(2)}) collective-permute-start(bf16[128,256]{1,0:T(8,128)(2,1)S(1)} %get-tuple-element.29), channel_id=1, source_target_pairs={{0,4},{4,0},{1,5},{5,1},{2,6},{6,2},{3,7},{7,3},{8,12},{12,8},{9,1... | collective-permute-start | bytes 196616 | tf_op jit(solution)/shard_map/ppermute | solution.py:19

commit v8 on v7

--- a/solution.py
+++ b/solution.py
@@ -217,41 +217,42 @@
     out[...] = project_terms(gathered, out_proj_t, lax.axis_index("seq"))
 
 
-def project_sum_kernel(started, arrived, gathered, terms, residual):
+def project_sum_kernel(started, arrived, gathered, fanned):
     reqs, _, drafts, lanes = gathered.shape
-    exps, _, padded = terms.shape
+    exps, tokens, padded = fanned.shape
     width = started.shape[1]
-    side = lax.axis_index("seq")
-    tokens = reqs * drafts
+    side, exp = lax.axis_index("seq"), lax.axis_index("exp")
     own_rows = drafts // (2 * exps)
     total = (started[...] + arrived[:tokens, :width].astype(F32)).astype(BF16)
 
+    def parts(i):
+        token_exp, req = i // (tokens // exps), i // (2 * own_rows) % reqs
+        return token_exp, req, i // own_rows % 2, i % own_rows
+
     def source(i):
-        exp, req = i // (tokens // exps), i // (2 * own_rows) % reqs
-        seq, row = i // own_rows % 2, i % own_rows
-        return ((req * 2 + seq) * exps + exp) * own_rows + row
+        token_exp, req, seq, row = parts(i)
+        return ((req * 2 + seq) * exps + token_exp) * own_rows + row
 
     total = jnp.dot(one_hot((tokens, tokens), source), total, preferred_element_type=F32)
     total = jnp.concatenate([total, jnp.zeros((tokens, padded - width), F32)], -1)
-    terms[...] = total.astype(BF16).reshape(terms.shape)
-    picked = jnp.zeros(residual.shape, F32)
     for rows, from_side in (
         (residual_rows(gathered, side, padded // lanes), side),
         (arrived[tokens:], 1 - side),
     ):
 
         def residual_source(i):
-            req, seq, row = i // (2 * own_rows), i // own_rows % 2, i % own_rows
-            return jnp.where(seq == from_side, req * own_rows + row, -1)
-
-        order = one_hot((residual.shape[0], rows.shape[0]), residual_source)
-        picked += jnp.dot(order, rows, preferred_element_type=F32)
-    residual[...] = picked.astype(BF16)
-
-
-def hidden_kernel(terms, residual, fanned):
-    attended = jnp.sum(terms[...].astype(F32), 0).astype(BF16)
-    hidden = (residual[...].astype(F32) + attended.astype(F32)).astype(BF16)
+            token_exp, req, seq, row = parts(i)
+            return jnp.where((seq == from_side) & (token_exp == exp), req * own_rows + row, -1)
+
+        order = one_hot((tokens, rows.shape[0]), residual_source)
+        total += jnp.dot(order, rows, preferred_element_type=F32)
+    total = total.astype(BF16)
+    for dest in range(exps):
+        fanned[dest] = total
+
+
+def hidden_kernel(terms, fanned):
+    hidden = jnp.sum(terms[...].astype(F32), 0).astype(BF16)
     for dest in range(fanned.shape[0]):
         fanned[dest] = hidden
 
@@ -431,22 +432,12 @@
         )
     )
     started = call(project_own_kernel, shape((tokens, width), F32), gathered, out_proj_t)
-    terms, resid = call(
-        project_sum_kernel,
-        (
-            shape((n_exp, tokens // n_exp, padded), BF16),
-            shape((tokens // n_exp, padded), BF16),
-        ),
-        started,
-        arrived,
-        gathered,
+    terms = call(
+        project_sum_kernel, shape((n_exp, tokens, padded), BF16), started, arrived, gathered
     )
     terms = lax.all_to_all(terms, "exp", split_axis=0, concat_axis=0, tiled=True)
-    fanned = call(
-        hidden_kernel, shape((n_req * n_exp, tokens // n_exp, padded), BF16), terms, resid
-    )
-    own = lax.all_to_all(fanned, ("req", "exp"), split_axis=0, concat_axis=0, tiled=True)
-    own = own.reshape(n_req, tokens, padded)
+    fanned = call(hidden_kernel, shape((n_req, tokens, padded), BF16), terms)
+    own = lax.all_to_all(fanned, "req", split_axis=0, concat_axis=0, tiled=True)
     other = swap(own)
     started = call(
         gate_up_own_kernel,

time: 128 us -> 129 us (level)
  blocking collectives: 95.2 us -> 96.6 us
    all_to_all x1, blocking collectives: 8.9 us -> 12.7 us  [per_device(): lax.all_to_all(terms, 'exp', split_axis=0, concat_axis=0, tiled=True)]
    all_to_all x1, blocking collectives: 32.1 us -> 29.5 us  [per_device(): own = lax.all_to_all(fanned, 'req', split_axis=0, concat_axis=0, tiled=True)]
where the time goes in v8:
time: 129 us; the launch traced here: 127 us
  blocking collectives  96.6 us (75%)
  Pallas kernels  14.3 us (11%)
  waiting for transfers between devices  7.53 us (6%)
  starting transfers between devices  7.21 us (6%)
    all_to_all x1, blocking collectives, per_device(): lax.all_to_all(pieces, ('exp', 'req'), split_axis=0, concat_axis=0, tiled...  29.7 us
    all_to_all x1, blocking collectives, per_device(): own = lax.all_to_all(fanned, 'req', split_axis=0, concat_axis=0, tiled=True)  29.5 us
    all_to_all x1, blocking collectives, per_device(): lax.all_to_all(fanned, 'req', split_axis=0, concat_axis=0, tiled=True)  24.8 us
    pallas_call x10, Pallas kernels, call(): pl.pallas_call(kernel, out_shape=out_shape, in_specs=[pl.BlockSpec(memory...  14.3 us
    all_to_all x1, blocking collectives, per_device(): lax.all_to_all(terms, 'exp', split_axis=0, concat_axis=0, tiled=True)  12.7 us
    ppermute x6, waiting for transfers between devices, swap(): return lax.ppermute(x, 'seq', SWAP)  7.53 us
    ppermute x6, starting transfers between devices, swap(): return lax.ppermute(x, 'seq', SWAP)  7.21 us
  transfers between devices with their start and end apart: 6, of which 4 were waited for; matrix products, arithmetic and copies ran while one was open for 0% of the time, Pallas kernels for 5%

profile of v8, /device:TPU:1, one launch (start us, length us, event | category | flops | bytes accessed | tf_op | source)
XLA Modules:
  0.0 127.1 jit_solution(9885048133397732223)
XLA Ops:
  0.0 1.4 %collective-permute-start.2 = (bf16[256,7168]{1,0:T(8,128)(2,1)}, bf16[256,7168]{1,0:T(8,128)(2,1)S(1)}, u32[]{:S(2)}, u32[]{:S(2)}) collective-permute-start(bf16[256,7168]{1,0:T(8,128)(2,1)} %bitcast.12), channel_id=1, source_target_pairs={{0,4},{4,0},{1,5},{5,1},{2,6},{6,2},{3,7},{7,3},{8,12},{12,8},{9,1... | collective-permute-start | bytes 11010056 | tf_op jit(solution)/shard_map/ppermute | solution.py:19
  2.0 0.6 copy-done.7
  2.7 3.0 %shard_map.127 = (bf16[256,640]{1,0:T(8,128)(2,1)S(1)}, f32[256,512]{1,0:T(8,128)S(1)}, f32[256,256]{1,0:T(8,128)S(1)}, bf16[16,512,128]{2,1,0:T(8,128)(2,1)S(1)}) custom-call(s32[1]{0:T(128)S(6)} %copy.14.lengths, s32[2]{0:T(128)S(1)} %bitcast.18, bf16[16,32,576]{2,1,0:T(8,128)(2,1)} %bitcast.19, bf16[192,576]{1,0:T(8,128)(2,1)} %bitcast.20, ...), custom_call_target="tpu_custom_call" | custom-call | tf_op jit(solution)/shard_map/pallas_call | solution.py:28
  5.7 0.6 collective-permute-start
  6.3 4.4 %collective-permute-done.arrived = bf16[256,640]{1,0:T(8,128)(2,1)S(1)} collective-permute-done((bf16[256,640]{1,0:T(8,128)(2,1)S(1)}, bf16[256,640]{1,0:T(8,128)(2,1)S(1)}, u32[]{:S(2)}, u32[]{:S(2)}) %collective-permute-start) | collective-permute-done | bytes 327712 | tf_op jit(solution)/shard_map/ppermute | solution.py:19
  10.7 1.1 shard_map.128
  11.8 24.8 %all_to_all.20.gathered = bf16[16,17,16,128]{3,2,1,0:T(8,128)(2,1)S(1)} all-to-all(bf16[16,17,16,128]{3,2,1,0:T(8,128)(2,1)S(1)} %shard_map.128), channel_id=1, replica_groups=mesh['req'=16,'seq'=2,'exp'=4] {'req'}, dimensions={0} | all-to-all | bytes 2228224 | tf_op jit(solution)/shard_map/all_to_all | solution.py:424
  36.6 0.5 shard_map.130
  37.1 1.7 %collective-permute-start.3 = (bf16[288,256]{1,0:T(8,128)(2,1)S(1)}, bf16[288,256]{1,0:T(8,128)(2,1)S(1)}, u32[]{:S(2)}, u32[]{:S(2)}) collective-permute-start(bf16[288,256]{1,0:T(8,128)(2,1)S(1)} %shard_map.130), channel_id=1, source_target_pairs={{0,4},{4,0},{1,5},{5,1},{2,6},{6,2},{3,7},{7,3},{8,12},{12,8},{9,1... | collective-permute-start | bytes 442376 | tf_op jit(solution)/shard_map/ppermute | solution.py:19
  38.8 0.5 shard_map.129.started
  39.3 0.5 collective-permute-done.3.arrived
  39.9 0.4 shard_map.131
  40.2 12.7 %all_to_all.21.terms = bf16[4,256,256]{2,1,0:T(8,128)(2,1)S(1)} all-to-all(bf16[4,256,256]{2,1,0:T(8,128)(2,1)S(1)} %shard_map.131), channel_id=1, replica_groups=mesh['req'=16,'seq'=2,'exp'=4] {'exp'}, dimensions={0} | all-to-all | bytes 1048576 | tf_op jit(solution)/shard_map/all_to_all | solution.py:438
  52.9 0.2 shard_map.132
  53.2 29.5 %all_to_all.22.own = bf16[16,256,256]{2,1,0:T(8,128)(2,1)S(1)} all-to-all(bf16[16,256,256]{2,1,0:T(8,128)(2,1)S(1)} %shard_map.132), channel_id=1, replica_groups=mesh['req'=16,'seq'=2,'exp'=4] {'req'}, dimensions={0} | all-to-all | bytes 4194304 | tf_op jit(solution)/shard_map/all_to_all | solution.py:440
  82.6 3.0 %collective-permute-start.4 = (bf16[16,256,256]{2,1,0:T(8,128)(2,1)S(1)}, bf16[16,256,256]{2,1,0:T(8,128)(2,1)S(1)}, u32[]{:S(2)}, u32[]{:S(2)}) collective-permute-start(bf16[16,256,256]{2,1,0:T(8,128)(2,1)S(1)} %all_to_all.22.own), channel_id=1, source_target_pairs={{0,4},{4,0},{1,5},{5,1},{2,6},{6,2},{3,7},{7,3},{8,12},{12,8},{9,1... | collective-permute-start | bytes 6291464 | tf_op jit(solution)/shard_map/ppermute | solution.py:19
  85.7 2.0 %shard_map.133 = (f32[256,256]{1,0:T(8,128)S(1)}, f32[256,256]{1,0:T(8,128)S(1)}, f32[256,16]{1,0:T(8,128)S(1)}, f32[256,128]{1,0:T(8,128)S(1)}) custom-call(bf16[16,256,256]{2,1,0:T(8,128)(2,1)S(1)} %all_to_all.22.own, bf16[1,7168]{1,0:T(2,128)(2,1)S(1)} %reshape.7.gains, bf16[7168,256]{1,0:T(8,128)(2,1)S(1)} %bitcast.8, bf16[7168,256]{1,0:T(8,128)(2,1)S(1)} %bitcast.10, ...), custom_call_target="tpu_custom_call" | custom-call | tf_op jit(solution)/shard_map/pallas_call | solution.py:28
  87.8 1.7 %collective-permute-done.4.other = bf16[16,256,256]{2,1,0:T(8,128)(2,1)S(1)} collective-permute-done((bf16[16,256,256]{2,1,0:T(8,128)(2,1)S(1)}, bf16[16,256,256]{2,1,0:T(8,128)(2,1)S(1)}, u32[]{:S(2)}, u32[]{:S(2)}) %collective-permute-start.4) | collective-permute-done | bytes 2097184 | tf_op jit(solution)/shard_map/ppermute | solution.py:19
  89.5 2.6 %shard_map.134 = (bf16[128,256]{1,0:T(8,128)(2,1)S(1)}, bf16[128,256]{1,0:T(8,128)(2,1)S(1)}, f32[32,2,256]{2,1,0:T(2,128)S(1)}) custom-call(f32[256,256]{1,0:T(8,128)S(1)} %get-tuple-element.20.gate, f32[256,256]{1,0:T(8,128)S(1)} %get-tuple-element.21.up, f32[256,16]{1,0:T(8,128)S(1)} %get-tuple-element.22.logits, ...), custom_call_target="tpu_custom_call" | custom-call | tf_op jit(solution)/shard_map/pallas_call | solution.py:28
  92.1 0.5 collective-permute-start.5
  92.5 0.9 collective-permute-done.5.act_other
  93.5 3.0 %shard_map.135 = bf16[64,16,896]{2,1,0:T(8,128)(2,1)S(1)} custom-call(bf16[128,256]{1,0:T(8,128)(2,1)S(1)} %get-tuple-element.24.act, bf16[128,256]{1,0:T(8,128)(2,1)S(1)} %collective-permute-done.5.act_other, bf16[256,7168]{1,0:T(8,128)(2,1)S(1)} %bitcast.13, bf16[256,7168]{1,0:T(8,128)(2,1)S(1)} %collective-permute-done.2.swapped.w_down_other), custom_call_target="tpu_custom_call" | custom-call | tf_op jit(solution)/shard_map/pallas_call | solution.py:28
  96.5 29.7 %all_to_all.23.pieces = bf16[64,16,896]{2,1,0:T(8,128)(2,1)S(1)} all-to-all(bf16[64,16,896]{2,1,0:T(8,128)(2,1)S(1)} %shard_map.135), channel_id=1, replica_groups=mesh['req'=16,'seq'=2,'exp'=4] {'exp','req'}, dimensions={0} | all-to-all | bytes 3670016 | tf_op jit(solution)/shard_map/all_to_all | solution.py:480
  126.2 1.0 shard_map.136
  (21 shorter events, 0.1 us)
Async XLA Ops:
  0.0 36.6 %collective-permute-start.2 = (bf16[256,7168]{1,0:T(8,128)(2,1)}, bf16[256,7168]{1,0:T(8,128)(2,1)S(1)}, u32[]{:S(2)}, u32[]{:S(2)}) collective-permute-start(bf16[256,7168]{1,0:T(8,128)(2,1)} %bitcast.12), channel_id=1, source_target_pairs={{0,4},{4,0},{1,5},{5,1},{2,6},{6,2},{3,7},{7,3},{8,12},{12,8},{9,1... | collective-permute-start | bytes 11010056 | tf_op jit(solution)/shard_map/ppermute | solution.py:19
  1.4 35.2 %collective-permute-start.1 = (bf16[224,4096]{1,0:T(8,128)(2,1)}, bf16[224,4096]{1,0:T(8,128)(2,1)S(1)}, u32[]{:S(2)}, u32[]{:S(2)}) collective-permute-start(bf16[224,4096]{1,0:T(8,128)(2,1)} %bitcast.14), channel_id=1, source_target_pairs={{0,4},{4,0},{1,5},{5,1},{2,6},{6,2},{3,7},{7,3},{8,12},{12,8},{9,1... | collective-permute-start | bytes 5505032 | tf_op jit(solution)/shard_map/ppermute | solution.py:19
  2.0 0.7 copy-start.7
  2.7 8.0 %copy-start.5 = (bf16[2,7168]{1,0:T(2,128)(2,1)S(1)}, bf16[2,7168]{1,0:T(2,128)(2,1)}, u32[]{:S(2)}) copy-start(bf16[2,7168]{1,0:T(2,128)(2,1)} %residual.1) | copy-start | bytes 86020
  2.7 8.0 %copy-start.6 = (s32[2,8]{1,0:T(2,128)S(1)}, s32[2,8]{1,0:T(2,128)}, u32[]{:S(2)}) copy-start(s32[2,8]{1,0:T(2,128)} %expert_ids.1) | copy-start | bytes 196
  5.7 5.0 %collective-permute-start = (bf16[256,640]{1,0:T(8,128)(2,1)S(1)}, bf16[256,640]{1,0:T(8,128)(2,1)S(1)}, u32[]{:S(2)}, u32[]{:S(2)}) collective-permute-start(bf16[256,640]{1,0:T(8,128)(2,1)S(1)} %get-tuple-element.18), channel_id=1, source_target_pairs={{0,4},{4,0},{1,5},{5,1},{2,6},{6,2},{3,7},{7,3},{8,12},{12,8},{9,1... | collective-permute-start | bytes 983048 | tf_op jit(solution)/shard_map/ppermute | solution.py:19
  36.6 2.3 %copy-start.3 = (bf16[4096,224]{0,1:T(8,128)(2,1)S(1)}, bf16[4096,224]{0,1:T(8,128)(2,1)}, u32[]{:S(2)}) copy-start(bf16[4096,224]{0,1:T(8,128)(2,1)} %param.19) | copy-start | bytes 5505028
  37.1 2.8 %collective-permute-start.3 = (bf16[288,256]{1,0:T(8,128)(2,1)S(1)}, bf16[288,256]{1,0:T(8,128)(2,1)S(1)}, u32[]{:S(2)}, u32[]{:S(2)}) collective-permute-start(bf16[288,256]{1,0:T(8,128)(2,1)S(1)} %shard_map.130), channel_id=1, source_target_pairs={{0,4},{4,0},{1,5},{5,1},{2,6},{6,2},{3,7},{7,3},{8,12},{12,8},{9,1... | collective-permute-start | bytes 442376 | tf_op jit(solution)/shard_map/ppermute | solution.py:19
  40.2 45.5 %copy-start.1 = (bf16[1,7168,256]{2,1,0:T(8,128)(2,1)S(1)}, bf16[1,7168,256]{2,1,0:T(8,128)(2,1)}, u32[]{:S(2)}) copy-start(bf16[1,7168,256]{2,1,0:T(8,128)(2,1)} %param.24) | copy-start | bytes 11010052
  53.1 32.5 %copy-start.8 = (bf16[7168]{0:T(1024)(128)(2,1)S(1)}, bf16[7168]{0:T(1024)(128)(2,1)}, u32[]{:S(2)}) copy-start(bf16[7168]{0:T(1024)(128)(2,1)} %param.20) | copy-start | bytes 43012
  53.1 32.6 %copy-start = (bf16[1,7168,256]{2,1,0:T(8,128)(2,1)S(1)}, bf16[1,7168,256]{2,1,0:T(8,128)(2,1)}, u32[]{:S(2)}) copy-start(bf16[1,7168,256]{2,1,0:T(8,128)(2,1)} %param.23) | copy-start | bytes 11010052
  53.2 32.6 %copy-start.4 = (bf16[7168,16]{0,1:T(8,128)(2,1)S(1)}, bf16[7168,16]{0,1:T(8,128)(2,1)}, u32[]{:S(2)}) copy-start(bf16[7168,16]{0,1:T(8,128)(2,1)} %param.21) | copy-start | bytes 688132
  82.6 6.8 %collective-permute-start.4 = (bf16[16,256,256]{2,1,0:T(8,128)(2,1)S(1)}, bf16[16,256,256]{2,1,0:T(8,128)(2,1)S(1)}, u32[]{:S(2)}, u32[]{:S(2)}) collective-permute-start(bf16[16,256,256]{2,1,0:T(8,128)(2,1)S(1)} %all_to_all.22.own), channel_id=1, source_target_pairs={{0,4},{4,0},{1,5},{5,1},{2,6},{6,2},{3,7},{7,3},{8,12},{12,8},{9,1... | collective-permute-start | bytes 6291464 | tf_op jit(solution)/shard_map/ppermute | solution.py:19
  89.5 4.0 %copy-start.2 = (bf16[1,256,7168]{2,1,0:T(8,128)(2,1)S(1)}, bf16[1,256,7168]{2,1,0:T(8,128)(2,1)}, u32[]{:S(2)}) copy-start(bf16[1,256,7168]{2,1,0:T(8,128)(2,1)} %param.25) | copy-start | bytes 11010052
  92.1 1.4 %collective-permute-start.5 = (bf16[128,256]{1,0:T(8,128)(2,1)S(1)}, bf16[128,256]{1,0:T(8,128)(2,1)S(1)}, u32[]{:S(2)}, u32[]{:S(2)}) collective-permute-start(bf16[128,256]{1,0:T(8,128)(2,1)S(1)} %get-tuple-element.25), channel_id=1, source_target_pairs={{0,4},{4,0},{1,5},{5,1},{2,6},{6,2},{3,7},{7,3},{8,12},{12,8},{9,1... | collective-permute-start | bytes 196616 | tf_op jit(solution)/shard_map/ppermute | solution.py:19

commit v9 on v7

--- a/solution.py
+++ b/solution.py
@@ -13,6 +13,7 @@
 F32 = jnp.float32
 BF16 = jnp.bfloat16
 SWAP = [(0, 1), (1, 0)]
+PACK = 4
 
 
 def swap(x):
@@ -233,7 +234,6 @@
 
     total = jnp.dot(one_hot((tokens, tokens), source), total, preferred_element_type=F32)
     total = jnp.concatenate([total, jnp.zeros((tokens, padded - width), F32)], -1)
-    terms[...] = total.astype(BF16).reshape(terms.shape)
     picked = jnp.zeros(residual.shape, F32)
     for rows, from_side in (
         (residual_rows(gathered, side, padded // lanes), side),
@@ -247,17 +247,36 @@
         order = one_hot((residual.shape[0], rows.shape[0]), residual_source)
         picked += jnp.dot(order, rows, preferred_element_type=F32)
     residual[...] = picked.astype(BF16)
+    lane = lax.broadcasted_iota(jnp.int32, residual.shape, 1)
+    named = jnp.where(lane < width, 0.0, picked)
+    for dest in range(exps):
+        rows = total[dest * residual.shape[0] : (dest + 1) * residual.shape[0]]
+        terms[dest] = (rows + named).astype(BF16)
 
 
 def hidden_kernel(terms, residual, fanned):
     attended = jnp.sum(terms[...].astype(F32), 0).astype(BF16)
-    hidden = (residual[...].astype(F32) + attended.astype(F32)).astype(BF16)
+    hidden = residual[...].astype(F32) + attended.astype(F32)
+    rows, width = fanned.shape[1], fanned.shape[2] // PACK
+    packed = jnp.concatenate(
+        [hidden[i * rows : (i + 1) * rows, :width] for i in range(PACK)], -1
+    ).astype(BF16)
     for dest in range(fanned.shape[0]):
-        fanned[dest] = hidden
+        fanned[dest] = packed
+
+
+def unpacked(rows, i, width):
+    exps = rows.shape[1]
+    pieces = []
+    for exp in range(exps):
+        tile = rows[i, exp].astype(F32)
+        pieces += [tile[:, j * width : (j + 1) * width] for j in range(PACK)]
+    return jnp.concatenate(pieces, 0)
 
 
 def expert_terms(rows, gains, w_gate, w_up, router_t, side):
-    steps, tokens, _ = rows.shape
+    steps, exps, packed_rows, _ = rows.shape
+    tokens = exps * packed_rows * PACK
     width = gains.shape[1] // (2 * steps)
     gate = jnp.zeros((tokens, w_gate.shape[1]), F32)
     up = jnp.zeros((tokens, w_up.shape[1]), F32)
@@ -271,7 +290,7 @@
 
     for i in range(steps):
         start = pl.multiple_of((i * 2 + side) * width, 32)
-        hidden = rows[i][:, :width].astype(F32)
+        hidden = unpacked(rows, i, width)
         scaled = (hidden * columns_of(gains, i)).astype(BF16)
         gate += jnp.dot(scaled, w_gate[pl.ds(start, width), :], preferred_element_type=F32)
         up += jnp.dot(scaled, w_up[pl.ds(start, width), :], preferred_element_type=F32)
@@ -292,29 +311,33 @@
 
 
 def gate_up_both_kernel(
-    gate, up, logits, squares, own, other, gains, w_gate, w_up, router_t,
+    gate, up, logits, squares, own, other, terms, gains, w_gate, w_up, router_t,
     act_mine, act_theirs, rows_here,
 ):
     side = lax.axis_index("seq")
     own_rows = rows_here.shape[1]
-    place = (lax.axis_index("exp") * own.shape[0] + lax.axis_index("req")) * 2 + side
-    place = place * own_rows
-    around = pl.ds(pl.multiple_of(place // 16 * 16, 16), 16)
-    near = lax.broadcasted_iota(jnp.int32, (16, own.shape[2]), 0)
+    exp, req = lax.axis_index("exp"), lax.axis_index("req")
+    packed_rows = own.shape[2]
+    place = (req * 2 + side) * own_rows
+    group, first = place // packed_rows, place % packed_rows
+    part = rows_here.shape[2]
+    near = lax.broadcasted_iota(jnp.int32, own.shape[2:], 0)
     for rows, from_side in ((own, side), (other, 1 - side)):
         for i in range(own.shape[0]):
-            tile = rows[i, around, :].astype(F32)
-            picked = [
-                jnp.sum(jnp.where(near == place % 16 + row, tile, 0.0), 0, keepdims=True)
-                for row in range(own_rows)
-            ]
-            rows_here[i * 2 + from_side] = jnp.concatenate(picked, 0)
+            tile = rows[i, exp].astype(F32)
+            for row in range(own_rows):
+                line = jnp.sum(jnp.where(near == first + row, tile, 0.0), 0, keepdims=True)
+                picked = line[:, :part]
+                for j in range(1, PACK):
+                    picked = jnp.where(group == j, line[:, j * part : (j + 1) * part], picked)
+                rows_here[i * 2 + from_side, row : row + 1, :] = picked
     width = gains.shape[1] // (2 * own.shape[0])
     experts = logits.shape[1]
     columns = gains.shape[1]
     a, b, c, d = expert_terms(other, gains, w_gate, w_up, router_t, 1 - side)
     scale = lax.rsqrt((squares[:, 0:1] + d) / columns + 1e-06)
-    named = own[0, :, width : width + experts].astype(F32)
+    tokens = gate.shape[0]
+    named = terms[...].reshape(tokens, terms.shape[2])[:, width : width + experts].astype(F32)
     chosen = named * jax.nn.sigmoid((logits[...] + c) * scale)
     mine = lax.broadcasted_iota(jnp.int32, chosen.shape, 1) == lax.axis_index("req")
     weight = jnp.sum(jnp.where(mine, chosen, 0.0), -1, keepdims=True)
@@ -443,10 +466,13 @@
     )
     terms = lax.all_to_all(terms, "exp", split_axis=0, concat_axis=0, tiled=True)
     fanned = call(
-        hidden_kernel, shape((n_req * n_exp, tokens // n_exp, padded), BF16), terms, resid
+        hidden_kernel,
+        shape((n_req * n_exp, tokens // n_exp // PACK, width * PACK), BF16),
+        terms,
+        resid,
     )
     own = lax.all_to_all(fanned, ("req", "exp"), split_axis=0, concat_axis=0, tiled=True)
-    own = own.reshape(n_req, tokens, padded)
+    own = own.reshape(n_req, n_exp, tokens // n_exp // PACK, width * PACK)
     other = swap(own)
     started = call(
         gate_up_own_kernel,
@@ -467,11 +493,12 @@
         (
             shape((tokens // 2, hidden_units), BF16),
             shape((tokens // 2, hidden_units), BF16),
-            shape((n_req * 2, own_rows, padded), F32),
+            shape((n_req * 2, own_rows, width), F32),
         ),
         *started,
         own,
         other,
+        terms,
         gains,
         w_gate,
         w_up,

time: 128 us -> 133 us (1.039)
  Pallas kernels: 14.2 us -> 22.7 us
  blocking collectives: 95.2 us -> 92.8 us
    pallas_call x10, Pallas kernels: 14.2 us -> 22.7 us  [call(): pl.pallas_call(kernel, out_shape=out_shape, in_specs=[pl.BlockSpec(memory...]
    all_to_all x1, blocking collectives: 32.1 us -> 29.6 us  [per_device(): lax.all_to_all(fanned, ('req', 'exp'), split_axis=0, concat_axis=0, tiled...]
where the time goes in v9:
time: 133 us; the launch traced here: 132 us
  blocking collectives  92.8 us (70%)
  Pallas kernels  22.7 us (17%)
  starting transfers between devices  7.56 us (6%)
  waiting for transfers between devices  6.98 us (5%)
    all_to_all x1, blocking collectives, per_device(): lax.all_to_all(fanned, ('req', 'exp'), split_axis=0, concat_axis=0, tiled...  29.6 us
    all_to_all x1, blocking collectives, per_device(): lax.all_to_all(pieces, ('exp', 'req'), split_axis=0, concat_axis=0, tiled...  29.5 us
    all_to_all x1, blocking collectives, per_device(): lax.all_to_all(fanned, 'req', split_axis=0, concat_axis=0, tiled=True)  24.8 us
    pallas_call x10, Pallas kernels, call(): pl.pallas_call(kernel, out_shape=out_shape, in_specs=[pl.BlockSpec(memory...  22.7 us
    all_to_all x1, blocking collectives, per_device(): lax.all_to_all(terms, 'exp', split_axis=0, concat_axis=0, tiled=True)  8.91 us
    ppermute x6, starting transfers between devices, swap(): return lax.ppermute(x, 'seq', SWAP)  7.56 us
    ppermute x6, waiting for transfers between devices, swap(): return lax.ppermute(x, 'seq', SWAP)  6.98 us
  transfers between devices with their start and end apart: 6, of which 4 were waited for; matrix products, arithmetic and copies ran while one was open for 0% of the time, Pallas kernels for 5%

profile of v9, /device:TPU:1, one launch (start us, length us, event | category | flops | bytes accessed | tf_op | source)
XLA Modules:
  0.0 131.5 jit_solution(13920594141553428270)
XLA Ops:
  0.0 1.4 %collective-permute-start.2 = (bf16[256,7168]{1,0:T(8,128)(2,1)}, bf16[256,7168]{1,0:T(8,128)(2,1)S(1)}, u32[]{:S(2)}, u32[]{:S(2)}) collective-permute-start(bf16[256,7168]{1,0:T(8,128)(2,1)} %bitcast.16), channel_id=1, source_target_pairs={{0,4},{4,0},{1,5},{5,1},{2,6},{6,2},{3,7},{7,3},{8,12},{12,8},{9,1... | collective-permute-start | bytes 11010056 | tf_op jit(solution)/shard_map/ppermute | solution.py:20
  2.0 0.6 copy-done.7
  2.7 3.0 %shard_map.127 = (bf16[256,640]{1,0:T(8,128)(2,1)S(1)}, f32[256,512]{1,0:T(8,128)S(1)}, f32[256,256]{1,0:T(8,128)S(1)}, bf16[16,512,128]{2,1,0:T(8,128)(2,1)S(1)}) custom-call(s32[1]{0:T(128)S(6)} %copy.14.lengths, s32[2]{0:T(128)S(1)} %bitcast.22, bf16[16,32,576]{2,1,0:T(8,128)(2,1)} %bitcast.23, bf16[192,576]{1,0:T(8,128)(2,1)} %bitcast.24, ...), custom_call_target="tpu_custom_call" | custom-call | tf_op jit(solution)/shard_map/pallas_call | solution.py:29
  5.7 0.6 collective-permute-start
  6.3 4.4 %collective-permute-done.arrived = bf16[256,640]{1,0:T(8,128)(2,1)S(1)} collective-permute-done((bf16[256,640]{1,0:T(8,128)(2,1)S(1)}, bf16[256,640]{1,0:T(8,128)(2,1)S(1)}, u32[]{:S(2)}, u32[]{:S(2)}) %collective-permute-start) | collective-permute-done | bytes 327712 | tf_op jit(solution)/shard_map/ppermute | solution.py:20
  10.7 1.1 shard_map.128
  11.8 24.8 %all_to_all.20.gathered = bf16[16,17,16,128]{3,2,1,0:T(8,128)(2,1)S(1)} all-to-all(bf16[16,17,16,128]{3,2,1,0:T(8,128)(2,1)S(1)} %shard_map.128), channel_id=1, replica_groups=mesh['req'=16,'seq'=2,'exp'=4] {'req'}, dimensions={0} | all-to-all | bytes 2228224 | tf_op jit(solution)/shard_map/all_to_all | solution.py:446
  36.6 0.5 shard_map.130
  37.1 1.7 %collective-permute-start.3 = (bf16[288,256]{1,0:T(8,128)(2,1)S(1)}, bf16[288,256]{1,0:T(8,128)(2,1)S(1)}, u32[]{:S(2)}, u32[]{:S(2)}) collective-permute-start(bf16[288,256]{1,0:T(8,128)(2,1)S(1)} %shard_map.130), channel_id=1, source_target_pairs={{0,4},{4,0},{1,5},{5,1},{2,6},{6,2},{3,7},{7,3},{8,12},{12,8},{9,1... | collective-permute-start | bytes 442376 | tf_op jit(solution)/shard_map/ppermute | solution.py:20
  38.8 0.5 shard_map.129.started
  39.3 0.5 collective-permute-done.3.arrived
  39.9 0.3 shard_map.131
  40.1 8.9 %all_to_all.21.terms = bf16[4,64,256]{2,1,0:T(8,128)(2,1)S(1)} all-to-all(bf16[4,64,256]{2,1,0:T(8,128)(2,1)S(1)} %get-tuple-element.22), channel_id=1, replica_groups=mesh['req'=16,'seq'=2,'exp'=4] {'exp'}, dimensions={0} | all-to-all | bytes 262144 | tf_op jit(solution)/shard_map/all_to_all | solution.py:467
  49.1 0.2 shard_map.132
  49.3 29.6 %all_to_all.22 = bf16[64,16,896]{2,1,0:T(8,128)(2,1)S(1)} all-to-all(bf16[64,16,896]{2,1,0:T(8,128)(2,1)S(1)} %shard_map.132), channel_id=1, replica_groups=mesh['req'=16,'seq'=2,'exp'=4] {'req','exp'}, dimensions={0} | all-to-all | bytes 3670016 | tf_op jit(solution)/shard_map/all_to_all | solution.py:474
  78.9 3.4 %collective-permute-start.4 = (bf16[16,4,16,896]{3,2,1,0:T(8,128)(2,1)S(1)}, bf16[16,4,16,896]{3,2,1,0:T(8,128)(2,1)S(1)}, u32[]{:S(2)}, u32[]{:S(2)}) collective-permute-start(bf16[16,4,16,896]{3,2,1,0:T(8,128)(2,1)S(1)} %bitcast.9), channel_id=1, source_target_pairs={{0,4},{4,0},{1,5},{5,1},{2,6},{6,2},{3,7},{7,3},{8,12},{12,8},{9,1... | collective-permute-start | bytes 5505032 | tf_op jit(solution)/shard_map/ppermute | solution.py:20
  82.4 2.2 %shard_map.133 = (f32[256,256]{1,0:T(8,128)S(1)}, f32[256,256]{1,0:T(8,128)S(1)}, f32[256,16]{1,0:T(8,128)S(1)}, f32[256,128]{1,0:T(8,128)S(1)}) custom-call(bf16[16,4,16,896]{3,2,1,0:T(8,128)(2,1)S(1)} %bitcast.10, bf16[1,7168]{1,0:T(2,128)(2,1)S(1)} %reshape.11.gains, bf16[7168,256]{1,0:T(8,128)(2,1)S(1)} %bitcast.12, bf16[7168,256]{1,0:T(8,128)(2,1)S(1)} %bitcast.14, ...), custom_call_target="tpu_custom_call" | custom-call | tf_op jit(solution)/shard_map/pallas_call | solution.py:29
  84.6 1.1 collective-permute-done.4.other
  85.8 11.0 %shard_map.134 = (bf16[128,256]{1,0:T(8,128)(2,1)S(1)}, bf16[128,256]{1,0:T(8,128)(2,1)S(1)}, f32[32,2,224]{2,1,0:T(2,128)S(1)}) custom-call(f32[256,256]{1,0:T(8,128)S(1)} %get-tuple-element.24.gate, f32[256,256]{1,0:T(8,128)S(1)} %get-tuple-element.25.up, f32[256,16]{1,0:T(8,128)S(1)} %get-tuple-element.26.logits, ...), custom_call_target="tpu_custom_call" | custom-call | tf_op jit(solution)/shard_map/pallas_call | solution.py:29
  96.8 0.4 collective-permute-start.5
  97.2 0.9 collective-permute-done.5.act_other
  98.1 3.0 %shard_map.135 = bf16[64,16,896]{2,1,0:T(8,128)(2,1)S(1)} custom-call(bf16[128,256]{1,0:T(8,128)(2,1)S(1)} %get-tuple-element.28.act, bf16[128,256]{1,0:T(8,128)(2,1)S(1)} %collective-permute-done.5.act_other, bf16[256,7168]{1,0:T(8,128)(2,1)S(1)} %bitcast.17, bf16[256,7168]{1,0:T(8,128)(2,1)S(1)} %collective-permute-done.2.swapped.w_down_other), custom_call_target="tpu_custom_call" | custom-call | tf_op jit(solution)/shard_map/pallas_call | solution.py:29
  101.1 29.5 %all_to_all.23.pieces = bf16[64,16,896]{2,1,0:T(8,128)(2,1)S(1)} all-to-all(bf16[64,16,896]{2,1,0:T(8,128)(2,1)S(1)} %shard_map.135), channel_id=1, replica_groups=mesh['req'=16,'seq'=2,'exp'=4] {'exp','req'}, dimensions={0} | all-to-all | bytes 3670016 | tf_op jit(solution)/shard_map/all_to_all | solution.py:516
  130.6 0.9 shard_map.136
  (21 shorter events, 0.1 us)
Async XLA Ops:
  0.0 36.6 %collective-permute-start.2 = (bf16[256,7168]{1,0:T(8,128)(2,1)}, bf16[256,7168]{1,0:T(8,128)(2,1)S(1)}, u32[]{:S(2)}, u32[]{:S(2)}) collective-permute-start(bf16[256,7168]{1,0:T(8,128)(2,1)} %bitcast.16), channel_id=1, source_target_pairs={{0,4},{4,0},{1,5},{5,1},{2,6},{6,2},{3,7},{7,3},{8,12},{12,8},{9,1... | collective-permute-start | bytes 11010056 | tf_op jit(solution)/shard_map/ppermute | solution.py:20
  1.4 35.2 %collective-permute-start.1 = (bf16[224,4096]{1,0:T(8,128)(2,1)}, bf16[224,4096]{1,0:T(8,128)(2,1)S(1)}, u32[]{:S(2)}, u32[]{:S(2)}) collective-permute-start(bf16[224,4096]{1,0:T(8,128)(2,1)} %bitcast.18), channel_id=1, source_target_pairs={{0,4},{4,0},{1,5},{5,1},{2,6},{6,2},{3,7},{7,3},{8,12},{12,8},{9,1... | collective-permute-start | bytes 5505032 | tf_op jit(solution)/shard_map/ppermute | solution.py:20
  2.0 0.7 copy-start.7
  2.7 8.0 %copy-start.5 = (bf16[2,7168]{1,0:T(2,128)(2,1)S(1)}, bf16[2,7168]{1,0:T(2,128)(2,1)}, u32[]{:S(2)}) copy-start(bf16[2,7168]{1,0:T(2,128)(2,1)} %residual.1) | copy-start | bytes 86020
  2.7 8.0 %copy-start.6 = (s32[2,8]{1,0:T(2,128)S(1)}, s32[2,8]{1,0:T(2,128)}, u32[]{:S(2)}) copy-start(s32[2,8]{1,0:T(2,128)} %expert_ids.1) | copy-start | bytes 196
  5.7 5.0 %collective-permute-start = (bf16[256,640]{1,0:T(8,128)(2,1)S(1)}, bf16[256,640]{1,0:T(8,128)(2,1)S(1)}, u32[]{:S(2)}, u32[]{:S(2)}) collective-permute-start(bf16[256,640]{1,0:T(8,128)(2,1)S(1)} %get-tuple-element.20), channel_id=1, source_target_pairs={{0,4},{4,0},{1,5},{5,1},{2,6},{6,2},{3,7},{7,3},{8,12},{12,8},{9,1... | collective-permute-start | bytes 983048 | tf_op jit(solution)/shard_map/ppermute | solution.py:20
  36.6 2.3 %copy-start.3 = (bf16[4096,224]{0,1:T(8,128)(2,1)S(1)}, bf16[4096,224]{0,1:T(8,128)(2,1)}, u32[]{:S(2)}) copy-start(bf16[4096,224]{0,1:T(8,128)(2,1)} %param.19) | copy-start | bytes 5505028
  37.1 2.8 %collective-permute-start.3 = (bf16[288,256]{1,0:T(8,128)(2,1)S(1)}, bf16[288,256]{1,0:T(8,128)(2,1)S(1)}, u32[]{:S(2)}, u32[]{:S(2)}) collective-permute-start(bf16[288,256]{1,0:T(8,128)(2,1)S(1)} %shard_map.130), channel_id=1, source_target_pairs={{0,4},{4,0},{1,5},{5,1},{2,6},{6,2},{3,7},{7,3},{8,12},{12,8},{9,1... | collective-permute-start | bytes 442376 | tf_op jit(solution)/shard_map/ppermute | solution.py:20
  38.8 43.5 %copy-start.4 = (bf16[7168,16]{0,1:T(8,128)(2,1)S(1)}, bf16[7168,16]{0,1:T(8,128)(2,1)}, u32[]{:S(2)}) copy-start(bf16[7168,16]{0,1:T(8,128)(2,1)} %param.21) | copy-start | bytes 688132
  39.9 42.5 %copy-start.1 = (bf16[1,7168,256]{2,1,0:T(8,128)(2,1)S(1)}, bf16[1,7168,256]{2,1,0:T(8,128)(2,1)}, u32[]{:S(2)}) copy-start(bf16[1,7168,256]{2,1,0:T(8,128)(2,1)} %param.24) | copy-start | bytes 11010052
  49.1 33.3 %copy-start.8 = (bf16[7168]{0:T(1024)(128)(2,1)S(1)}, bf16[7168]{0:T(1024)(128)(2,1)}, u32[]{:S(2)}) copy-start(bf16[7168]{0:T(1024)(128)(2,1)} %param.20) | copy-start | bytes 43012
  49.3 33.1 %copy-start = (bf16[1,7168,256]{2,1,0:T(8,128)(2,1)S(1)}, bf16[1,7168,256]{2,1,0:T(8,128)(2,1)}, u32[]{:S(2)}) copy-start(bf16[1,7168,256]{2,1,0:T(8,128)(2,1)} %param.23) | copy-start | bytes 11010052
  78.9 6.8 %collective-permute-start.4 = (bf16[16,4,16,896]{3,2,1,0:T(8,128)(2,1)S(1)}, bf16[16,4,16,896]{3,2,1,0:T(8,128)(2,1)S(1)}, u32[]{:S(2)}, u32[]{:S(2)}) collective-permute-start(bf16[16,4,16,896]{3,2,1,0:T(8,128)(2,1)S(1)} %bitcast.9), channel_id=1, source_target_pairs={{0,4},{4,0},{1,5},{5,1},{2,6},{6,2},{3,7},{7,3},{8,12},{12,8},{9,1... | collective-permute-start | bytes 5505032 | tf_op jit(solution)/shard_map/ppermute | solution.py:20
  85.8 12.4 %copy-start.2 = (bf16[1,256,7168]{2,1,0:T(8,128)(2,1)S(1)}, bf16[1,256,7168]{2,1,0:T(8,128)(2,1)}, u32[]{:S(2)}) copy-start(bf16[1,256,7168]{2,1,0:T(8,128)(2,1)} %param.25) | copy-start | bytes 11010052
  96.8 1.4 %collective-permute-start.5 = (bf16[128,256]{1,0:T(8,128)(2,1)S(1)}, bf16[128,256]{1,0:T(8,128)(2,1)S(1)}, u32[]{:S(2)}, u32[]{:S(2)}) collective-permute-start(bf16[128,256]{1,0:T(8,128)(2,1)S(1)} %get-tuple-element.29), channel_id=1, source_target_pairs={{0,4},{4,0},{1,5},{5,1},{2,6},{6,2},{3,7},{7,3},{8,12},{12,8},{9,1... | collective-permute-start | bytes 196616 | tf_op jit(solution)/shard_map/ppermute | solution.py:20

commit v10 on v9

--- a/solution.py
+++ b/solution.py
@@ -312,25 +312,26 @@
 
 def gate_up_both_kernel(
     gate, up, logits, squares, own, other, terms, gains, w_gate, w_up, router_t,
-    act_mine, act_theirs, rows_here,
+    act_mine, act_theirs, rows_here, lines,
 ):
     side = lax.axis_index("seq")
-    own_rows = rows_here.shape[1]
+    own_rows = rows_here.shape[0] // (2 * own.shape[0])
     exp, req = lax.axis_index("exp"), lax.axis_index("req")
     packed_rows = own.shape[2]
     place = (req * 2 + side) * own_rows
     group, first = place // packed_rows, place % packed_rows
-    part = rows_here.shape[2]
+    part = rows_here.shape[1]
     near = lax.broadcasted_iota(jnp.int32, own.shape[2:], 0)
     for rows, from_side in ((own, side), (other, 1 - side)):
         for i in range(own.shape[0]):
             tile = rows[i, exp].astype(F32)
             for row in range(own_rows):
                 line = jnp.sum(jnp.where(near == first + row, tile, 0.0), 0, keepdims=True)
-                picked = line[:, :part]
-                for j in range(1, PACK):
-                    picked = jnp.where(group == j, line[:, j * part : (j + 1) * part], picked)
-                rows_here[i * 2 + from_side, row : row + 1, :] = picked
+                lines[pl.ds((i * 2 + from_side) * own_rows + row, 1), :] = line
+    picked = lines[:, :part]
+    for j in range(1, PACK):
+        picked = jnp.where(group == j, lines[:, j * part : (j + 1) * part], picked)
+    rows_here[...] = picked
     width = gains.shape[1] // (2 * own.shape[0])
     experts = logits.shape[1]
     columns = gains.shape[1]
@@ -376,11 +377,11 @@
 
 
 def finish_kernel(pieces, hidden_rows, out):
-    blocks, rows = hidden_rows.shape[0], out.shape[0]
-    width = out.shape[1] // blocks
+    rows = out.shape[0]
+    blocks = hidden_rows.shape[0] // rows
     total = jnp.sum(pieces[...].astype(F32), 0)
     total = jnp.concatenate([total[i * rows : (i + 1) * rows] for i in range(CHUNKS)], -1)
-    hidden = jnp.concatenate([hidden_rows[block, :rows, :width] for block in range(blocks)], -1)
+    hidden = jnp.concatenate([hidden_rows[block * rows : (block + 1) * rows] for block in range(blocks)], -1)
     out[...] = (hidden + total).astype(BF16)
 
 
@@ -493,7 +494,7 @@
         (
             shape((tokens // 2, hidden_units), BF16),
             shape((tokens // 2, hidden_units), BF16),
-            shape((n_req * 2, own_rows, width), F32),
+            shape((n_req * 2 * own_rows, width), F32),
         ),
         *started,
         own,
@@ -503,6 +504,7 @@
         w_gate,
         w_up,
         router_t,
+        scratch=(pltpu.VMEM((n_req * 2 * own_rows, width * PACK), F32),),
     )
     pieces = call(
         down_kernel,

time: 133 us -> 126 us (0.947)
  Pallas kernels: 22.7 us -> 15 us
    pallas_call x10, Pallas kernels: 22.7 us -> 15 us  [call(): pl.pallas_call(kernel, out_shape=out_shape, in_specs=[pl.BlockSpec(memory...]
where the time goes in v10:
time: 126 us; the launch traced here: 124 us
  blocking collectives  92.8 us (74%)
  Pallas kernels  15 us (12%)
  starting transfers between devices  7.7 us (6%)
  waiting for transfers between devices  6.98 us (6%)
    all_to_all x1, blocking collectives, per_device(): lax.all_to_all(fanned, ('req', 'exp'), split_axis=0, concat_axis=0, tiled...  29.6 us
    all_to_all x1, blocking collectives, per_device(): lax.all_to_all(pieces, ('exp', 'req'), split_axis=0, concat_axis=0, tiled...  29.5 us
    all_to_all x1, blocking collectives, per_device(): lax.all_to_all(fanned, 'req', split_axis=0, concat_axis=0, tiled=True)  24.8 us
    pallas_call x10, Pallas kernels, call(): pl.pallas_call(kernel, out_shape=out_shape, in_specs=[pl.BlockSpec(memory...  15 us
    all_to_all x1, blocking collectives, per_device(): lax.all_to_all(terms, 'exp', split_axis=0, concat_axis=0, tiled=True)  8.91 us
    ppermute x6, starting transfers between devices, swap(): return lax.ppermute(x, 'seq', SWAP)  7.7 us
    ppermute x6, waiting for transfers between devices, swap(): return lax.ppermute(x, 'seq', SWAP)  6.98 us
  transfers between devices with their start and end apart: 6, of which 4 were waited for; matrix products, arithmetic and copies ran while one was open for 0% of the time, Pallas kernels for 5%

profile of v10, /device:TPU:1, one launch (start us, length us, event | category | flops | bytes accessed | tf_op | source)
XLA Modules:
  0.0 124.0 jit_solution(6013152306009543605)
XLA Ops:
  0.0 1.4 %collective-permute-start.2 = (bf16[256,7168]{1,0:T(8,128)(2,1)}, bf16[256,7168]{1,0:T(8,128)(2,1)S(1)}, u32[]{:S(2)}, u32[]{:S(2)}) collective-permute-start(bf16[256,7168]{1,0:T(8,128)(2,1)} %bitcast.16), channel_id=1, source_target_pairs={{0,4},{4,0},{1,5},{5,1},{2,6},{6,2},{3,7},{7,3},{8,12},{12,8},{9,1... | collective-permute-start | bytes 11010056 | tf_op jit(solution)/shard_map/ppermute | solution.py:20
  2.0 0.6 copy-done.7
  2.7 3.0 %shard_map.127 = (bf16[256,640]{1,0:T(8,128)(2,1)S(1)}, f32[256,512]{1,0:T(8,128)S(1)}, f32[256,256]{1,0:T(8,128)S(1)}, bf16[16,512,128]{2,1,0:T(8,128)(2,1)S(1)}) custom-call(s32[1]{0:T(128)S(6)} %copy.14.lengths, s32[2]{0:T(128)S(1)} %bitcast.22, bf16[16,32,576]{2,1,0:T(8,128)(2,1)} %bitcast.23, bf16[192,576]{1,0:T(8,128)(2,1)} %bitcast.24, ...), custom_call_target="tpu_custom_call" | custom-call | tf_op jit(solution)/shard_map/pallas_call | solution.py:29
  5.7 0.6 collective-permute-start
  6.3 4.4 %collective-permute-done.arrived = bf16[256,640]{1,0:T(8,128)(2,1)S(1)} collective-permute-done((bf16[256,640]{1,0:T(8,128)(2,1)S(1)}, bf16[256,640]{1,0:T(8,128)(2,1)S(1)}, u32[]{:S(2)}, u32[]{:S(2)}) %collective-permute-start) | collective-permute-done | bytes 327712 | tf_op jit(solution)/shard_map/ppermute | solution.py:20
  10.7 1.1 shard_map.128
  11.8 24.8 %all_to_all.20.gathered = bf16[16,17,16,128]{3,2,1,0:T(8,128)(2,1)S(1)} all-to-all(bf16[16,17,16,128]{3,2,1,0:T(8,128)(2,1)S(1)} %shard_map.128), channel_id=1, replica_groups=mesh['req'=16,'seq'=2,'exp'=4] {'req'}, dimensions={0} | all-to-all | bytes 2228224 | tf_op jit(solution)/shard_map/all_to_all | solution.py:447
  36.6 0.5 shard_map.130
  37.1 1.7 %collective-permute-start.3 = (bf16[288,256]{1,0:T(8,128)(2,1)S(1)}, bf16[288,256]{1,0:T(8,128)(2,1)S(1)}, u32[]{:S(2)}, u32[]{:S(2)}) collective-permute-start(bf16[288,256]{1,0:T(8,128)(2,1)S(1)} %shard_map.130), channel_id=1, source_target_pairs={{0,4},{4,0},{1,5},{5,1},{2,6},{6,2},{3,7},{7,3},{8,12},{12,8},{9,1... | collective-permute-start | bytes 442376 | tf_op jit(solution)/shard_map/ppermute | solution.py:20
  38.8 0.5 shard_map.129.started
  39.3 0.5 collective-permute-done.3.arrived
  39.9 0.3 shard_map.131
  40.1 8.9 %all_to_all.21.terms = bf16[4,64,256]{2,1,0:T(8,128)(2,1)S(1)} all-to-all(bf16[4,64,256]{2,1,0:T(8,128)(2,1)S(1)} %get-tuple-element.22), channel_id=1, replica_groups=mesh['req'=16,'seq'=2,'exp'=4] {'exp'}, dimensions={0} | all-to-all | bytes 262144 | tf_op jit(solution)/shard_map/all_to_all | solution.py:468
  49.1 0.2 shard_map.132
  49.3 29.6 %all_to_all.22 = bf16[64,16,896]{2,1,0:T(8,128)(2,1)S(1)} all-to-all(bf16[64,16,896]{2,1,0:T(8,128)(2,1)S(1)} %shard_map.132), channel_id=1, replica_groups=mesh['req'=16,'seq'=2,'exp'=4] {'req','exp'}, dimensions={0} | all-to-all | bytes 3670016 | tf_op jit(solution)/shard_map/all_to_all | solution.py:475
  78.9 3.4 %collective-permute-start.4 = (bf16[16,4,16,896]{3,2,1,0:T(8,128)(2,1)S(1)}, bf16[16,4,16,896]{3,2,1,0:T(8,128)(2,1)S(1)}, u32[]{:S(2)}, u32[]{:S(2)}) collective-permute-start(bf16[16,4,16,896]{3,2,1,0:T(8,128)(2,1)S(1)} %bitcast.9), channel_id=1, source_target_pairs={{0,4},{4,0},{1,5},{5,1},{2,6},{6,2},{3,7},{7,3},{8,12},{12,8},{9,1... | collective-permute-start | bytes 5505032 | tf_op jit(solution)/shard_map/ppermute | solution.py:20
  82.4 2.2 %shard_map.133 = (f32[256,256]{1,0:T(8,128)S(1)}, f32[256,256]{1,0:T(8,128)S(1)}, f32[256,16]{1,0:T(8,128)S(1)}, f32[256,128]{1,0:T(8,128)S(1)}) custom-call(bf16[16,4,16,896]{3,2,1,0:T(8,128)(2,1)S(1)} %bitcast.10, bf16[1,7168]{1,0:T(2,128)(2,1)S(1)} %reshape.11.gains, bf16[7168,256]{1,0:T(8,128)(2,1)S(1)} %bitcast.12, bf16[7168,256]{1,0:T(8,128)(2,1)S(1)} %bitcast.14, ...), custom_call_target="tpu_custom_call" | custom-call | tf_op jit(solution)/shard_map/pallas_call | solution.py:29
  84.6 1.1 collective-permute-done.4.other
  85.8 3.3 %shard_map.134 = (bf16[128,256]{1,0:T(8,128)(2,1)S(1)}, bf16[128,256]{1,0:T(8,128)(2,1)S(1)}, f32[64,224]{1,0:T(8,128)S(1)}) custom-call(f32[256,256]{1,0:T(8,128)S(1)} %get-tuple-element.24.gate, f32[256,256]{1,0:T(8,128)S(1)} %get-tuple-element.25.up, f32[256,16]{1,0:T(8,128)S(1)} %get-tuple-element.26.logits, f32[256,128]{1,0:T(8,128)S(1)} %get-tuple-element.27.squares, ...), custom_call_target="tpu_custom_call" | custom-call | tf_op jit(solution)/shard_map/pallas_call | solution.py:29
  89.0 0.6 collective-permute-start.5
  89.6 0.9 collective-permute-done.5.act_other
  90.5 3.0 %shard_map.135 = bf16[64,16,896]{2,1,0:T(8,128)(2,1)S(1)} custom-call(bf16[128,256]{1,0:T(8,128)(2,1)S(1)} %get-tuple-element.28.act, bf16[128,256]{1,0:T(8,128)(2,1)S(1)} %collective-permute-done.5.act_other, bf16[256,7168]{1,0:T(8,128)(2,1)S(1)} %bitcast.17, bf16[256,7168]{1,0:T(8,128)(2,1)S(1)} %collective-permute-done.2.swapped.w_down_other), custom_call_target="tpu_custom_call" | custom-call | tf_op jit(solution)/shard_map/pallas_call | solution.py:29
  93.5 29.5 %all_to_all.23.pieces = bf16[64,16,896]{2,1,0:T(8,128)(2,1)S(1)} all-to-all(bf16[64,16,896]{2,1,0:T(8,128)(2,1)S(1)} %shard_map.135), channel_id=1, replica_groups=mesh['req'=16,'seq'=2,'exp'=4] {'exp','req'}, dimensions={0} | all-to-all | bytes 3670016 | tf_op jit(solution)/shard_map/all_to_all | solution.py:518
  123.0 1.0 shard_map.136
  (21 shorter events, 0.1 us)
Async XLA Ops:
  0.0 36.6 %collective-permute-start.2 = (bf16[256,7168]{1,0:T(8,128)(2,1)}, bf16[256,7168]{1,0:T(8,128)(2,1)S(1)}, u32[]{:S(2)}, u32[]{:S(2)}) collective-permute-start(bf16[256,7168]{1,0:T(8,128)(2,1)} %bitcast.16), channel_id=1, source_target_pairs={{0,4},{4,0},{1,5},{5,1},{2,6},{6,2},{3,7},{7,3},{8,12},{12,8},{9,1... | collective-permute-start | bytes 11010056 | tf_op jit(solution)/shard_map/ppermute | solution.py:20
  1.4 35.2 %collective-permute-start.1 = (bf16[224,4096]{1,0:T(8,128)(2,1)}, bf16[224,4096]{1,0:T(8,128)(2,1)S(1)}, u32[]{:S(2)}, u32[]{:S(2)}) collective-permute-start(bf16[224,4096]{1,0:T(8,128)(2,1)} %bitcast.18), channel_id=1, source_target_pairs={{0,4},{4,0},{1,5},{5,1},{2,6},{6,2},{3,7},{7,3},{8,12},{12,8},{9,1... | collective-permute-start | bytes 5505032 | tf_op jit(solution)/shard_map/ppermute | solution.py:20
  2.0 0.7 copy-start.7
  2.7 8.0 %copy-start.5 = (bf16[2,7168]{1,0:T(2,128)(2,1)S(1)}, bf16[2,7168]{1,0:T(2,128)(2,1)}, u32[]{:S(2)}) copy-start(bf16[2,7168]{1,0:T(2,128)(2,1)} %residual.1) | copy-start | bytes 86020
  2.7 8.0 %copy-start.6 = (s32[2,8]{1,0:T(2,128)S(1)}, s32[2,8]{1,0:T(2,128)}, u32[]{:S(2)}) copy-start(s32[2,8]{1,0:T(2,128)} %expert_ids.1) | copy-start | bytes 196
  5.7 5.0 %collective-permute-start = (bf16[256,640]{1,0:T(8,128)(2,1)S(1)}, bf16[256,640]{1,0:T(8,128)(2,1)S(1)}, u32[]{:S(2)}, u32[]{:S(2)}) collective-permute-start(bf16[256,640]{1,0:T(8,128)(2,1)S(1)} %get-tuple-element.20), channel_id=1, source_target_pairs={{0,4},{4,0},{1,5},{5,1},{2,6},{6,2},{3,7},{7,3},{8,12},{12,8},{9,1... | collective-permute-start | bytes 983048 | tf_op jit(solution)/shard_map/ppermute | solution.py:20
  36.6 2.3 %copy-start.3 = (bf16[4096,224]{0,1:T(8,128)(2,1)S(1)}, bf16[4096,224]{0,1:T(8,128)(2,1)}, u32[]{:S(2)}) copy-start(bf16[4096,224]{0,1:T(8,128)(2,1)} %param.19) | copy-start | bytes 5505028
  37.1 2.8 %collective-permute-start.3 = (bf16[288,256]{1,0:T(8,128)(2,1)S(1)}, bf16[288,256]{1,0:T(8,128)(2,1)S(1)}, u32[]{:S(2)}, u32[]{:S(2)}) collective-permute-start(bf16[288,256]{1,0:T(8,128)(2,1)S(1)} %shard_map.130), channel_id=1, source_target_pairs={{0,4},{4,0},{1,5},{5,1},{2,6},{6,2},{3,7},{7,3},{8,12},{12,8},{9,1... | collective-permute-start | bytes 442376 | tf_op jit(solution)/shard_map/ppermute | solution.py:20
  38.8 43.5 %copy-start.4 = (bf16[7168,16]{0,1:T(8,128)(2,1)S(1)}, bf16[7168,16]{0,1:T(8,128)(2,1)}, u32[]{:S(2)}) copy-start(bf16[7168,16]{0,1:T(8,128)(2,1)} %param.21) | copy-start | bytes 688132
  39.9 42.5 %copy-start.1 = (bf16[1,7168,256]{2,1,0:T(8,128)(2,1)S(1)}, bf16[1,7168,256]{2,1,0:T(8,128)(2,1)}, u32[]{:S(2)}) copy-start(bf16[1,7168,256]{2,1,0:T(8,128)(2,1)} %param.24) | copy-start | bytes 11010052
  49.1 33.3 %copy-start.8 = (bf16[7168]{0:T(1024)(128)(2,1)S(1)}, bf16[7168]{0:T(1024)(128)(2,1)}, u32[]{:S(2)}) copy-start(bf16[7168]{0:T(1024)(128)(2,1)} %param.20) | copy-start | bytes 43012
  49.3 33.1 %copy-start = (bf16[1,7168,256]{2,1,0:T(8,128)(2,1)S(1)}, bf16[1,7168,256]{2,1,0:T(8,128)(2,1)}, u32[]{:S(2)}) copy-start(bf16[1,7168,256]{2,1,0:T(8,128)(2,1)} %param.23) | copy-start | bytes 11010052
  78.9 6.8 %collective-permute-start.4 = (bf16[16,4,16,896]{3,2,1,0:T(8,128)(2,1)S(1)}, bf16[16,4,16,896]{3,2,1,0:T(8,128)(2,1)S(1)}, u32[]{:S(2)}, u32[]{:S(2)}) collective-permute-start(bf16[16,4,16,896]{3,2,1,0:T(8,128)(2,1)S(1)} %bitcast.9), channel_id=1, source_target_pairs={{0,4},{4,0},{1,5},{5,1},{2,6},{6,2},{3,7},{7,3},{8,12},{12,8},{9,1... | collective-permute-start | bytes 5505032 | tf_op jit(solution)/shard_map/ppermute | solution.py:20
  85.8 4.8 %copy-start.2 = (bf16[1,256,7168]{2,1,0:T(8,128)(2,1)S(1)}, bf16[1,256,7168]{2,1,0:T(8,128)(2,1)}, u32[]{:S(2)}) copy-start(bf16[1,256,7168]{2,1,0:T(8,128)(2,1)} %param.25) | copy-start | bytes 11010052
  89.0 1.5 %collective-permute-start.5 = (bf16[128,256]{1,0:T(8,128)(2,1)S(1)}, bf16[128,256]{1,0:T(8,128)(2,1)S(1)}, u32[]{:S(2)}, u32[]{:S(2)}) collective-permute-start(bf16[128,256]{1,0:T(8,128)(2,1)S(1)} %get-tuple-element.29), channel_id=1, source_target_pairs={{0,4},{4,0},{1,5},{5,1},{2,6},{6,2},{3,7},{7,3},{8,12},{12,8},{9,1... | collective-permute-start | bytes 196616 | tf_op jit(solution)/shard_map/ppermute | solution.py:20
